TPU v7x, 128 devices: a whole 4x4x4 slice. The times are simulated.
128 devices in a mesh: seq: 16 (over z, x), dp: 8 (over y, core).
Axes of the slice: x: 4, y: 4, z: 4, core: 2. Of those that a mesh axis runs over, the one named last changes fastest.
Arguments:
- query_input: bfloat16 [8, 8192, 2048], P('dp', 'seq'), may hold values from -300 to 300
- key_input: bfloat16 [8, 8192, 2048], P('dp', 'seq'), may hold values from -6 to 6
- value_input: bfloat16 [8, 8192, 2048], P('dp', 'seq'), may hold values from -6 to 6
- keep_blocks: int32 [8, 16], P('dp'), may hold values from 0 to 63, as said below
- dest_slots: int32 [8, 16], P('dp'), may hold values from 0 to 15, each once within a row
- proj_weights: bfloat16 [3, 2048, 2048], P(None, None, 'seq'), may hold values from -5 to 5
- cotangent: bfloat16 [8, 2048, 2048], P('dp', None, 'seq'), may hold values from -6 to 6
Outputs:
- window_out: bfloat16 [8, 8192, 2048], P('dp', 'seq')
- causal_out: bfloat16 [8, 2048, 2048], P('dp', None, 'seq')
- weight_grad: float32 [3, 2048, 2048], P(None, None, 'seq')
- row_grad: bfloat16 [8, 2048, 2048], P('dp', 'seq')
Inputs may be any that keep to these rules, and one draw needn't show every extreme that they name: `keep_blocks`: each row lists 16 distinct block numbers in increasing order, block b covering positions b * 128 to b * 128 + 127. The 4 blocks on one index of seq contribute at most 2 kept blocks, and in every document some index of seq contributes exactly 2. `dest_slots`: each row is a permutation.
All inputs are finite; a program needn't handle non-finite values.
Results may differ from a plain program's by a relative error of at most 0.015.
Values may be sent and summed in bfloat16 or wider, within the bound.
A program may use at most 192 MiB of HBM per device.

v0:
```python
import jax
import jax.numpy as jnp
from jax import lax
from jax.sharding import PartitionSpec as P

HEAD = 128
WIN = 1024
BLK = 128


def passed_along(x, axis, by):
    length = lax.axis_size(axis)
    pairs = [(i, i + by) for i in range(length) if 0 <= i + by < length]
    return lax.ppermute(x, axis, pairs)


def window_head(query_rows, key_rows, value_rows, allowed):
    score_scale = HEAD ** (-0.5)
    scores = (
        lax.dot_general(
            query_rows, key_rows, (((1,), (1,)), ((), ())), preferred_element_type=jnp.float32
        )
        * score_scale
    )
    scores = jnp.where(allowed, scores, -1e30)
    row_max = jnp.max(scores, axis=1, keepdims=True)
    weight = jnp.where(allowed, jnp.exp(scores - row_max), 0.0)
    probabilities = (weight / jnp.sum(weight, axis=1, keepdims=True)).astype(jnp.bfloat16)
    return jnp.dot(probabilities, value_rows, preferred_element_type=jnp.float32).astype(
        jnp.bfloat16
    )


def norm_rows(rows_in):
    values_f = rows_in.astype(jnp.float32)
    mean_square = jnp.mean(values_f * values_f, axis=1, keepdims=True)
    return (values_f * lax.rsqrt(mean_square + 1e-06)).astype(jnp.bfloat16)


def global_head(query_rows, key_rows, value_rows, grad_rows, positions):
    row_count = query_rows.shape[0]
    block_rows = min(512, row_count)
    block_count = row_count // block_rows
    score_scale = HEAD ** (-0.5)

    def step_block(accumulators, block_index):
        key_acc, value_acc = accumulators
        start_row = block_index * block_rows
        query_block = lax.dynamic_slice_in_dim(query_rows, start_row, block_rows, 0)
        grad_block = lax.dynamic_slice_in_dim(grad_rows, start_row, block_rows, 0)
        place_block = lax.dynamic_slice_in_dim(positions, start_row, block_rows, 0)
        causal = positions[None, :] <= place_block[:, None]
        scores = (
            lax.dot_general(
                query_block, key_rows, (((1,), (1,)), ((), ())), preferred_element_type=jnp.float32
            )
            * score_scale
        )
        scores = jnp.where(causal, scores, -1e30)
        row_max = jnp.max(scores, axis=1, keepdims=True)
        weight = jnp.where(causal, jnp.exp(scores - row_max), 0.0)
        soft_weights = weight / jnp.sum(weight, axis=1, keepdims=True)
        probabilities = soft_weights.astype(jnp.bfloat16)
        head_output = jnp.dot(probabilities, value_rows, preferred_element_type=jnp.float32).astype(
            jnp.bfloat16
        )
        d_probs = lax.dot_general(
            grad_block, value_rows, (((1,), (1,)), ((), ())), preferred_element_type=jnp.float32
        )
        value_acc = value_acc + lax.dot_general(
            probabilities, grad_block, (((0,), (0,)), ((), ())), preferred_element_type=jnp.float32
        )
        row_delta = jnp.sum(soft_weights * d_probs, axis=1, keepdims=True)
        d_scores = (soft_weights * (d_probs - row_delta) * score_scale).astype(jnp.bfloat16)
        grad_query = jnp.dot(d_scores, key_rows, preferred_element_type=jnp.float32).astype(
            jnp.bfloat16
        )
        key_acc = key_acc + lax.dot_general(
            d_scores, query_block, (((0,), (0,)), ((), ())), preferred_element_type=jnp.float32
        )
        return ((key_acc, value_acc), (head_output, grad_query))

    zero_acc = jnp.zeros(key_rows.shape, jnp.float32)
    (key_acc, value_acc), (outputs, grad_queries) = lax.scan(
        step_block, (zero_acc, zero_acc), jnp.arange(block_count)
    )
    head_width = query_rows.shape[1]
    return (
        outputs.reshape(row_count, head_width),
        grad_queries.reshape(row_count, head_width),
        key_acc.astype(jnp.bfloat16),
        value_acc.astype(jnp.bfloat16),
    )


def shards(query_input, key_input, value_input, keep_blocks, dest_slots, proj_weights, cotangent):
    query_rows = query_input[0]
    key_rows = key_input[0]
    value_rows = value_input[0]
    tok_rows, feature_width = query_rows.shape
    head_count = feature_width // HEAD
    shard_index = lax.axis_index("seq")
    seq_count = lax.axis_size("seq")
    reach_rows = WIN - 1
    depth_hops = (reach_rows + tok_rows - 1) // tok_rows
    before_keys = []
    before_values = []
    for distance in range(1, depth_hops + 1):
        need_rows = min(tok_rows, reach_rows - (distance - 1) * tok_rows)
        edge_pair = jnp.stack(
            [key_rows[tok_rows - need_rows :], value_rows[tok_rows - need_rows :]]
        )
        arrived = passed_along(edge_pair, "seq", distance)
        before_keys.insert(0, arrived[0])
        before_values.insert(0, arrived[1])
    key_ext = jnp.concatenate(before_keys + [key_rows], axis=0)
    value_ext = jnp.concatenate(before_values + [value_rows], axis=0)
    row_ids = jnp.arange(tok_rows)[:, None]
    col_ids = jnp.arange(tok_rows + reach_rows)[None, :]
    allowed = (
        (col_ids >= row_ids)
        & (col_ids <= row_ids + reach_rows)
        & (col_ids + shard_index * tok_rows >= reach_rows)
    )

    def head_window(head_index):
        column = head_index * HEAD
        return window_head(
            lax.dynamic_slice_in_dim(query_rows, column, HEAD, 1),
            lax.dynamic_slice_in_dim(key_ext, column, HEAD, 1),
            lax.dynamic_slice_in_dim(value_ext, column, HEAD, 1),
            allowed,
        )

    stacked = lax.map(head_window, jnp.arange(head_count))
    window_out = jnp.transpose(stacked, (1, 0, 2)).reshape(tok_rows, feature_width)
    keep_list = keep_blocks[0]
    slot_list = dest_slots[0]
    kept_total = keep_list.shape[0]
    per_shard = tok_rows // BLK
    most_blocks = max(1, per_shard // 2)
    order_inverse = jnp.argsort(slot_list)
    rows_total = kept_total * BLK
    compact_ids = jnp.arange(rows_total, dtype=jnp.int32)
    kept_index = order_inverse[compact_ids // BLK]
    positions = keep_list[kept_index] * BLK + compact_ids % BLK
    local_cols = proj_weights.shape[2]
    wide_weights = jnp.concatenate([proj_weights[0], proj_weights[1], proj_weights[2]], axis=1)
    own_count = rows_total // seq_count
    kept_shard = keep_list // per_shard
    first_kept = jnp.sum(kept_shard < shard_index)
    kept_count = jnp.sum(kept_shard == shard_index)
    slot_ids = jnp.arange(most_blocks)
    pick_index = jnp.minimum(first_kept + slot_ids, kept_total - 1)
    valid_mask = jnp.repeat(slot_ids < kept_count, BLK)
    local_ids = (
        (keep_list[pick_index] % per_shard * BLK)[:, None] + jnp.arange(BLK)[None, :]
    ).reshape(-1)
    packed_rows = norm_rows(jnp.where(valid_mask[:, None], window_out[local_ids], 0))
    shard_piece = lax.all_gather(packed_rows, "seq", axis=0, tiled=True)
    gathered = shard_piece
    projected = jnp.dot(shard_piece, wide_weights, preferred_element_type=jnp.float32).astype(
        jnp.bfloat16
    )
    first_of = jnp.sum(kept_shard[None, :] < kept_shard[:, None], axis=1)
    pack_start = kept_shard * (most_blocks * BLK) + (jnp.arange(kept_total) - first_of) * BLK
    packed_index = pack_start[kept_index] + compact_ids % BLK
    gathered = gathered[packed_index]
    projected = projected[packed_index]
    grad_doc = cotangent[0]
    head_index = 0
    low = head_index * HEAD
    head_result = global_head(
        projected[:, low : low + HEAD],
        projected[:, local_cols + low : local_cols + low + HEAD],
        projected[:, 2 * local_cols + low : 2 * local_cols + low + HEAD],
        grad_doc,
        positions,
    )
    outputs = head_result[0]
    grad_query = head_result[1]
    grad_key = head_result[2]
    grad_value = head_result[3]
    grad_parts = (grad_query, grad_key, grad_value)
    local_grads = jnp.stack(
        [
            lax.dot_general(
                gathered, part, (((0,), (0,)), ((), ())), preferred_element_type=jnp.float32
            )
            for part in grad_parts
        ]
    )
    weight_grad = lax.psum(local_grads.astype(jnp.bfloat16), "dp").astype(jnp.float32)
    term = jnp.zeros((own_count * lax.axis_size("seq"), feature_width), jnp.float32)
    for which_proj in range(3):
        grad_slice = grad_parts[which_proj]
        term = term + lax.dot_general(
            grad_slice,
            proj_weights[which_proj],
            (((1,), (1,)), ((), ())),
            preferred_element_type=jnp.float32,
        )
    row_grad = lax.psum_scatter(term.astype(jnp.bfloat16), "seq", scatter_dimension=0, tiled=True)
    return (window_out[None], outputs[None], weight_grad, row_grad[None])


def solution(mesh):
    return jax.shard_map(
        shards,
        mesh=mesh,
        in_specs=(
            P("dp", "seq", None),
            P("dp", "seq", None),
            P("dp", "seq", None),
            P("dp", None),
            P("dp", None),
            P(None, None, "seq"),
            P("dp", None, "seq"),
        ),
        out_specs=(
            P("dp", "seq", None),
            P("dp", None, "seq"),
            P(None, None, "seq"),
            P("dp", "seq", None),
        ),
        check_vma=False,
    )
```

profile of v0, /device:TPU:0, one launch (start us, length us, event | category | flops | bytes accessed | tf_op | source)
XLA Modules:
  0.0 815.9 jit_solution(6254746076496905836)
XLA Ops:
  9.3 3.2 copy.31
  13.1 5.2 copy.32
  18.3 10.9 %pad_maximum_fusion.1 = bf16[2,511,2048]{2,0,1:T(2,128)(2,1)} fusion(bf16[1,511,2048]{2,0,1:T(2,128)(2,1)} %copy.32, bf16[1,511,2048]{2,0,1:T(2,128)(2,1)S(1)} %copy.31), kind=kLoop, calls=%fused_computation.54 | loop fusion | flops 8372224 | bytes 8372224 | tf_op jit(solution)/shard_map/stack | solution.py:110
  29.2 7.1 collective-permute-start
  38.6 4.7 collective-permute-start.1
  46.1 79.3 %collective-permute-done = bf16[2,511,2048]{2,0,1:T(2,128)(2,1)} collective-permute-done((bf16[2,511,2048]{2,0,1:T(2,128)(2,1)}, bf16[2,511,2048]{2,0,1:T(2,128)(2,1)}, u32[]{:S(2)}, u32[]{:S(2)}) %collective-permute-start) | collective-permute-done | bytes 4186144 | tf_op jit(solution)/shard_map/ppermute | solution.py:14
  125.5 8.7 %fusion.65 = (bf16[1,511,2048]{2,0,1:T(2,128)(2,1)S(1)}, bf16[1,511,2048]{2,0,1:T(2,128)(2,1)S(1)}) fusion(bf16[2,511,2048]{2,0,1:T(2,128)(2,1)} %collective-permute-done), kind=kLoop, calls=%fused_computation.174 | loop fusion | bytes 8372224 | tf_op jit(solution)/shard_map/slice | solution.py:115
  134.1 4.7 copy_bitcast_fusion.1
  138.8 75.4 %collective-permute-done.1 = bf16[2,512,2048]{2,1,0:T(8,128)(2,1)} collective-permute-done((bf16[2,512,2048]{2,1,0:T(8,128)(2,1)}, bf16[2,512,2048]{2,1,0:T(8,128)(2,1)}, u32[]{:S(2)}, u32[]{:S(2)}) %collective-permute-start.1) | collective-permute-done | bytes 4194336 | tf_op jit(solution)/shard_map/ppermute | solution.py:14
  214.2 4.8 slice_bitcast_fusion
  219.0 31.6 %concatenate.10 = bf16[1535,2048]{1,0:T(8,128)(2,1)} concatenate(bf16[511,2048]{1,0:T(8,128)(2,1)} %get-tuple-element.281, bf16[512,2048]{1,0:T(8,128)(2,1)} %get-tuple-element.223, bf16[512,2048]{1,0:T(8,128)(2,1)S(1)} %bitcast.151), dimensions={0} | concatenate | bytes 12574720 | tf_op jit(solution)/shard_map/concatenate | solution.py:117
  250.6 33.6 %concatenate.9 = bf16[1535,2048]{1,0:T(8,128)(2,1)} concatenate(bf16[511,2048]{1,0:T(8,128)(2,1)} %get-tuple-element.282, bf16[512,2048]{1,0:T(8,128)(2,1)} %get-tuple-element.224, bf16[512,2048]{1,0:T(8,128)(2,1)} %bitcast.152), dimensions={0} | concatenate | bytes 12574720 | tf_op jit(solution)/shard_map/concatenate | solution.py:116
  284.2 110.0 %while.28 = (s32[]{:T(128)}, bf16[16,512,128]{2,1,0:T(8,128)(2,1)S(1)}, s32[16]{0:T(128)S(1)}, bf16[512,2048]{1,0:T(8,128)(2,1)}, bf16[1535,2048]{1,0:T(8,128)(2...) while((s32[]{:T(128)}, ...), condition=%wide.region_3.4_spmd.clone, body=%wide.region_0.3_spmd.clone.sunk | while | flops 419745792 | bytes 10504381 | solution.py:135
  404.7 4.3 compare_select_fusion.5
  409.0 5.6 select_select_fusion.1
  414.7 4.5 compare_select_fusion.12
  419.3 5.6 select_select_fusion
  425.0 4.4 compare_select_fusion.11
  429.4 5.5 fusion.51
  437.2 78.3 %all-gather.2.cloned.1.call-done = bf16[4096,2048]{1,0:T(8,128)(2,1)} async-done(((bf16[256,2048]{1,0:T(8,128)(2,1)}), bf16[4096,2048]{1,0:T(8,128)(2,1)}) %all-gather.2.cloned.1.call-update) | async-done | bytes 16777232 | tf_op jit(solution)/shard_map/all_gather | solution.py:160
  515.4 13.7 %convolution_convert_fusion.2 = bf16[4096,384]{1,0:T(8,128)(2,1)} fusion(bf16[4096,2048]{1,0:T(8,128)(2,1)} %all-gather.2.cloned.1.call-done, bf16[2048,128]{1,0:T(8,128)(2,1)S(1)} %get-tuple-element.231, bf16[2048,128]{1,0:T(8,128)(2,1)} %get-tuple-element.232, bf16[2048,128]{1,0:T(8,128)(2,1)S(1)} %get-tuple-element.230), kind=kOutput, calls=%fused_computation.52 | convolution fusion | flops 6448742400 | bytes 21495808 | tf_op jit(solution)/shard_map/dot_general | solution.py:162
  529.1 11.2 %gather_fusion.2 = bf16[2048,384]{1,0:T(8,128)(2,1)} fusion(bf16[4096,384]{1,0:T(8,128)(2,1)} %convolution_convert_fusion.2, s32[2048]{0:T(1024)S(1)} %broadcast_clamp_fusion), kind=kCustom, calls=%fused_computation.2 | custom fusion | bytes 3153920 | tf_op jit(solution)/shard_map/gather | solution.py:169
  542.5 58.0 %while.29 = (s32[]{:T(128)}, f32[2048,128]{1,0:T(8,128)S(1)}, f32[2048,128]{1,0:T(8,128)S(1)}, bf16[4,512,128]{2,1,0:T(8,128)(2,1)}, bf16[4,512,128]{2,1,0:T(8,1...) while((s32[]{:T(128)}, f32[2048,128]{1,0:T(8,128)S(1)}, ...), condition=%wide.region_13.14_spmd.clone, body=%wide.region_9.13_spmd.clone.sunk | while | flops 1636956672 | bytes 55361836 | solution.py:84
  600.4 9.1 %fusion.47 = f32[2048,2048]{1,0:T(8,128)} fusion(f32[2048,128]{1,0:T(8,128)S(1)} %get-tuple-element.106, bf16[3,2048,128]{2,1,0:T(8,128)(2,1)} %param.16), kind=kOutput, calls=%fused_computation.82 | convolution fusion | flops 1074003968 | bytes 18350080 | tf_op jit(solution)/shard_map/dot_general | solution.py:197
  609.5 24.5 %gather_fusion.3 = bf16[2048,2048]{1,0:T(8,128)(2,1)} fusion(bf16[4096,2048]{1,0:T(8,128)(2,1)} %all-gather.2.cloned.1.call-done, s32[2048]{0:T(1024)S(1)} %broadcast_clamp_fusion), kind=kCustom, calls=%fused_computation.3 | custom fusion | bytes 16785408 | tf_op jit(solution)/shard_map/gather | solution.py:168
  634.0 5.9 fusion.36
  642.4 9.1 %fusion.62 = f32[2048,2048]{1,0:T(8,128)} fusion(bf16[2048,128]{1,0:T(8,128)(2,1)S(1)} %bitcast.156, bf16[3,2048,128]{2,1,0:T(8,128)(2,1)} %param.16), kind=kOutput, calls=%fused_computation.172 | convolution fusion | flops 1073741824 | bytes 17825792 | tf_op jit(solution)/shard_map/dot_general | solution.py:197
  655.3 15.8 %add_convert_fusion = bf16[2048,2048]{1,0:T(8,128)(2,1)} fusion(f32[2048,2048]{1,0:T(8,128)} %fusion.62, f32[2048,2048]{1,0:T(8,128)} %fusion.47, f32[2048,128]{1,0:T(8,128)S(1)} %get-tuple-element.107, bf16[3,2048,128]{2,1,0:T(8,128)(2,1)} %param.16), kind=kOutput, calls=%fused_computation.51 | convolution fusion | flops 1086586880 | bytes 43515904 | tf_op jit(solution)/shard_map/dot_general | solution.py:197
  675.4 4.2 broadcast_in_dim_reshape.7
  679.6 39.6 %all-reduce.2.cloned.1.call-done = bf16[3,2048,128]{2,1,0:T(8,128)(2,1)} async-done(((bf16[3,2048,128]{2,1,0:T(8,128)(2,1)}), bf16[3,2048,128]{2,1,0:T(8,128)(2,1)}) %all-reduce.2.cloned.1.call-update) | async-done | bytes 1572880 | tf_op jit(solution)/shard_map/psum | solution.py:193
  719.1 3.3 convert_element_type.59
  722.4 86.5 %reduce-scatter.2.cloned.1.call-done = bf16[128,2048]{1,0:T(8,128)(2,1)} async-done(((bf16[2048,2048]{1,0:T(8,128)(2,1)}), bf16[128,2048]{1,0:T(8,128)(2,1)}) %reduce-scatter.2.cloned.1.call-update) | async-done | bytes 524304 | tf_op jit(solution)/shard_map/reduce_scatter | solution.py:203
  (197 shorter events, 179.6 us)
Async XLA Ops:
  7.2 508.2 %all-gather.2.cloned.1.call-start = ((), (), s32[]{:S(2)}) async-start(), calls=%async_computation.1 | async-start | bytes 17825792 | tf_op jit(solution)/shard_map/all_gather | solution.py:160
  9.3 3.3 copy-start.2
  18.3 18.0 %copy-start.3 = (bf16[1,512,2048]{2,1,0:T(8,128)(2,1)S(1)}, bf16[1,512,2048]{2,1,0:T(8,128)(2,1)}, u32[]{:S(2)}) copy-start(bf16[1,512,2048]{2,1,0:T(8,128)(2,1)} %param.12) | copy-start | bytes 6291460
  29.2 14.1 %copy-start = (s32[1,16]{1,0:T(1,128)S(1)}, s32[1,16]{1,0:T(1,128)}, u32[]{:S(2)}) copy-start(s32[1,16]{1,0:T(1,128)} %param.14) | copy-start | bytes 196
  29.2 96.3 %collective-permute-start = (bf16[2,511,2048]{2,0,1:T(2,128)(2,1)}, bf16[2,511,2048]{2,0,1:T(2,128)(2,1)}, u32[]{:S(2)}, u32[]{:S(2)}) collective-permute-start(bf16[2,511,2048]{2,0,1:T(2,128)(2,1)} %pad_maximum_fusion.1), channel_id=1, source_target_pairs={{0,16},{8,24},{16,32},{24,40},{32,48},{40,56},{48,64},{56,72},{64,... | collective-permute-start | bytes 12558344 | tf_op jit(solution)/shard_map/ppermute | solution.py:14
  38.6 175.6 %collective-permute-start.1 = (bf16[2,512,2048]{2,1,0:T(8,128)(2,1)}, bf16[2,512,2048]{2,1,0:T(8,128)(2,1)}, u32[]{:S(2)}, u32[]{:S(2)}) collective-permute-start(bf16[2,512,2048]{2,1,0:T(8,128)(2,1)} %pad_maximum_fusion), channel_id=1, source_target_pairs={{0,8},{8,16},{16,24},{24,32},{32,40},{40,48},{48,56},{56,64},{64,7... | collective-permute-start | bytes 12582920 | tf_op jit(solution)/shard_map/ppermute | solution.py:14
  250.6 33.6 %copy-start.4 = (bf16[16,512,128]{2,1,0:T(8,128)(2,1)S(1)}, bf16[16,512,128]{2,1,0:T(8,128)(2,1)}, u32[]{:S(2)}) copy-start(bf16[16,512,128]{2,1,0:T(8,128)(2,1)} %custom-call.10) | copy-start | bytes 6291460
  394.2 1.3 copy-start.5
  398.8 1.9 copy-start.10
  400.6 318.5 %all-reduce.2.cloned.1.call-start = ((), (), s32[]{:S(2)}) async-start(), calls=%async_computation.2 | async-start | bytes 3145728 | tf_op jit(solution)/shard_map/psum | solution.py:193
  554.1 1.2 copy-start.7
  557.1 1.0 copy-start.9
  566.5 1.2 copy-start.7
  569.5 1.0 copy-start.9
  578.9 1.2 copy-start.7
  581.9 1.0 copy-start.9
  591.3 1.2 copy-start.7
  594.3 1.0 copy-start.9
  634.0 6.0 copy-start.1
  634.0 6.0 copy-start.8
  655.3 153.7 %reduce-scatter.2.cloned.1.call-start = ((), (), s32[]{:S(2)}) async-start(), calls=%async_computation.3 | async-start | bytes 8912896 | tf_op jit(solution)/shard_map/reduce_scatter | solution.py:203
  671.2 1.6 copy-start.6
Sparse Core Ops, SparseCore 0:
  400.7 114.6 all-gather.1
  655.4 63.6 all-reduce.1
  723.1 85.7 reduce-scatter.1
where the time goes:
time: 828 us; the launch traced here: 816 us
  waiting for transfers between devices  359 us (43%)
  matrix products  165 us (20%)
  local copies, waits for them, and re-layouts  164 us (20%)
  other arithmetic  79.7 us (10%)
  loops' own time  21.7 us (3%)
  between operations  14.5 us (2%)
  starting transfers between devices  11.9 us (1%)
    ppermute x2, waiting for transfers between devices, passed_along(): return lax.ppermute(x, axis, pairs)  155 us
    reduce_scatter x1, waiting for transfers between devices, shards(): lax.psum_scatter(term.astype(jnp.bfloat16), 'seq', scatter_dimension=0, t...  86.5 us
    all_gather x1, waiting for transfers between devices, shards(): shard_piece = lax.all_gather(packed_rows, 'seq', axis=0, tiled=True)  78.3 us
    psum x1, waiting for transfers between devices, shards(): lax.psum(local_grads.astype(jnp.bfloat16), 'dp').astype(jnp.float32)  39.6 us
    dot_general x16, matrix products, window_head(): jnp.dot(probabilities, value_rows, preferred_element_type=jnp.float32)  36.5 us
    dot_general x16, matrix products, window_head(): lax.dot_general(query_rows, key_rows, (((1,), (1,)), ((), ())), preferred...  34.4 us
    dot_general x3, matrix products, shards(): lax.dot_general(grad_slice, proj_weights[which_proj], (((1,), (1,)), ((),...  34 us
    concatenate x1, local copies, waits for them, and re-layouts, shards(): key_ext = jnp.concatenate(before_keys + [key_rows], axis=0)  33.6 us
  transfers between devices with their start and end apart: 5, of which 5 were waited for; matrix products, arithmetic and copies ran while one was open for 10% of the time, Pallas kernels for 0%

commit v1 on v0

v1 whole, which is shorter than its diff:
```python
import functools

import jax
import jax.numpy as jnp
from jax import lax
from jax.experimental import pallas as pl
from jax.experimental.pallas import tpu as pltpu
from jax.sharding import PartitionSpec as P

HEAD = 128
BLK = 128
SEQ = "seq"
MESH = pl.DeviceIdType.MESH
SCALE = HEAD ** (-0.5)
LOG2E = 1.4426950408889634
SCALE2 = SCALE * LOG2E
LOW = -1e30
NT = (((1,), (1,)), ((), ()))
BF16 = jnp.bfloat16
F32 = jnp.float32
VMEM_LIMIT = 56 * 1024 * 1024


def window_part(query, key, value_t, bias):
    scores = lax.dot_general(key, query, NT, preferred_element_type=F32)
    if bias is not None:
        scores = scores + bias
    top = jnp.max(scores, axis=0, keepdims=True)
    weight = jnp.exp2((scores - top) * SCALE2)
    total = jnp.sum(weight, axis=0, keepdims=True)
    out = jnp.dot(value_t, weight.astype(BF16), preferred_element_type=F32)
    return out / total, top * SCALE2 + jnp.log2(total)


def merged(out_a, lse_a, out_b, lse_b):
    top = jnp.maximum(lse_a, lse_b)
    weight_a = jnp.exp2(lse_a - top)
    weight_b = jnp.exp2(lse_b - top)
    total = weight_a + weight_b
    return out_a * (weight_a / total) + out_b * (weight_b / total), top + jnp.log2(total)


def window_kernel(
    chunks, per_chunk, sel, q_in, k_in, v_in, out,
    q_own, q_one, q_two, v_t, o_own, l_own, o_snd2, l_snd2, o_got2, l_got2, o_snd1, l_snd1, o_got1, l_got1,
    bias_own, bias_two, send_sem, recv_sem,
):
    shard = lax.axis_index(SEQ)
    count = lax.axis_size(SEQ)
    right = lax.rem(shard + 1, count)
    left = lax.rem(shard + count - 1, count)
    width = per_chunk * HEAD
    rows = q_own.shape[1]
    picks = rows // BLK

    def copy(which, c, src, dst, target):
        return pltpu.make_async_remote_copy(
            src_ref=src.at[c], dst_ref=dst.at[c],
            send_sem=send_sem.at[which, c], recv_sem=recv_sem.at[which, c],
            device_id={SEQ: target}, device_id_type=MESH,
        )

    def hop_one(c):
        return copy(0, c, q_own, q_one, left)

    def hop_two(c):
        return copy(1, c, q_one, q_two, left)

    def back_two(c):
        return (copy(2, c, o_snd2, o_got2, right), copy(3, c, l_snd2, l_got2, right))

    def back_one(c):
        return (copy(4, c, o_snd1, o_got1, right), copy(5, c, l_snd1, l_got1, right))

    barrier = pltpu.get_barrier_semaphore()
    for neighbour in (left, right):
        pl.semaphore_signal(barrier, inc=1, device_id={SEQ: neighbour}, device_id_type=MESH)

    for a in range(picks):
        block = q_in[sel[a]]
        for c in range(chunks):
            q_own[c, a * BLK : (a + 1) * BLK, :] = block[:, c * width : (c + 1) * width]
    pl.semaphore_wait(barrier, 2)
    for c in range(chunks):
        hop_one(c).start()

    lane = lax.broadcasted_iota(jnp.int32, (1, rows), 1)
    key_at = lax.broadcasted_iota(jnp.int32, bias_own.shape, 0)
    for base, ref in ((0, bias_own), (2 * picks, bias_two)):
        place = lane
        for a in range(picks):
            place = jnp.where(lane // BLK == a, (lane - a * BLK) + sel[base + a] * BLK, place)
        seen = (key_at <= place) if base == 0 else (key_at > place)
        ref[...] = jnp.where(seen, 0.0, LOW)

    def head_of(c, h):
        return pl.ds(pl.multiple_of(c * width + h * HEAD, HEAD), HEAD)

    def spread(row):
        return jnp.broadcast_to(row, (8 // per_chunk, rows))

    def lse_rows(h):
        return slice(h * (8 // per_chunk), (h + 1) * (8 // per_chunk))

    def own_part(c, carry):
        hop_one(c).wait_recv()
        hop_two(c).start()
        for h in range(per_chunk):
            cols = head_of(c, h)
            value_t = v_in[:, cols].T
            v_t[cols, :] = value_t
            part, lse = window_part(
                q_own[c, :, h * HEAD : (h + 1) * HEAD], k_in[:, cols], value_t, bias_own[...]
            )
            o_own[c, h * HEAD : (h + 1) * HEAD, :] = part
            l_own[c, lse_rows(h), :] = spread(lse)
        return carry

    lax.fori_loop(0, chunks, own_part, 0)

    def step(t, carry):
        @pl.when(t < chunks)
        def _():
            c = t
            hop_two(c).wait_recv()
            for h in range(per_chunk):
                cols = head_of(c, h)
                part, lse = window_part(
                    q_two[c, :, h * HEAD : (h + 1) * HEAD], k_in[:, cols], v_t[cols, :], bias_two[...]
                )
                o_snd2[c, h * HEAD : (h + 1) * HEAD, :] = part.astype(BF16)
                l_snd2[c, lse_rows(h), :] = spread(lse)
            for one in back_two(c):
                one.start()

        @pl.when((t >= 1) & (t <= chunks))
        def _():
            c = t - 1
            parts = []
            for h in range(per_chunk):
                cols = head_of(c, h)
                parts.append(
                    window_part(q_one[c, :, h * HEAD : (h + 1) * HEAD], k_in[:, cols], v_t[cols, :], None)
                )
            for one in back_two(c):
                one.wait_recv()
            for h in range(per_chunk):
                part, lse = parts[h]
                lse_in = jnp.where(shard == 0, LOW, l_got2[c, h * (8 // per_chunk) : h * (8 // per_chunk) + 1, :])
                part, lse = merged(part, lse, o_got2[c, h * HEAD : (h + 1) * HEAD, :].astype(F32), lse_in)
                o_snd1[c, h * HEAD : (h + 1) * HEAD, :] = part.astype(BF16)
                l_snd1[c, lse_rows(h), :] = spread(lse)
            for one in back_one(c):
                one.start()

        @pl.when(t >= 2)
        def _():
            c = t - 2
            for one in back_one(c):
                one.wait_recv()
            for h in range(per_chunk):
                first = h * (8 // per_chunk)
                lse_in = jnp.where(shard == 0, LOW, l_got1[c, first : first + 1, :])
                part, lse = merged(
                    o_own[c, h * HEAD : (h + 1) * HEAD, :], l_own[c, first : first + 1, :],
                    o_got1[c, h * HEAD : (h + 1) * HEAD, :].astype(F32), lse_in,
                )
                final = part.T.astype(BF16)
                for a in range(picks):
                    out[a, :, head_of(c, h)] = final[a * BLK : (a + 1) * BLK, :]

        return carry

    lax.fori_loop(0, chunks + 2, step, 0)

    def drain(c, carry):
        hop_one(c).wait_send()
        hop_two(c).wait_send()
        for one in back_two(c) + back_one(c):
            one.wait_send()
        return carry

    lax.fori_loop(0, chunks, drain, 0)


def window(sel, query, key, value, part, parts, per_chunk, ident):
    blocks, _, full = query.shape
    tok = key.shape[0]
    cols = full // parts
    chunks = cols // HEAD // per_chunk
    width = per_chunk * HEAD
    rows = sel.shape[0] // 3 * BLK
    out_t = (chunks, width, rows)
    lse_t = (chunks, 8, rows)
    return pl.pallas_call(
        functools.partial(window_kernel, chunks, per_chunk),
        out_shape=jax.ShapeDtypeStruct((rows // BLK, BLK, cols), BF16),
        grid=(1,),
        in_specs=[
            pl.BlockSpec(memory_space=pltpu.SMEM),
            pl.BlockSpec((blocks, BLK, cols), lambda g: (0, 0, part)),
            pl.BlockSpec((tok, cols), lambda g: (0, part)),
            pl.BlockSpec((tok, cols), lambda g: (0, part)),
        ],
        out_specs=pl.BlockSpec((rows // BLK, BLK, cols), lambda g: (0, 0, 0)),
        scratch_shapes=[
            pltpu.VMEM((chunks, rows, width), BF16),
            pltpu.VMEM((chunks, rows, width), BF16),
            pltpu.VMEM((chunks, rows, width), BF16),
            pltpu.VMEM((cols, tok), BF16),
            pltpu.VMEM(out_t, F32),
            pltpu.VMEM(lse_t, F32),
            pltpu.VMEM(out_t, BF16),
            pltpu.VMEM(lse_t, F32),
            pltpu.VMEM(out_t, BF16),
            pltpu.VMEM(lse_t, F32),
            pltpu.VMEM(out_t, BF16),
            pltpu.VMEM(lse_t, F32),
            pltpu.VMEM(out_t, BF16),
            pltpu.VMEM(lse_t, F32),
            pltpu.VMEM((tok, rows), F32),
            pltpu.VMEM((tok, rows), F32),
            pltpu.SemaphoreType.DMA((6, chunks)),
            pltpu.SemaphoreType.DMA((6, chunks)),
        ],
        compiler_params=pltpu.CompilerParams(
            collective_id=ident, has_side_effects=True, vmem_limit_bytes=VMEM_LIMIT
        ),
        cost_estimate=pl.CostEstimate(
            flops=12 * rows * tok * cols, bytes_accessed=16 * 1024 * 1024 * cols // full, transcendentals=0
        ),
        name=f"window_{ident}",
    )(sel, query, key, value)


def project_kernel(index, a0, a1, b0, b1, weights, normed, projected):
    half = a0.shape[2]
    eps_width = 2 * half
    pieces = []
    for low, high in ((a0, b0), (a1, b1)):
        x0 = low[0].astype(F32)
        x1 = high[0].astype(F32)
        mean = (
            jnp.sum(x0 * x0, axis=1, keepdims=True) + jnp.sum(x1 * x1, axis=1, keepdims=True)
        ) * (1.0 / eps_width)
        inv = lax.rsqrt(mean + 1e-06)
        pieces.append(((x0 * inv).astype(BF16), (x1 * inv).astype(BF16)))
    n0 = jnp.concatenate([pieces[0][0], pieces[1][0]], axis=0)
    n1 = jnp.concatenate([pieces[0][1], pieces[1][1]], axis=0)
    normed[:, :half] = n0
    normed[:, half:] = n1
    projected[...] = (
        jnp.dot(n0, weights[:half, :], preferred_element_type=F32)
        + jnp.dot(n1, weights[half:, :], preferred_element_type=F32)
    ).astype(BF16)


def project(index, low, high, weights):
    kept = index.shape[0]
    half = low.shape[2]
    local = weights.shape[1]
    block = (1, BLK, half)
    return pl.pallas_call(
        project_kernel,
        out_shape=(
            jax.ShapeDtypeStruct((kept * BLK, 2 * half), BF16),
            jax.ShapeDtypeStruct((kept * BLK, local), BF16),
        ),
        grid_spec=pltpu.PrefetchScalarGridSpec(
            num_scalar_prefetch=1,
            grid=(kept // 2,),
            in_specs=[
                pl.BlockSpec(block, lambda g, idx: (idx[2 * g], 0, 0)),
                pl.BlockSpec(block, lambda g, idx: (idx[2 * g + 1], 0, 0)),
                pl.BlockSpec(block, lambda g, idx: (idx[2 * g], 0, 0)),
                pl.BlockSpec(block, lambda g, idx: (idx[2 * g + 1], 0, 0)),
                pl.BlockSpec((2 * half, local), lambda g, idx: (0, 0)),
            ],
            out_specs=[
                pl.BlockSpec((2 * BLK, 2 * half), lambda g, idx: (g, 0)),
                pl.BlockSpec((2 * BLK, local), lambda g, idx: (g, 0)),
            ],
        ),
        compiler_params=pltpu.CompilerParams(vmem_limit_bytes=VMEM_LIMIT),
        name="project",
    )(index, low, low, high, high, weights)


QB = 256
KB = 512


def causal_kernel(dest, qkv, cot, out, d_all, d_all_t, v_t, k_t, do_own, do_t, p_buf, dk_acc, dv_acc, dq_t):
    kept = dest.shape[0]
    total_rows = qkv.shape[0]
    for j in range(kept):
        do_own[j * BLK : (j + 1) * BLK, :] = cot[pl.ds(pl.multiple_of(dest[j] * BLK, BLK), BLK), :]

    def prepare(c, carry):
        at = pl.ds(pl.multiple_of(c * QB, QB), QB)
        k_t[:, at] = qkv[at, HEAD : 2 * HEAD].T
        v_t[:, at] = qkv[at, 2 * HEAD : 3 * HEAD].T
        do_t[:, at] = do_own[at, :].T
        return carry

    lax.fori_loop(0, total_rows // QB, prepare, 0)
    dk_acc[...] = jnp.zeros_like(dk_acc)
    dv_acc[...] = jnp.zeros_like(dv_acc)
    key_at = lax.broadcasted_iota(jnp.int32, (KB, QB), 0)
    row_at = lax.broadcasted_iota(jnp.int32, (KB, QB), 1)

    for i in range(total_rows // QB):
        rows = slice(i * QB, (i + 1) * QB)
        chunks = (i + 1) * QB // KB + (1 if (i + 1) * QB % KB else 0)
        q_i = qkv[rows, :HEAD]
        do_i = do_own[rows, :]

        def scores_of(c, masked):
            keys = pl.ds(pl.multiple_of(c * KB, KB), KB)
            scores = lax.dot_general(qkv[keys, HEAD : 2 * HEAD], q_i, NT, preferred_element_type=F32)
            if masked:
                scores = jnp.where(key_at <= row_at + (i * QB - (chunks - 1) * KB), scores, LOW)
            p_buf[keys, :] = scores
            return jnp.max(scores, axis=0, keepdims=True)

        top = scores_of(chunks - 1, True)
        if chunks > 1:
            top = lax.fori_loop(0, chunks - 1, lambda c, m: jnp.maximum(m, scores_of(c, False)), top)

        def weigh(c, carry):
            total, acc = carry
            keys = pl.ds(pl.multiple_of(c * KB, KB), KB)
            weight = jnp.exp2((p_buf[keys, :] - top) * SCALE2)
            p_buf[keys, :] = weight
            total = total + jnp.sum(weight, axis=0, keepdims=True)
            acc = acc + jnp.dot(v_t[:, keys], weight.astype(BF16), preferred_element_type=F32)
            return total, acc

        total, acc = lax.fori_loop(
            0, chunks, weigh, (jnp.zeros((1, QB), F32), jnp.zeros((HEAD, QB), F32))
        )
        inv = 1.0 / total
        o_t = acc * inv
        delta = jnp.sum(o_t * do_t[:, rows].astype(F32), axis=0, keepdims=True)
        o_i = o_t.T.astype(BF16)
        for b in range(QB // BLK):
            slot = dest[i * (QB // BLK) + b]
            out[pl.ds(pl.multiple_of(slot * BLK, BLK), BLK), :] = o_i[b * BLK : (b + 1) * BLK, :]

        def back(c, acc):
            keys = pl.ds(pl.multiple_of(c * KB, KB), KB)
            soft = p_buf[keys, :] * inv
            dv_acc[keys, :] += jnp.dot(soft.astype(BF16), do_i, preferred_element_type=F32)
            d_probs = lax.dot_general(qkv[keys, 2 * HEAD :], do_i, NT, preferred_element_type=F32)
            d_scores = (soft * (d_probs - delta) * SCALE).astype(BF16)
            dk_acc[keys, :] += jnp.dot(d_scores, q_i, preferred_element_type=F32)
            return acc + jnp.dot(k_t[:, keys], d_scores, preferred_element_type=F32)

        dq_t[:, rows] = lax.fori_loop(0, chunks, back, jnp.zeros((HEAD, QB), F32))

    def finish(c, carry):
        at = pl.ds(pl.multiple_of(c * QB, QB), QB)
        d_q = dq_t[:, at]
        d_all_t[:HEAD, at] = d_q.astype(BF16)
        d_all[at, :HEAD] = d_q.T.astype(BF16)
        for which, acc in ((1, dk_acc), (2, dv_acc)):
            value = acc[at, :]
            d_all[at, which * HEAD : (which + 1) * HEAD] = value.astype(BF16)
            d_all_t[which * HEAD : (which + 1) * HEAD, at] = value.T.astype(BF16)
        return carry

    lax.fori_loop(0, total_rows // QB, finish, 0)


def causal(dest, qkv, cot):
    total_rows, local = qkv.shape
    vmem = pl.BlockSpec(memory_space=pltpu.VMEM)
    return pl.pallas_call(
        causal_kernel,
        out_shape=(
            jax.ShapeDtypeStruct((total_rows, HEAD), BF16),
            jax.ShapeDtypeStruct((total_rows, local), BF16),
            jax.ShapeDtypeStruct((local, total_rows), BF16),
        ),
        in_specs=[pl.BlockSpec(memory_space=pltpu.SMEM), vmem, vmem],
        out_specs=[vmem, vmem, vmem],
        scratch_shapes=[
            pltpu.VMEM((HEAD, total_rows), BF16),
            pltpu.VMEM((HEAD, total_rows), BF16),
            pltpu.VMEM((total_rows, HEAD), BF16),
            pltpu.VMEM((HEAD, total_rows), BF16),
            pltpu.VMEM((total_rows, QB), F32),
            pltpu.VMEM((total_rows, HEAD), F32),
            pltpu.VMEM((total_rows, HEAD), F32),
            pltpu.VMEM((HEAD, total_rows), F32),
        ],
        compiler_params=pltpu.CompilerParams(vmem_limit_bytes=VMEM_LIMIT),
        name="causal",
    )(dest, qkv, cot)


def term_kernel(dest, d_all, weights, out):
    value = lax.dot_general(d_all[...], weights[...], NT, preferred_element_type=F32).astype(BF16)
    for j in range(value.shape[0] // BLK):
        out[pl.ds(pl.multiple_of(dest[j] * BLK, BLK), BLK), :] = value[j * BLK : (j + 1) * BLK, :]


def term(dest, d_all, weights, step=256):
    total_rows, local = d_all.shape
    full = weights.shape[0]
    return pl.pallas_call(
        term_kernel,
        out_shape=jax.ShapeDtypeStruct((total_rows, full), BF16),
        grid=(full // step,),
        in_specs=[
            pl.BlockSpec(memory_space=pltpu.SMEM),
            pl.BlockSpec((total_rows, local), lambda g: (0, 0)),
            pl.BlockSpec((step, local), lambda g: (g, 0)),
        ],
        out_specs=pl.BlockSpec((total_rows, step), lambda g: (0, g)),
        compiler_params=pltpu.CompilerParams(vmem_limit_bytes=VMEM_LIMIT),
        name="term",
    )(dest, d_all, weights)


def weight_grad_kernel(d_t, normed, out):
    value = jnp.dot(d_t[...], normed[...], preferred_element_type=F32)
    for at in range(3):
        out[at] = value[at * HEAD : (at + 1) * HEAD, :].T.astype(BF16)


def weight_grad(d_t, normed, step=256):
    local, total_rows = d_t.shape
    full = normed.shape[1]
    return pl.pallas_call(
        weight_grad_kernel,
        out_shape=jax.ShapeDtypeStruct((3, full, HEAD), BF16),
        grid=(full // step,),
        in_specs=[
            pl.BlockSpec((local, total_rows), lambda g: (0, 0)),
            pl.BlockSpec((total_rows, step), lambda g: (0, g)),
        ],
        out_specs=pl.BlockSpec((3, step, HEAD), lambda g: (0, g, 0)),
        compiler_params=pltpu.CompilerParams(vmem_limit_bytes=VMEM_LIMIT),
        name="weight_grad",
    )(d_t, normed)


def assemble_kernel(table, low, high, rest, out):
    first = table[3 * pl.program_id(0)] == 1

    @pl.when(first)
    def _():
        half = low.shape[2]
        out[:, :half] = low[0]
        out[:, half:] = high[0]

    @pl.when(jnp.logical_not(first))
    def _():
        out[...] = rest[0]


def assemble(table, low, high, rest):
    blocks = 2 * low.shape[0]
    half = low.shape[2]
    return pl.pallas_call(
        assemble_kernel,
        out_shape=jax.ShapeDtypeStruct((blocks * BLK, 2 * half), BF16),
        grid_spec=pltpu.PrefetchScalarGridSpec(
            num_scalar_prefetch=1,
            grid=(blocks,),
            in_specs=[
                pl.BlockSpec((1, BLK, half), lambda g, t: (t[3 * g + 1], 0, 0)),
                pl.BlockSpec((1, BLK, half), lambda g, t: (t[3 * g + 1], 0, 0)),
                pl.BlockSpec((1, BLK, 2 * half), lambda g, t: (t[3 * g + 2], 0, 0)),
            ],
            out_specs=pl.BlockSpec((BLK, 2 * half), lambda g, t: (g, 0)),
        ),
        name="assemble",
    )(table, low, high, rest)


def shards(query_input, key_input, value_input, keep_blocks, dest_slots, proj_weights, cotangent):
    tok, full = query_input.shape[1:]
    per_shard = tok // BLK
    shard = lax.axis_index(SEQ)
    count = lax.axis_size(SEQ)
    half_blocks = per_shard // 2
    query = query_input.reshape(per_shard, BLK, full)
    key = key_input[0]
    value = value_input[0]
    keep = keep_blocks[0]
    dest = dest_slots[0]

    kept = jnp.any(
        keep[None, None, :] == jnp.arange(count * per_shard).reshape(count, per_shard)[:, :, None], axis=2
    )
    order_key = jnp.where(kept, 0, per_shard) + jnp.arange(per_shard)[None, :]
    rank = jnp.sum(order_key[:, None, :] < order_key[:, :, None], axis=2).astype(jnp.int32)
    order = jnp.sum(
        jnp.where(
            rank[:, None, :] == jnp.arange(per_shard)[None, :, None], jnp.arange(per_shard)[None, None, :], 0
        ),
        axis=2,
    ).astype(jnp.int32)
    wrapped = jnp.concatenate([order, order[:2]], axis=0)
    near = lax.dynamic_slice_in_dim(wrapped, shard, 3, 0)
    sel_first = near[:, :half_blocks].reshape(-1)
    sel_rest = near[:, half_blocks:].reshape(-1)
    own_rank = lax.dynamic_slice_in_dim(rank, shard, 1, 0)[0]
    in_first = (own_rank < half_blocks).astype(jnp.int32)
    at = own_rank % half_blocks
    table = jnp.stack([in_first, at * in_first, at * (1 - in_first)], axis=1).reshape(-1)
    keep_shard = keep // per_shard
    before = jnp.sum((keep_shard[None, :] == keep_shard[:, None]) & (keep[None, :] < keep[:, None]), axis=1)
    packed = (keep_shard * half_blocks + before).astype(jnp.int32)
    weights = jnp.concatenate([proj_weights[0], proj_weights[1], proj_weights[2]], axis=1)

    low = window(sel_first, query, key, value, 0, 2, 2, 0)
    low_all = lax.all_gather(low, SEQ, axis=0, tiled=True)
    high = window(sel_first, query, key, value, 1, 2, 2, 1)
    high_all = lax.all_gather(high, SEQ, axis=0, tiled=True)

    normed, qkv = project(packed, low_all, high_all, weights)
    causal_out, d_all, d_all_t = causal(dest, qkv, cotangent[0])
    terms = term(dest, d_all, weights)
    row_grad = lax.psum_scatter(terms, SEQ, scatter_dimension=0, tiled=True)
    grads = weight_grad(d_all_t, normed)
    grads = lax.psum(grads, "dp").astype(F32)
    sel_late, terms = lax.optimization_barrier((sel_rest, d_all))
    rest = window(sel_late, query, key, value, 0, 1, 2, 2)
    window_out = assemble(table, low, high, rest)
    return (window_out[None], causal_out[None], grads, row_grad[None])


def solution(mesh):
    return jax.shard_map(
        shards,
        mesh=mesh,
        in_specs=(
            P("dp", "seq", None),
            P("dp", "seq", None),
            P("dp", "seq", None),
            P("dp", None),
            P("dp", None),
            P(None, None, "seq"),
            P("dp", None, "seq"),
        ),
        out_specs=(
            P("dp", "seq", None),
            P("dp", None, "seq"),
            P(None, None, "seq"),
            P("dp", "seq", None),
        ),
        check_vma=False,
    )
```

time: 828 us -> 440 us (0.53); the launches traced: 816 us -> 440 us
  Pallas kernels: 0 us -> 289 us
  waiting for transfers between devices: 359 us -> 128 us
  matrix products: 165 us -> 0 us
  local copies, waits for them, and re-layouts: 164 us -> 2.42 us
  other arithmetic: 79.7 us -> 6.38 us
  loops' own time: 21.7 us -> 0 us
  starting transfers between devices: 11.9 us -> 0.57 us
    pallas_call x0 -> x8, Pallas kernels: none -> 289 us  [the longest x3 228 us: window(): pl.pallas_call(functools.partial(window_kernel, chunks, per_chunk), out_s...]
    dot_general x63 -> x0, matrix products: 165 us -> none  [the longest x16 36.5 us: window_head(): jnp.dot(probabilities, value_rows, preferred_element_type=jnp.float32)]
    ppermute x2 -> x0, waiting for transfers between devices: 155 us -> none  [passed_along(): return lax.ppermute(x, axis, pairs)]
    concatenate x2 -> x0, local copies, waits for them, and re-layouts: 65.2 us -> none  [the longest x1 33.6 us: shards(): key_ext = jnp.concatenate(before_keys + [key_rows], axis=0)]
    reduce_scatter x1, waiting for transfers between devices: 86.5 us -> 36.6 us  [shards(): row_grad = lax.psum_scatter(terms, SEQ, scatter_dimension=0, tiled=True)]
    gather x7 -> x0, local copies, waits for them, and re-layouts: 39.8 us -> none  [the longest x1 24.5 us: shards(): gathered = gathered[packed_index]]
    psum x1, waiting for transfers between devices: 39.6 us -> 0.01 us  [shards(): grads = lax.psum(grads, 'dp').astype(F32)]
    reduce_sum x23 -> x3, other arithmetic: 25.2 us -> 0.23 us  [the longest x1 0.18 us: shards(): jnp.sum((keep_shard[None, :] == keep_shard[:, None]) & (keep[None, :] < k...]
  transfers between devices with their start and end apart: 5 -> 4, of which waited for: 5 -> 3; matrix products, arithmetic and copies ran while one was open for 10% -> 2% of each run, Pallas kernels for 0% -> 42%
where the time goes in v1:
time: 440 us
  Pallas kernels  289 us (66%)
  waiting for transfers between devices  128 us (29%)
  between operations  13.9 us (3%)
  other arithmetic  6.38 us (1%)
    pallas_call x3, Pallas kernels, window(): pl.pallas_call(functools.partial(window_kernel, chunks, per_chunk), out_s...  228 us
    all_gather x1, waiting for transfers between devices, shards(): low_all = lax.all_gather(low, SEQ, axis=0, tiled=True)  71 us
    reduce_scatter x1, waiting for transfers between devices, shards(): row_grad = lax.psum_scatter(terms, SEQ, scatter_dimension=0, tiled=True)  36.6 us
    pallas_call x1, Pallas kernels, causal(): pl.pallas_call(causal_kernel, out_shape=(jax.ShapeDtypeStruct((total_rows...  24.8 us
    all_gather x1, waiting for transfers between devices, shards(): high_all = lax.all_gather(high, SEQ, axis=0, tiled=True)  19.9 us
    pallas_call x1, Pallas kernels, project(): pl.pallas_call(project_kernel, out_shape=(jax.ShapeDtypeStruct((kept * BL...  12 us
    pallas_call x1, Pallas kernels, term(): pl.pallas_call(term_kernel, out_shape=jax.ShapeDtypeStruct((total_rows, f...  10.1 us
    pallas_call x1, Pallas kernels, weight_grad(): pl.pallas_call(weight_grad_kernel, out_shape=jax.ShapeDtypeStruct((3, ful...  9.82 us
  transfers between devices with their start and end apart: 4, of which 3 were waited for; matrix products, arithmetic and copies ran while one was open for 2% of the time, Pallas kernels for 42%

profile of v1, /device:TPU:0, one launch (start us, length us, event | category | flops | bytes accessed | tf_op | source)
XLA Modules:
  0.0 439.6 jit_solution(10459667270271868574)
XLA Ops:
  7.2 0.0 all-gather.5.cloned.1.call-start
  7.2 0.9 compare_reduce_fusion
  8.2 0.1 pad_add_fusion.1
  8.2 0.1 constant_dynamic-slice_fusion
  8.3 0.1 copy.20
  8.4 0.6 reshape.170.sel
  9.0 55.5 %window_1.1.high = bf16[2,128,1024]{2,1,0:T(8,128)(2,1)} custom-call(s32[6]{0:T(128)} %reshape.170.sel, bf16[4,128,2048]{2,1,0:T(8,128)(2,1)} %bitcast.31, bf16[512,2048]{1,0:T(8,128)(2,1)} %bitcast.34, bf16[512,2048]{1,0:T(8,128)(2,1)} %bitcast.37), custom_call_target="tpu_custom_call" | custom-call | flops 1610612736 | bytes 8388608 | tf_op jit(solution)/shard_map/window_1/pallas_call | solution.py:195
  64.5 0.0 all-gather.5.cloned.1.call-update
  64.5 0.0 all-gather.3.cloned.1.call-start
  64.6 65.4 %window_0.1.low = bf16[2,128,1024]{2,1,0:T(8,128)(2,1)} custom-call(s32[6]{0:T(128)} %reshape.170.sel, bf16[4,128,2048]{2,1,0:T(8,128)(2,1)} %bitcast.32, bf16[512,2048]{1,0:T(8,128)(2,1)} %bitcast.35, bf16[512,2048]{1,0:T(8,128)(2,1)} %bitcast.38), custom_call_target="tpu_custom_call" | custom-call | flops 1610612736 | bytes 8388608 | tf_op jit(solution)/shard_map/window_0/pallas_call | solution.py:195
  130.0 0.0 all-gather.3.cloned.1.call-update
  130.0 0.2 all-reduce.2.cloned.1.call-start
  130.3 0.2 convert_reduce_fusion
  130.4 0.5 multiply_add_fusion.1.index
  131.0 0.1 slice_bitcast_fusion.2
  131.1 1.3 pad_maximum_fusion.weights
  132.4 19.9 %all-gather.5.cloned.1.call-done.b0.b1 = bf16[32,128,1024]{2,1,0:T(8,128)(2,1)} async-done(((bf16[2,128,1024]{2,1,0:T(8,128)(2,1)}), bf16[32,128,1024]{2,1,0:T(8,128)(2,1)}) %all-gather.5.cloned.1.call-update) | async-done | bytes 8388624 | tf_op jit(solution)/shard_map/all_gather | solution.py:522
  152.4 71.0 %all-gather.3.cloned.1.call-done.a0.a1 = bf16[32,128,1024]{2,1,0:T(8,128)(2,1)} async-done(((bf16[2,128,1024]{2,1,0:T(8,128)(2,1)}), bf16[32,128,1024]{2,1,0:T(8,128)(2,1)}) %all-gather.3.cloned.1.call-update) | async-done | bytes 8388624 | tf_op jit(solution)/shard_map/all_gather | solution.py:520
  223.3 12.0 %project.1 = (bf16[2048,2048]{1,0:T(8,128)(2,1)}, bf16[2048,384]{1,0:T(8,128)(2,1)}) custom-call(s32[16]{0:T(128)} %multiply_add_fusion.1.index, bf16[32,128,1024]{2,1,0:T(8,128)(2,1)} %all-gather.3.cloned.1.call-done.a0.a1, bf16[32,128,1024]{2,1,0:T(8,128)(2,1)} %all-gather.3.cloned.1.call-done.a0.a1, ...), custom_call_target="tpu_custom_call" | custom-call | tf_op jit(solution)/shard_map/project/pallas_call | solution.py:263
  235.3 24.8 %causal.1 = (bf16[2048,128]{1,0:T(8,128)(2,1)}, bf16[2048,384]{1,0:T(8,128)(2,1)}, bf16[384,2048]{1,0:T(8,128)(2,1)}) custom-call(s32[16]{0:T(128)} %bitcast.45, bf16[2048,384]{1,0:T(8,128)(2,1)} %get-tuple-element.10.qkv, bf16[2048,128]{1,0:T(8,128)(2,1)} %bitcast.41), custom_call_target="tpu_custom_call" | custom-call | tf_op jit(solution)/shard_map/causal/pallas_call | solution.py:378
  260.1 9.8 %weight_grad.1 = bf16[3,2048,128]{2,1,0:T(8,128)(2,1)} custom-call(bf16[384,2048]{1,0:T(8,128)(2,1)} %get-tuple-element.14.d_t, bf16[2048,2048]{1,0:T(8,128)(2,1)} %get-tuple-element.15.normed), custom_call_target="tpu_custom_call" | custom-call | tf_op jit(solution)/shard_map/weight_grad/pallas_call | solution.py:435
  269.9 0.3 reduce-scatter.2.cloned.1.call-start
  270.2 10.1 %term.1 = bf16[2048,2048]{1,0:T(8,128)(2,1)} custom-call(s32[16]{0:T(128)} %bitcast.46, bf16[2048,384]{1,0:T(8,128)(2,1)} %get-tuple-element.11.d_all, bf16[2048,384]{1,0:T(8,128)(2,1)} %pad_maximum_fusion.weights), custom_call_target="tpu_custom_call" | custom-call | tf_op jit(solution)/shard_map/term/pallas_call | solution.py:411
  280.3 0.2 dynamic-slice_reduce_fusion
  280.5 0.1 copy.19
  280.6 0.6 reshape.169.table
  281.2 0.1 copy.21
  281.3 0.6 reshape.172.sel
  281.9 106.7 %window_2.1.rest = bf16[2,128,2048]{2,1,0:T(8,128)(2,1)} custom-call(s32[6]{0:T(128)} %reshape.172.sel, bf16[4,128,2048]{2,1,0:T(8,128)(2,1)} %bitcast.33, bf16[512,2048]{1,0:T(8,128)(2,1)} %bitcast.36, bf16[512,2048]{1,0:T(8,128)(2,1)} %bitcast.39), custom_call_target="tpu_custom_call" | custom-call | flops 3221225472 | bytes 16777216 | tf_op jit(solution)/shard_map/window_2/pallas_call | solution.py:195
  388.5 4.7 %assemble.1 = bf16[512,2048]{1,0:T(8,128)(2,1)} custom-call(s32[12]{0:T(128)} %reshape.169.table, bf16[2,128,1024]{2,1,0:T(8,128)(2,1)} %window_0.1.low, bf16[2,128,1024]{2,1,0:T(8,128)(2,1)} %window_1.1.high, bf16[2,128,2048]{2,1,0:T(8,128)(2,1)} %window_2.1.rest), custom_call_target="tpu_custom_call" | custom-call | tf_op jit(solution)/shard_map/assemble/pallas_call | solution.py:466
  393.2 3.3 convert_element_type.26
  396.5 36.6 %reduce-scatter.2.cloned.1.call-done = bf16[128,2048]{1,0:T(8,128)(2,1)} async-done(((bf16[2048,2048]{1,0:T(8,128)(2,1)}), bf16[128,2048]{1,0:T(8,128)(2,1)}) %reduce-scatter.2.cloned.1.call-update) | async-done | bytes 524304 | tf_op jit(solution)/shard_map/reduce_scatter | solution.py:527
  (17 shorter events, 0.2 us)
Async XLA Ops:
  7.2 145.2 %all-gather.5.cloned.1.call-start = ((), (), s32[]{:S(2)}) async-start(), calls=%async_computation.2 | async-start | bytes 8912896 | tf_op jit(solution)/shard_map/all_gather | solution.py:522
  64.5 65.7 %copy-start.1 = (s32[1,16]{1,0:T(1,128)S(1)}, s32[1,16]{1,0:T(1,128)}, u32[]{:S(2)}) copy-start(s32[1,16]{1,0:T(1,128)} %param.10) | copy-start | bytes 196
  64.5 66.4 %copy-start = (bf16[3,2048,128]{2,1,0:T(8,128)(2,1)S(1)}, bf16[3,2048,128]{2,1,0:T(8,128)(2,1)}, u32[]{:S(2)}) copy-start(bf16[3,2048,128]{2,1,0:T(8,128)(2,1)} %param.12) | copy-start | bytes 4718596
  64.5 158.8 %all-gather.3.cloned.1.call-start = ((), (), s32[]{:S(2)}) async-start(), calls=%async_computation.1 | async-start | bytes 8912896 | tf_op jit(solution)/shard_map/all_gather | solution.py:520
  130.0 263.2 %all-reduce.2.cloned.1.call-start = ((), (), s32[]{:S(2)}) async-start(), calls=%async_computation.3 | async-start | bytes 3145728 | tf_op jit(solution)/shard_map/psum | solution.py:529
  269.9 163.2 %reduce-scatter.2.cloned.1.call-start = ((), (), s32[]{:S(2)}) async-start(), calls=%async_computation.4 | async-start | bytes 8912896 | tf_op jit(solution)/shard_map/reduce_scatter | solution.py:527
Sparse Core Ops, SparseCore 0:
  64.6 87.6 all-gather.4
  154.5 68.7 all-gather.2
  270.0 64.1 all-reduce.1
  338.1 94.9 reduce-scatter.1

commit v2 on v1

--- a/solution.py
+++ b/solution.py
@@ -49,6 +49,8 @@
     count = lax.axis_size(SEQ)
     right = lax.rem(shard + 1, count)
     left = lax.rem(shard + count - 1, count)
+    right_two = lax.rem(shard + 2, count)
+    left_two = lax.rem(shard + count - 2, count)
     width = per_chunk * HEAD
     rows = q_own.shape[1]
     picks = rows // BLK
@@ -64,7 +66,7 @@
         return copy(0, c, q_own, q_one, left)
 
     def hop_two(c):
-        return copy(1, c, q_one, q_two, left)
+        return copy(1, c, q_own, q_two, left_two)
 
     def back_two(c):
         return (copy(2, c, o_snd2, o_got2, right), copy(3, c, l_snd2, l_got2, right))
@@ -73,16 +75,21 @@
         return (copy(4, c, o_snd1, o_got1, right), copy(5, c, l_snd1, l_got1, right))
 
     barrier = pltpu.get_barrier_semaphore()
-    for neighbour in (left, right):
+    for neighbour in (left, right, left_two, right_two):
         pl.semaphore_signal(barrier, inc=1, device_id={SEQ: neighbour}, device_id_type=MESH)
 
     for a in range(picks):
         block = q_in[sel[a]]
         for c in range(chunks):
             q_own[c, a * BLK : (a + 1) * BLK, :] = block[:, c * width : (c + 1) * width]
-    pl.semaphore_wait(barrier, 2)
-    for c in range(chunks):
+    pl.semaphore_wait(barrier, 4)
+
+    def send(c, carry):
+        hop_two(c).start()
         hop_one(c).start()
+        return carry
+
+    lax.fori_loop(0, chunks, send, 0)
 
     lane = lax.broadcasted_iota(jnp.int32, (1, rows), 1)
     key_at = lax.broadcasted_iota(jnp.int32, bias_own.shape, 0)
@@ -103,8 +110,6 @@
         return slice(h * (8 // per_chunk), (h + 1) * (8 // per_chunk))
 
     def own_part(c, carry):
-        hop_one(c).wait_recv()
-        hop_two(c).start()
         for h in range(per_chunk):
             cols = head_of(c, h)
             value_t = v_in[:, cols].T
@@ -136,6 +141,7 @@
         @pl.when((t >= 1) & (t <= chunks))
         def _():
             c = t - 1
+            hop_one(c).wait_recv()
             parts = []
             for h in range(per_chunk):
                 cols = head_of(c, h)
@@ -167,7 +173,7 @@
                 )
                 final = part.T.astype(BF16)
                 for a in range(picks):
-                    out[a, :, head_of(c, h)] = final[a * BLK : (a + 1) * BLK, :]
+                    out[a * BLK : (a + 1) * BLK, head_of(c, h)] = final[a * BLK : (a + 1) * BLK, :]
 
         return carry
 
@@ -194,7 +200,7 @@
     lse_t = (chunks, 8, rows)
     return pl.pallas_call(
         functools.partial(window_kernel, chunks, per_chunk),
-        out_shape=jax.ShapeDtypeStruct((rows // BLK, BLK, cols), BF16),
+        out_shape=jax.ShapeDtypeStruct((rows, cols), BF16),
         grid=(1,),
         in_specs=[
             pl.BlockSpec(memory_space=pltpu.SMEM),
@@ -202,7 +208,7 @@
             pl.BlockSpec((tok, cols), lambda g: (0, part)),
             pl.BlockSpec((tok, cols), lambda g: (0, part)),
         ],
-        out_specs=pl.BlockSpec((rows // BLK, BLK, cols), lambda g: (0, 0, 0)),
+        out_specs=pl.BlockSpec((rows, cols), lambda g: (0, 0)),
         scratch_shapes=[
             pltpu.VMEM((chunks, rows, width), BF16),
             pltpu.VMEM((chunks, rows, width), BF16),
@@ -233,57 +239,39 @@
     )(sel, query, key, value)
 
 
-def project_kernel(index, a0, a1, b0, b1, weights, normed, projected):
-    half = a0.shape[2]
-    eps_width = 2 * half
-    pieces = []
-    for low, high in ((a0, b0), (a1, b1)):
-        x0 = low[0].astype(F32)
-        x1 = high[0].astype(F32)
-        mean = (
-            jnp.sum(x0 * x0, axis=1, keepdims=True) + jnp.sum(x1 * x1, axis=1, keepdims=True)
-        ) * (1.0 / eps_width)
-        inv = lax.rsqrt(mean + 1e-06)
-        pieces.append(((x0 * inv).astype(BF16), (x1 * inv).astype(BF16)))
-    n0 = jnp.concatenate([pieces[0][0], pieces[1][0]], axis=0)
-    n1 = jnp.concatenate([pieces[0][1], pieces[1][1]], axis=0)
-    normed[:, :half] = n0
-    normed[:, half:] = n1
-    projected[...] = (
-        jnp.dot(n0, weights[:half, :], preferred_element_type=F32)
-        + jnp.dot(n1, weights[half:, :], preferred_element_type=F32)
-    ).astype(BF16)
-
-
-def project(index, low, high, weights):
+def project_kernel(index, first, second, weights, normed, projected):
+    for at, block in enumerate((first, second)):
+        x = block[...].astype(F32)
+        mean = jnp.sum(x * x, axis=1, keepdims=True) * (1.0 / x.shape[1])
+        normed[at * BLK : (at + 1) * BLK, :] = (x * lax.rsqrt(mean + 1e-06)).astype(BF16)
+    projected[...] = jnp.dot(normed[...], weights[...], preferred_element_type=F32).astype(BF16)
+
+
+def project(index, rows, weights):
     kept = index.shape[0]
-    half = low.shape[2]
-    local = weights.shape[1]
-    block = (1, BLK, half)
+    full, local = weights.shape
     return pl.pallas_call(
         project_kernel,
         out_shape=(
-            jax.ShapeDtypeStruct((kept * BLK, 2 * half), BF16),
+            jax.ShapeDtypeStruct((kept * BLK, full), BF16),
             jax.ShapeDtypeStruct((kept * BLK, local), BF16),
         ),
         grid_spec=pltpu.PrefetchScalarGridSpec(
             num_scalar_prefetch=1,
             grid=(kept // 2,),
             in_specs=[
-                pl.BlockSpec(block, lambda g, idx: (idx[2 * g], 0, 0)),
-                pl.BlockSpec(block, lambda g, idx: (idx[2 * g + 1], 0, 0)),
-                pl.BlockSpec(block, lambda g, idx: (idx[2 * g], 0, 0)),
-                pl.BlockSpec(block, lambda g, idx: (idx[2 * g + 1], 0, 0)),
-                pl.BlockSpec((2 * half, local), lambda g, idx: (0, 0)),
+                pl.BlockSpec((BLK, full), lambda g, idx: (idx[2 * g], 0)),
+                pl.BlockSpec((BLK, full), lambda g, idx: (idx[2 * g + 1], 0)),
+                pl.BlockSpec((full, local), lambda g, idx: (0, 0)),
             ],
             out_specs=[
-                pl.BlockSpec((2 * BLK, 2 * half), lambda g, idx: (g, 0)),
+                pl.BlockSpec((2 * BLK, full), lambda g, idx: (g, 0)),
                 pl.BlockSpec((2 * BLK, local), lambda g, idx: (g, 0)),
             ],
         ),
         compiler_params=pltpu.CompilerParams(vmem_limit_bytes=VMEM_LIMIT),
         name="project",
-    )(index, low, low, high, high, weights)
+    )(index, rows, rows, weights)
 
 
 QB = 256
@@ -399,28 +387,173 @@
     )(dest, qkv, cot)
 
 
-def term_kernel(dest, d_all, weights, out):
-    value = lax.dot_general(d_all[...], weights[...], NT, preferred_element_type=F32).astype(BF16)
-    for j in range(value.shape[0] // BLK):
-        out[pl.ds(pl.multiple_of(dest[j] * BLK, BLK), BLK), :] = value[j * BLK : (j + 1) * BLK, :]
-
-
-def term(dest, d_all, weights, step=256):
-    total_rows, local = d_all.shape
+SIDE = 4
+
+
+def scatter_kernel(
+    slot_at, d_all, weights, out, terms, got1, snd2, got2, sums, last1, lasts2, last2,
+    send1, recv1, send2, recv2, send3, recv3, send4, recv4,
+):
+    shard = lax.axis_index(SEQ)
+    row, col = shard // SIDE, lax.rem(shard, SIDE)
+    wide = out.shape[1] // 2
+    part = wide // 2
+    place = ((row, col), (col, row))
+    halves = (slice(0, part), slice(part, wide))
+
+    def turn(at, by):
+        return lax.rem(at + by + SIDE, SIDE)
+
+    def slot(h, a, b):
+        return a * SIDE + b if h == 0 else b * SIDE + a
+
+    barrier = pltpu.get_barrier_semaphore()
+    for by in (1, -1):
+        for h in range(2):
+            a, b = place[h]
+            pl.semaphore_signal(
+                barrier, inc=1, device_id={SEQ: slot(h, turn(a, by), b)}, device_id_type=MESH
+            )
+
+    def group(h, a):
+        slots = [jnp.where(h == 0, a * SIDE + s, s * SIDE + a) for s in range(SIDE)]
+        rows = jnp.concatenate([d_all[slot_at[one]] for one in slots], axis=0)
+        cols = pl.ds(pl.multiple_of(h * wide, wide), wide)
+        value = lax.dot_general(rows, weights[cols, :], NT, preferred_element_type=F32).astype(BF16)
+        for s in range(SIDE):
+            terms[h, a, s] = value[s * BLK : (s + 1) * BLK, :]
+
+    def first_send(h, d, s):
+        a, b = place[h]
+        return pltpu.make_async_remote_copy(
+            src_ref=terms.at[h, turn(a, 2), s, :, halves[d]], dst_ref=got1.at[h, d, s],
+            send_sem=send1.at[h, d, s], recv_sem=recv1.at[h, d, s],
+            device_id={SEQ: slot(h, turn(a, 1 - 2 * d), b)}, device_id_type=MESH,
+        )
+
+    def second_send(h, d, s):
+        a, b = place[h]
+        return pltpu.make_async_remote_copy(
+            src_ref=snd2.at[h, d, s], dst_ref=got2.at[h, d, s],
+            send_sem=send2.at[h, d, s], recv_sem=recv2.at[h, d, s],
+            device_id={SEQ: slot(h, turn(a, 1 - 2 * d), b)}, device_id_type=MESH,
+        )
+
+    def third_send(h, d):
+        a, b = place[h]
+        return pltpu.make_async_remote_copy(
+            src_ref=sums.at[h, turn(b, 2), :, halves[d]], dst_ref=last1.at[h, d],
+            send_sem=send3.at[h, d], recv_sem=recv3.at[h, d],
+            device_id={SEQ: slot(h, a, turn(b, 1 - 2 * d))}, device_id_type=MESH,
+        )
+
+    def fourth_send(h, d):
+        a, b = place[h]
+        return pltpu.make_async_remote_copy(
+            src_ref=lasts2.at[h, d], dst_ref=last2.at[h, d],
+            send_sem=send4.at[h, d], recv_sem=recv4.at[h, d],
+            device_id={SEQ: slot(h, a, turn(b, 1 - 2 * d))}, device_id_type=MESH,
+        )
+
+    def group_far(h, carry):
+        group(h, turn(jnp.where(h == 0, row, col), 2))
+        return carry
+
+    def group_rest(g, carry):
+        h, which = lax.rem(g, 2), g // 2
+        by = jnp.where(which == 0, 1, jnp.where(which == 1, SIDE - 1, 0))
+        group(h, turn(jnp.where(h == 0, row, col), by))
+        return carry
+
+    lax.fori_loop(0, 2, group_far, 0)
+    pl.semaphore_wait(barrier, 4)
+    for k in (2, 1, 3, 0):
+        for h in range(2):
+            s = turn(place[h][1], k)
+            for d in range(2):
+                first_send(h, d, s).start()
+    lax.fori_loop(0, 6, group_rest, 0)
+    for k in (2, 1, 3, 0):
+        for h in range(2):
+            a, b = place[h]
+            s = turn(b, k)
+            for d in range(2):
+                first_send(h, d, s).wait_recv()
+                near = turn(a, 1 - 2 * d)
+                other = halves[1 - d]
+                snd2[h, d, s, :, other] = terms[h, near, s, :, other]
+                snd2[h, d, s, :, halves[d]] = (
+                    terms[h, near, s, :, halves[d]].astype(F32) + got1[h, d, s].astype(F32)
+                ).astype(BF16)
+                second_send(h, d, s).start()
+    for k in (2, 1, 3, 0):
+        for h in range(2):
+            a, b = place[h]
+            s = turn(b, k)
+            for d in range(2):
+                second_send(h, d, s).wait_recv()
+            total = (
+                terms[h, a, s].astype(F32) + got2[h, 0, s].astype(F32) + got2[h, 1, s].astype(F32)
+            )
+            if k != 0:
+                sums[h, s] = total.astype(BF16)
+            if k == 2:
+                for d in range(2):
+                    third_send(h, d).start()
+            elif k != 0:
+                d = 0 if k == 1 else 1
+                third_send(h, d).wait_recv()
+                other = halves[1 - d]
+                lasts2[h, d, :, other] = sums[h, s, :, other]
+                lasts2[h, d, :, halves[d]] = (total[:, halves[d]] + last1[h, d].astype(F32)).astype(BF16)
+                fourth_send(h, d).start()
+            else:
+                for d in range(2):
+                    fourth_send(h, d).wait_recv()
+                out[:, h * wide : (h + 1) * wide] = (
+                    total + last2[h, 0].astype(F32) + last2[h, 1].astype(F32)
+                ).astype(BF16)
+    for h in range(2):
+        for d in range(2):
+            for s in range(SIDE):
+                first_send(h, d, s).wait_send()
+                second_send(h, d, s).wait_send()
+            third_send(h, d).wait_send()
+            fourth_send(h, d).wait_send()
+
+
+def scatter_terms(slot_at, d_all, weights, ident):
+    blocks, _, local = d_all.shape
     full = weights.shape[0]
+    wide = full // 2
+    part = wide // 2
+    vmem = pl.BlockSpec(memory_space=pltpu.VMEM)
+    four = pltpu.SemaphoreType.DMA((2, 2, SIDE))
+    two = pltpu.SemaphoreType.DMA((2, 2))
     return pl.pallas_call(
-        term_kernel,
-        out_shape=jax.ShapeDtypeStruct((total_rows, full), BF16),
-        grid=(full // step,),
-        in_specs=[
-            pl.BlockSpec(memory_space=pltpu.SMEM),
-            pl.BlockSpec((total_rows, local), lambda g: (0, 0)),
-            pl.BlockSpec((step, local), lambda g: (g, 0)),
+        scatter_kernel,
+        out_shape=jax.ShapeDtypeStruct((BLK, full), BF16),
+        in_specs=[pl.BlockSpec(memory_space=pltpu.SMEM), vmem, vmem],
+        out_specs=vmem,
+        scratch_shapes=[
+            pltpu.VMEM((2, SIDE, SIDE, BLK, wide), BF16),
+            pltpu.VMEM((2, 2, SIDE, BLK, part), BF16),
+            pltpu.VMEM((2, 2, SIDE, BLK, wide), BF16),
+            pltpu.VMEM((2, 2, SIDE, BLK, wide), BF16),
+            pltpu.VMEM((2, SIDE, BLK, wide), BF16),
+            pltpu.VMEM((2, 2, BLK, part), BF16),
+            pltpu.VMEM((2, 2, BLK, wide), BF16),
+            pltpu.VMEM((2, 2, BLK, wide), BF16),
+            four, four, four, four, two, two, two, two,
         ],
-        out_specs=pl.BlockSpec((total_rows, step), lambda g: (0, g)),
-        compiler_params=pltpu.CompilerParams(vmem_limit_bytes=VMEM_LIMIT),
-        name="term",
-    )(dest, d_all, weights)
+        compiler_params=pltpu.CompilerParams(
+            collective_id=ident, has_side_effects=True, vmem_limit_bytes=VMEM_LIMIT
+        ),
+        cost_estimate=pl.CostEstimate(
+            flops=2 * blocks * BLK * local * full, bytes_accessed=100 * 1024 * 1024, transcendentals=0
+        ),
+        name="scatter_terms",
+    )(slot_at, d_all, weights)
 
 
 def weight_grad_kernel(d_t, normed, out):
@@ -446,38 +579,34 @@
     )(d_t, normed)
 
 
-def assemble_kernel(table, low, high, rest, out):
+def assemble_kernel(table, head, rest, out):
     first = table[3 * pl.program_id(0)] == 1
 
     @pl.when(first)
     def _():
-        half = low.shape[2]
-        out[:, :half] = low[0]
-        out[:, half:] = high[0]
+        out[...] = head[...]
 
     @pl.when(jnp.logical_not(first))
     def _():
-        out[...] = rest[0]
-
-
-def assemble(table, low, high, rest):
-    blocks = 2 * low.shape[0]
-    half = low.shape[2]
+        out[...] = rest[...]
+
+
+def assemble(table, head, rest):
+    rows, full = head.shape
     return pl.pallas_call(
         assemble_kernel,
-        out_shape=jax.ShapeDtypeStruct((blocks * BLK, 2 * half), BF16),
+        out_shape=jax.ShapeDtypeStruct((2 * rows, full), BF16),
         grid_spec=pltpu.PrefetchScalarGridSpec(
             num_scalar_prefetch=1,
-            grid=(blocks,),
+            grid=(2 * rows // BLK,),
             in_specs=[
-                pl.BlockSpec((1, BLK, half), lambda g, t: (t[3 * g + 1], 0, 0)),
-                pl.BlockSpec((1, BLK, half), lambda g, t: (t[3 * g + 1], 0, 0)),
-                pl.BlockSpec((1, BLK, 2 * half), lambda g, t: (t[3 * g + 2], 0, 0)),
+                pl.BlockSpec((BLK, full), lambda g, t: (t[3 * g + 1], 0)),
+                pl.BlockSpec((BLK, full), lambda g, t: (t[3 * g + 2], 0)),
             ],
-            out_specs=pl.BlockSpec((BLK, 2 * half), lambda g, t: (g, 0)),
+            out_specs=pl.BlockSpec((BLK, full), lambda g, t: (g, 0)),
         ),
         name="assemble",
-    )(table, low, high, rest)
+    )(table, head, rest)
 
 
 def shards(query_input, key_input, value_input, keep_blocks, dest_slots, proj_weights, cotangent):
@@ -516,20 +645,24 @@
     packed = (keep_shard * half_blocks + before).astype(jnp.int32)
     weights = jnp.concatenate([proj_weights[0], proj_weights[1], proj_weights[2]], axis=1)
 
-    low = window(sel_first, query, key, value, 0, 2, 2, 0)
-    low_all = lax.all_gather(low, SEQ, axis=0, tiled=True)
-    high = window(sel_first, query, key, value, 1, 2, 2, 1)
-    high_all = lax.all_gather(high, SEQ, axis=0, tiled=True)
-
-    normed, qkv = project(packed, low_all, high_all, weights)
+    slot_at = jnp.sum(
+        jnp.where(dest[None, :] == jnp.arange(dest.shape[0])[:, None], jnp.arange(dest.shape[0])[None, :], 0),
+        axis=1,
+    ).astype(jnp.int32)
+
+    first = window(sel_first, query, key, value, 0, 1, 2, 0)
+    gathered = lax.all_gather(first, SEQ, axis=0, tiled=True)
+    sel_late, _ = lax.optimization_barrier((sel_rest, first))
+    rest = window(sel_late, query, key, value, 0, 1, 2, 1)
+    window_out = assemble(table, first, rest)
+
+    packed_late, _ = lax.optimization_barrier((packed, rest))
+    normed, qkv = project(packed_late, gathered, weights)
     causal_out, d_all, d_all_t = causal(dest, qkv, cotangent[0])
-    terms = term(dest, d_all, weights)
-    row_grad = lax.psum_scatter(terms, SEQ, scatter_dimension=0, tiled=True)
-    grads = weight_grad(d_all_t, normed)
-    grads = lax.psum(grads, "dp").astype(F32)
-    sel_late, terms = lax.optimization_barrier((sel_rest, d_all))
-    rest = window(sel_late, query, key, value, 0, 1, 2, 2)
-    window_out = assemble(table, low, high, rest)
+    local_grads = weight_grad(d_all_t, normed)
+    grads = lax.psum(local_grads, "dp").astype(F32)
+    slot_late, _ = lax.optimization_barrier((slot_at, local_grads))
+    row_grad = scatter_terms(slot_late, d_all.reshape(dest.shape[0], BLK, -1), weights, 2)
     return (window_out[None], causal_out[None], grads, row_grad[None])
 
 

time: 440 us -> 378 us (0.86)
  waiting for transfers between devices: 128 us -> 53.9 us
  Pallas kernels: 289 us -> 299 us
    all_gather x2 -> x1, waiting for transfers between devices: 90.9 us -> 48.4 us  [shards(): gathered = lax.all_gather(first, SEQ, axis=0, tiled=True)]
    pallas_call x2, Pallas kernels: 14.7 us -> 55.6 us  [the longest x1 50.8 us: scatter_terms(): pl.pallas_call(scatter_kernel, out_shape=jax.ShapeDtypeStruct((BLK, full)...]
    reduce_scatter x1 -> x0, waiting for transfers between devices: 36.6 us -> none  [shards(): row_grad = lax.psum_scatter(terms, SEQ, scatter_dimension=0, tiled=True)]
    pallas_call x3 -> x2, Pallas kernels: 228 us -> 197 us  [window(): pl.pallas_call(functools.partial(window_kernel, chunks, per_chunk), out_s...]
    psum x1, waiting for transfers between devices: 0.01 us -> 5.42 us  [shards(): grads = lax.psum(local_grads, 'dp').astype(F32)]
  transfers between devices with their start and end apart: 4 -> 2, of which waited for: 3 -> 2; matrix products, arithmetic and copies ran while one was open for 2% -> 1% of each run, Pallas kernels for 42% -> 45%
where the time goes in v2:
time: 378 us
  Pallas kernels  299 us (79%)
  waiting for transfers between devices  53.9 us (14%)
  between operations  14.1 us (4%)
  other arithmetic  6.97 us (2%)
    pallas_call x2, Pallas kernels, window(): pl.pallas_call(functools.partial(window_kernel, chunks, per_chunk), out_s...  197 us
    pallas_call x1, Pallas kernels, scatter_terms(): pl.pallas_call(scatter_kernel, out_shape=jax.ShapeDtypeStruct((BLK, full)...  50.8 us
    all_gather x1, waiting for transfers between devices, shards(): gathered = lax.all_gather(first, SEQ, axis=0, tiled=True)  48.4 us
    pallas_call x1, Pallas kernels, causal(): pl.pallas_call(causal_kernel, out_shape=(jax.ShapeDtypeStruct((total_rows...  24.7 us
    pallas_call x1, Pallas kernels, project(): pl.pallas_call(project_kernel, out_shape=(jax.ShapeDtypeStruct((kept * BL...  12 us
    pallas_call x1, Pallas kernels, weight_grad(): pl.pallas_call(weight_grad_kernel, out_shape=jax.ShapeDtypeStruct((3, ful...  9.83 us
  transfers between devices with their start and end apart: 2, of which 2 were waited for; matrix products, arithmetic and copies ran while one was open for 1% of the time, Pallas kernels for 45%

profile of v2, /device:TPU:0, one launch (start us, length us, event | category | flops | bytes accessed | tf_op | source)
XLA Modules:
  0.0 377.6 jit_solution(11105821537422791518)
XLA Ops:
  7.2 0.0 all-gather.2.cloned.1.call-start
  7.2 0.9 compare_reduce_fusion
  8.2 0.1 pad_add_fusion.1
  8.2 0.1 constant_dynamic-slice_fusion
  8.3 0.1 copy.20
  8.4 0.6 reshape.173.sel
  9.0 83.5 %window_0.1.head = bf16[256,2048]{1,0:T(8,128)(2,1)} custom-call(s32[6]{0:T(128)} %reshape.173.sel, bf16[4,128,2048]{2,1,0:T(8,128)(2,1)} %bitcast.40, bf16[512,2048]{1,0:T(8,128)(2,1)} %bitcast.42, bf16[512,2048]{1,0:T(8,128)(2,1)} %bitcast.44), custom_call_target="tpu_custom_call" | custom-call | flops 3221225472 | bytes 16777216 | tf_op jit(solution)/shard_map/window_0/pallas_call | solution.py:201
  92.5 0.0 all-gather.2.cloned.1.call-update
  92.5 0.2 all-reduce.2.cloned.1.call-start
  92.8 0.2 dynamic-slice_reduce_fusion
  92.9 0.1 copy.21
  93.0 0.6 reshape.175.sel
  93.7 0.2 convert_reduce_fusion
  93.8 0.5 multiply_add_fusion.1.index
  94.4 113.4 %window_1.1.rest = bf16[256,2048]{1,0:T(8,128)(2,1)} custom-call(s32[6]{0:T(128)} %reshape.175.sel, bf16[4,128,2048]{2,1,0:T(8,128)(2,1)} %bitcast.41, bf16[512,2048]{1,0:T(8,128)(2,1)} %bitcast.43, bf16[512,2048]{1,0:T(8,128)(2,1)} %bitcast.45), custom_call_target="tpu_custom_call" | custom-call | flops 3221225472 | bytes 16777216 | tf_op jit(solution)/shard_map/window_1/pallas_call | solution.py:201
  207.8 0.0 copy-done.3
  207.8 0.6 select_reduce_fusion.slot_at
  208.4 0.0 copy-done
  208.4 0.1 slice_bitcast_fusion.2
  208.5 1.3 pad_maximum_fusion.weights
  209.9 48.4 %all-gather.2.cloned.1.call-done.first.second = bf16[4096,2048]{1,0:T(8,128)(2,1)} async-done(((bf16[256,2048]{1,0:T(8,128)(2,1)}), bf16[4096,2048]{1,0:T(8,128)(2,1)}) %all-gather.2.cloned.1.call-update) | async-done | bytes 16777232 | tf_op jit(solution)/shard_map/all_gather | solution.py:654
  258.3 12.0 %project.1 = (bf16[2048,2048]{1,0:T(8,128)(2,1)}, bf16[2048,384]{1,0:T(8,128)(2,1)}) custom-call(s32[16]{0:T(128)} %multiply_add_fusion.1.index, bf16[4096,2048]{1,0:T(8,128)(2,1)} %all-gather.2.cloned.1.call-done.first.second, bf16[4096,2048]{1,0:T(8,128)(2,1)} %all-gather.2.cloned.1.call-done.first.second, bf16[2048,384]{1,0:T(8,128)(2,1)} %pad_maximum_fusion.weights), custom_call_target="tpu_custom_call" | custom-call | tf_op jit(solution)/shard_map/project/pallas_call | solution.py:253
  270.4 24.7 %causal.1 = (bf16[2048,128]{1,0:T(8,128)(2,1)}, bf16[2048,384]{1,0:T(8,128)(2,1)}, bf16[384,2048]{1,0:T(8,128)(2,1)}) custom-call(s32[16]{0:T(128)} %bitcast.38, bf16[2048,384]{1,0:T(8,128)(2,1)} %get-tuple-element.14.qkv, bf16[2048,128]{1,0:T(8,128)(2,1)} %bitcast.33), custom_call_target="tpu_custom_call" | custom-call | tf_op jit(solution)/shard_map/causal/pallas_call | solution.py:366
  295.0 9.8 %weight_grad.1 = bf16[3,2048,128]{2,1,0:T(8,128)(2,1)} custom-call(bf16[384,2048]{1,0:T(8,128)(2,1)} %get-tuple-element.16.d_t, bf16[2048,2048]{1,0:T(8,128)(2,1)} %get-tuple-element.17.normed), custom_call_target="tpu_custom_call" | custom-call | tf_op jit(solution)/shard_map/weight_grad/pallas_call | solution.py:568
  304.9 0.0 all-reduce.2.cloned.1.call-update
  304.9 0.1 copy.19
  305.0 0.6 reshape.172.table
  305.6 4.8 %assemble.1 = bf16[512,2048]{1,0:T(8,128)(2,1)} custom-call(s32[12]{0:T(128)} %reshape.172.table, bf16[256,2048]{1,0:T(8,128)(2,1)} %window_0.1.head, bf16[256,2048]{1,0:T(8,128)(2,1)} %window_1.1.rest), custom_call_target="tpu_custom_call" | custom-call | tf_op jit(solution)/shard_map/assemble/pallas_call | solution.py:596
  310.4 50.8 %scatter_terms.1 = bf16[128,2048]{1,0:T(8,128)(2,1)} custom-call(s32[16]{0:T(128)} %select_reduce_fusion.slot_at, bf16[16,128,384]{2,1,0:T(8,128)(2,1)} %bitcast.46, bf16[2048,384]{1,0:T(8,128)(2,1)} %pad_maximum_fusion.weights), custom_call_target="tpu_custom_call" | custom-call | flops 3221225472 | bytes 104857600 | tf_op jit(solution)/shard_map/scatter_terms/pallas_call | solution.py:533
  361.2 5.4 %all-reduce.2.cloned.1.call-done = bf16[3,2048,128]{2,1,0:T(8,128)(2,1)} async-done(((bf16[3,2048,128]{2,1,0:T(8,128)(2,1)}), bf16[3,2048,128]{2,1,0:T(8,128)(2,1)}) %all-reduce.2.cloned.1.call-update) | async-done | bytes 1572880 | tf_op jit(solution)/shard_map/psum | solution.py:663
  366.7 3.3 convert_element_type.26
  369.9 0.8 copy.24
  (16 shorter events, 0.1 us)
Async XLA Ops:
  7.2 251.2 %all-gather.2.cloned.1.call-start = ((), (), s32[]{:S(2)}) async-start(), calls=%async_computation | async-start | bytes 17825792 | tf_op jit(solution)/shard_map/all_gather | solution.py:654
  9.0 84.6 %copy-start.2 = (s32[1,16]{1,0:T(1,128)S(1)}, s32[1,16]{1,0:T(1,128)}, u32[]{:S(2)}) copy-start(s32[1,16]{1,0:T(1,128)} %param.10) | copy-start | bytes 196
  92.5 274.1 %all-reduce.2.cloned.1.call-start = ((), (), s32[]{:S(2)}) async-start(), calls=%async_computation.1 | async-start | bytes 3145728 | tf_op jit(solution)/shard_map/psum | solution.py:663
  94.4 113.5 %copy-start.3 = (s32[1,16]{1,0:T(1,128)S(1)}, s32[1,16]{1,0:T(1,128)}, u32[]{:S(2)}) copy-start(s32[1,16]{1,0:T(1,128)} %param.11) | copy-start | bytes 196
  94.4 114.1 %copy-start = (bf16[3,2048,128]{2,1,0:T(8,128)(2,1)S(1)}, bf16[3,2048,128]{2,1,0:T(8,128)(2,1)}, u32[]{:S(2)}) copy-start(bf16[3,2048,128]{2,1,0:T(8,128)(2,1)} %param.12) | copy-start | bytes 4718596
  361.2 8.7 %copy-start.1 = (bf16[128,2048]{1,0:T(8,128)(2,1)S(1)}, bf16[128,2048]{1,0:T(8,128)(2,1)}, u32[]{:S(2)}) copy-start(bf16[128,2048]{1,0:T(8,128)(2,1)} %scatter_terms.1) | copy-start | bytes 1572868
Sparse Core Ops, SparseCore 0:
  92.6 165.6 all-gather.1
  305.0 61.5 all-reduce.1

commit v3 on v2

--- a/solution.py
+++ b/solution.py
@@ -40,202 +40,217 @@
     return out_a * (weight_a / total) + out_b * (weight_b / total), top + jnp.log2(total)
 
 
-def window_kernel(
-    chunks, per_chunk, sel, q_in, k_in, v_in, out,
-    q_own, q_one, q_two, v_t, o_own, l_own, o_snd2, l_snd2, o_got2, l_got2, o_snd1, l_snd1, o_got1, l_got1,
-    bias_own, bias_two, send_sem, recv_sem,
-):
-    shard = lax.axis_index(SEQ)
-    count = lax.axis_size(SEQ)
-    right = lax.rem(shard + 1, count)
-    left = lax.rem(shard + count - 1, count)
-    right_two = lax.rem(shard + 2, count)
-    left_two = lax.rem(shard + count - 2, count)
-    width = per_chunk * HEAD
-    rows = q_own.shape[1]
-    picks = rows // BLK
-
-    def copy(which, c, src, dst, target):
+class Flow:
+    def __init__(self, sel, q_in, k_in, v_in, out, scratch):
+        (
+            self.q_own, self.q_one, self.q_two, self.v_t, self.o_own, self.l_own, self.o_snd2, self.l_snd2,
+            self.o_got2, self.l_got2, self.o_snd1, self.l_snd1, self.o_got1, self.l_got1,
+            self.bias_own, self.bias_two, self.send_sem, self.recv_sem,
+        ) = scratch
+        self.sel, self.q_in, self.k_in, self.v_in, self.out = sel, q_in, k_in, v_in, out
+        self.chunks, self.rows, self.width = self.q_own.shape
+        self.per_chunk = self.width // HEAD
+        self.lse_step = 8 // self.per_chunk
+        self.shard = lax.axis_index(SEQ)
+        count = lax.axis_size(SEQ)
+        self.right = lax.rem(self.shard + 1, count)
+        self.left = lax.rem(self.shard + count - 1, count)
+
+    def copy(self, which, c, src, dst, target):
         return pltpu.make_async_remote_copy(
             src_ref=src.at[c], dst_ref=dst.at[c],
-            send_sem=send_sem.at[which, c], recv_sem=recv_sem.at[which, c],
+            send_sem=self.send_sem.at[which, c], recv_sem=self.recv_sem.at[which, c],
             device_id={SEQ: target}, device_id_type=MESH,
         )
 
-    def hop_one(c):
-        return copy(0, c, q_own, q_one, left)
-
-    def hop_two(c):
-        return copy(1, c, q_own, q_two, left_two)
-
-    def back_two(c):
-        return (copy(2, c, o_snd2, o_got2, right), copy(3, c, l_snd2, l_got2, right))
-
-    def back_one(c):
-        return (copy(4, c, o_snd1, o_got1, right), copy(5, c, l_snd1, l_got1, right))
-
-    barrier = pltpu.get_barrier_semaphore()
-    for neighbour in (left, right, left_two, right_two):
-        pl.semaphore_signal(barrier, inc=1, device_id={SEQ: neighbour}, device_id_type=MESH)
-
-    for a in range(picks):
-        block = q_in[sel[a]]
-        for c in range(chunks):
-            q_own[c, a * BLK : (a + 1) * BLK, :] = block[:, c * width : (c + 1) * width]
-    pl.semaphore_wait(barrier, 4)
-
-    def send(c, carry):
-        hop_two(c).start()
-        hop_one(c).start()
+    def hop_one(self, c):
+        return self.copy(0, c, self.q_own, self.q_one, self.left)
+
+    def hop_two(self, c):
+        return self.copy(1, c, self.q_one, self.q_two, self.left)
+
+    def back_two(self, c):
+        return (
+            self.copy(2, c, self.o_snd2, self.o_got2, self.right),
+            self.copy(3, c, self.l_snd2, self.l_got2, self.right),
+        )
+
+    def back_one(self, c):
+        return (
+            self.copy(4, c, self.o_snd1, self.o_got1, self.right),
+            self.copy(5, c, self.l_snd1, self.l_got1, self.right),
+        )
+
+    def begin(self, ahead):
+        barrier = pltpu.get_barrier_semaphore()
+        for neighbour in (self.left, self.right):
+            pl.semaphore_signal(barrier, inc=1, device_id={SEQ: neighbour}, device_id_type=MESH)
+        picks = self.rows // BLK
+        for a in range(picks):
+            block = self.q_in[self.sel[a]]
+            for c in range(self.chunks):
+                self.q_own[c, a * BLK : (a + 1) * BLK, :] = block[:, c * self.width : (c + 1) * self.width]
+        pl.semaphore_wait(barrier, 2)
+        for c in range(ahead):
+            self.hop_one(c).start()
+        self.ahead = ahead
+        lane = lax.broadcasted_iota(jnp.int32, (1, self.rows), 1)
+        key_at = lax.broadcasted_iota(jnp.int32, self.bias_own.shape, 0)
+        for base, ref in ((0, self.bias_own), (2 * picks, self.bias_two)):
+            place = lane
+            for a in range(picks):
+                place = jnp.where(lane // BLK == a, (lane - a * BLK) + self.sel[base + a] * BLK, place)
+            seen = (key_at <= place) if base == 0 else (key_at > place)
+            ref[...] = jnp.where(seen, 0.0, LOW)
+
+    def cols(self, c, h):
+        return pl.ds(pl.multiple_of(c * self.width + h * HEAD, HEAD), HEAD)
+
+    def lse_at(self, h):
+        return slice(h * self.lse_step, (h + 1) * self.lse_step)
+
+    def spread(self, row):
+        return jnp.broadcast_to(row, (self.lse_step, self.rows))
+
+    def head(self, h):
+        return slice(h * HEAD, (h + 1) * HEAD)
+
+    def pump(self, c):
+        self.hop_one(c).wait_recv()
+        self.hop_two(c).start()
+
+        @pl.when(c + self.ahead < self.chunks)
+        def _():
+            self.hop_one(c + self.ahead).start()
+
+    def own(self, c):
+        for h in range(self.per_chunk):
+            cols = self.cols(c, h)
+            value_t = self.v_in[:, cols].T
+            self.v_t[cols, :] = value_t
+            part, lse = window_part(
+                self.q_own[c, :, self.head(h)], self.k_in[:, cols], value_t, self.bias_own[...]
+            )
+            self.o_own[c, self.head(h), :] = part
+            self.l_own[c, self.lse_at(h), :] = self.spread(lse)
+
+    def two(self, c):
+        self.hop_two(c).wait_recv()
+        for h in range(self.per_chunk):
+            cols = self.cols(c, h)
+            part, lse = window_part(
+                self.q_two[c, :, self.head(h)], self.k_in[:, cols], self.v_t[cols, :], self.bias_two[...]
+            )
+            self.o_snd2[c, self.head(h), :] = part.astype(BF16)
+            self.l_snd2[c, self.lse_at(h), :] = self.spread(lse)
+        for each in self.back_two(c):
+            each.start()
+
+    def incoming(self, got, h, c):
+        first = h * self.lse_step
+        return jnp.where(self.shard == 0, LOW, got[c, first : first + 1, :])
+
+    def one(self, c):
+        parts = []
+        for h in range(self.per_chunk):
+            cols = self.cols(c, h)
+            parts.append(
+                window_part(self.q_one[c, :, self.head(h)], self.k_in[:, cols], self.v_t[cols, :], None)
+            )
+        for each in self.back_two(c):
+            each.wait_recv()
+        for h in range(self.per_chunk):
+            part, lse = merged(
+                *parts[h], self.o_got2[c, self.head(h), :].astype(F32), self.incoming(self.l_got2, h, c)
+            )
+            self.o_snd1[c, self.head(h), :] = part.astype(BF16)
+            self.l_snd1[c, self.lse_at(h), :] = self.spread(lse)
+        for each in self.back_one(c):
+            each.start()
+
+    def final(self, c):
+        for each in self.back_one(c):
+            each.wait_recv()
+        for h in range(self.per_chunk):
+            first = h * self.lse_step
+            part, _ = merged(
+                self.o_own[c, self.head(h), :], self.l_own[c, first : first + 1, :],
+                self.o_got1[c, self.head(h), :].astype(F32), self.incoming(self.l_got1, h, c),
+            )
+            self.out[:, self.cols(c, h)] = part.T.astype(BF16)
+
+    def step(self, t):
+        @pl.when(t < self.chunks)
+        def _():
+            self.pump(t)
+            self.own(t)
+
+        @pl.when((t >= 1) & (t <= self.chunks))
+        def _():
+            self.two(t - 1)
+
+        @pl.when((t >= 2) & (t <= self.chunks + 1))
+        def _():
+            self.one(t - 2)
+
+        @pl.when(t >= 3)
+        def _():
+            self.final(t - 3)
+
+    def drain(self):
+        def body(c, carry):
+            self.hop_one(c).wait_send()
+            self.hop_two(c).wait_send()
+            for each in self.back_two(c) + self.back_one(c):
+                each.wait_send()
+            return carry
+
+        lax.fori_loop(0, self.chunks, body, 0)
+
+    @staticmethod
+    def scratch(rows, tok, full, per_chunk):
+        width = per_chunk * HEAD
+        chunks = full // width
+        queries = pltpu.VMEM((chunks, rows, width), BF16)
+        outs = pltpu.VMEM((chunks, width, rows), BF16)
+        lses = pltpu.VMEM((chunks, 8, rows), F32)
+        return [
+            queries, queries, queries, pltpu.VMEM((full, tok), BF16), pltpu.VMEM((chunks, width, rows), F32), lses,
+            outs, lses, outs, lses, outs, lses, outs, lses,
+            pltpu.VMEM((tok, rows), F32), pltpu.VMEM((tok, rows), F32),
+            pltpu.SemaphoreType.DMA((6, chunks)), pltpu.SemaphoreType.DMA((6, chunks)),
+        ]
+
+
+def window_kernel(sel, q_in, k_in, v_in, out, *scratch):
+    flow = Flow(sel, q_in, k_in, v_in, out, scratch)
+    flow.begin(2)
+
+    def step(t, carry):
+        flow.step(t)
         return carry
 
-    lax.fori_loop(0, chunks, send, 0)
-
-    lane = lax.broadcasted_iota(jnp.int32, (1, rows), 1)
-    key_at = lax.broadcasted_iota(jnp.int32, bias_own.shape, 0)
-    for base, ref in ((0, bias_own), (2 * picks, bias_two)):
-        place = lane
-        for a in range(picks):
-            place = jnp.where(lane // BLK == a, (lane - a * BLK) + sel[base + a] * BLK, place)
-        seen = (key_at <= place) if base == 0 else (key_at > place)
-        ref[...] = jnp.where(seen, 0.0, LOW)
-
-    def head_of(c, h):
-        return pl.ds(pl.multiple_of(c * width + h * HEAD, HEAD), HEAD)
-
-    def spread(row):
-        return jnp.broadcast_to(row, (8 // per_chunk, rows))
-
-    def lse_rows(h):
-        return slice(h * (8 // per_chunk), (h + 1) * (8 // per_chunk))
-
-    def own_part(c, carry):
-        for h in range(per_chunk):
-            cols = head_of(c, h)
-            value_t = v_in[:, cols].T
-            v_t[cols, :] = value_t
-            part, lse = window_part(
-                q_own[c, :, h * HEAD : (h + 1) * HEAD], k_in[:, cols], value_t, bias_own[...]
-            )
-            o_own[c, h * HEAD : (h + 1) * HEAD, :] = part
-            l_own[c, lse_rows(h), :] = spread(lse)
-        return carry
-
-    lax.fori_loop(0, chunks, own_part, 0)
-
-    def step(t, carry):
-        @pl.when(t < chunks)
-        def _():
-            c = t
-            hop_two(c).wait_recv()
-            for h in range(per_chunk):
-                cols = head_of(c, h)
-                part, lse = window_part(
-                    q_two[c, :, h * HEAD : (h + 1) * HEAD], k_in[:, cols], v_t[cols, :], bias_two[...]
-                )
-                o_snd2[c, h * HEAD : (h + 1) * HEAD, :] = part.astype(BF16)
-                l_snd2[c, lse_rows(h), :] = spread(lse)
-            for one in back_two(c):
-                one.start()
-
-        @pl.when((t >= 1) & (t <= chunks))
-        def _():
-            c = t - 1
-            hop_one(c).wait_recv()
-            parts = []
-            for h in range(per_chunk):
-                cols = head_of(c, h)
-                parts.append(
-                    window_part(q_one[c, :, h * HEAD : (h + 1) * HEAD], k_in[:, cols], v_t[cols, :], None)
-                )
-            for one in back_two(c):
-                one.wait_recv()
-            for h in range(per_chunk):
-                part, lse = parts[h]
-                lse_in = jnp.where(shard == 0, LOW, l_got2[c, h * (8 // per_chunk) : h * (8 // per_chunk) + 1, :])
-                part, lse = merged(part, lse, o_got2[c, h * HEAD : (h + 1) * HEAD, :].astype(F32), lse_in)
-                o_snd1[c, h * HEAD : (h + 1) * HEAD, :] = part.astype(BF16)
-                l_snd1[c, lse_rows(h), :] = spread(lse)
-            for one in back_one(c):
-                one.start()
-
-        @pl.when(t >= 2)
-        def _():
-            c = t - 2
-            for one in back_one(c):
-                one.wait_recv()
-            for h in range(per_chunk):
-                first = h * (8 // per_chunk)
-                lse_in = jnp.where(shard == 0, LOW, l_got1[c, first : first + 1, :])
-                part, lse = merged(
-                    o_own[c, h * HEAD : (h + 1) * HEAD, :], l_own[c, first : first + 1, :],
-                    o_got1[c, h * HEAD : (h + 1) * HEAD, :].astype(F32), lse_in,
-                )
-                final = part.T.astype(BF16)
-                for a in range(picks):
-                    out[a * BLK : (a + 1) * BLK, head_of(c, h)] = final[a * BLK : (a + 1) * BLK, :]
-
-        return carry
-
-    lax.fori_loop(0, chunks + 2, step, 0)
-
-    def drain(c, carry):
-        hop_one(c).wait_send()
-        hop_two(c).wait_send()
-        for one in back_two(c) + back_one(c):
-            one.wait_send()
-        return carry
-
-    lax.fori_loop(0, chunks, drain, 0)
-
-
-def window(sel, query, key, value, part, parts, per_chunk, ident):
-    blocks, _, full = query.shape
-    tok = key.shape[0]
-    cols = full // parts
-    chunks = cols // HEAD // per_chunk
-    width = per_chunk * HEAD
+    lax.fori_loop(0, flow.chunks + 3, step, 0)
+    flow.drain()
+
+
+def window(sel, query, key, value, per_chunk, ident):
+    tok, full = key.shape
     rows = sel.shape[0] // 3 * BLK
-    out_t = (chunks, width, rows)
-    lse_t = (chunks, 8, rows)
+    vmem = pl.BlockSpec(memory_space=pltpu.VMEM)
     return pl.pallas_call(
-        functools.partial(window_kernel, chunks, per_chunk),
-        out_shape=jax.ShapeDtypeStruct((rows, cols), BF16),
-        grid=(1,),
-        in_specs=[
-            pl.BlockSpec(memory_space=pltpu.SMEM),
-            pl.BlockSpec((blocks, BLK, cols), lambda g: (0, 0, part)),
-            pl.BlockSpec((tok, cols), lambda g: (0, part)),
-            pl.BlockSpec((tok, cols), lambda g: (0, part)),
-        ],
-        out_specs=pl.BlockSpec((rows, cols), lambda g: (0, 0)),
-        scratch_shapes=[
-            pltpu.VMEM((chunks, rows, width), BF16),
-            pltpu.VMEM((chunks, rows, width), BF16),
-            pltpu.VMEM((chunks, rows, width), BF16),
-            pltpu.VMEM((cols, tok), BF16),
-            pltpu.VMEM(out_t, F32),
-            pltpu.VMEM(lse_t, F32),
-            pltpu.VMEM(out_t, BF16),
-            pltpu.VMEM(lse_t, F32),
-            pltpu.VMEM(out_t, BF16),
-            pltpu.VMEM(lse_t, F32),
-            pltpu.VMEM(out_t, BF16),
-            pltpu.VMEM(lse_t, F32),
-            pltpu.VMEM(out_t, BF16),
-            pltpu.VMEM(lse_t, F32),
-            pltpu.VMEM((tok, rows), F32),
-            pltpu.VMEM((tok, rows), F32),
-            pltpu.SemaphoreType.DMA((6, chunks)),
-            pltpu.SemaphoreType.DMA((6, chunks)),
-        ],
+        window_kernel,
+        out_shape=jax.ShapeDtypeStruct((rows, full), BF16),
+        in_specs=[pl.BlockSpec(memory_space=pltpu.SMEM), vmem, vmem, vmem],
+        out_specs=vmem,
+        scratch_shapes=Flow.scratch(rows, tok, full, per_chunk),
         compiler_params=pltpu.CompilerParams(
             collective_id=ident, has_side_effects=True, vmem_limit_bytes=VMEM_LIMIT
         ),
         cost_estimate=pl.CostEstimate(
-            flops=12 * rows * tok * cols, bytes_accessed=16 * 1024 * 1024 * cols // full, transcendentals=0
-        ),
-        name=f"window_{ident}",
+            flops=12 * rows * tok * full, bytes_accessed=16 * 1024 * 1024, transcendentals=0
+        ),
+        name="window",
     )(sel, query, key, value)
 
 
@@ -278,11 +293,20 @@
 KB = 512
 
 
-def causal_kernel(dest, qkv, cot, out, d_all, d_all_t, v_t, k_t, do_own, do_t, p_buf, dk_acc, dv_acc, dq_t):
+def causal_kernel(
+    dest, sel, qkv, cot, normed, q_in, k_in, v_in, out, d_all, grads, rest,
+    rows_in, rows_sem, d_all_t, v_t, k_t, do_own, do_t, p_buf, dk_acc, dv_acc, dq_t, *scratch,
+):
     kept = dest.shape[0]
     total_rows = qkv.shape[0]
+    blocks = total_rows // QB
+    rows_copy = pltpu.make_async_copy(normed, rows_in, rows_sem)
+    rows_copy.start()
+    flow = Flow(sel, q_in, k_in, v_in, rest, scratch)
+    flow.begin(2)
+
     for j in range(kept):
-        do_own[j * BLK : (j + 1) * BLK, :] = cot[pl.ds(pl.multiple_of(dest[j] * BLK, BLK), BLK), :]
+        do_own[j * BLK : (j + 1) * BLK, :] = cot[dest[j]]
 
     def prepare(c, carry):
         at = pl.ds(pl.multiple_of(c * QB, QB), QB)
@@ -291,15 +315,13 @@
         do_t[:, at] = do_own[at, :].T
         return carry
 
-    lax.fori_loop(0, total_rows // QB, prepare, 0)
+    lax.fori_loop(0, blocks, prepare, 0)
     dk_acc[...] = jnp.zeros_like(dk_acc)
     dv_acc[...] = jnp.zeros_like(dv_acc)
-    key_at = lax.broadcasted_iota(jnp.int32, (KB, QB), 0)
-    row_at = lax.broadcasted_iota(jnp.int32, (KB, QB), 1)
-
-    for i in range(total_rows // QB):
-        rows = slice(i * QB, (i + 1) * QB)
-        chunks = (i + 1) * QB // KB + (1 if (i + 1) * QB % KB else 0)
+
+    def query_block(i):
+        rows = pl.ds(pl.multiple_of(i * QB, QB), QB)
+        chunks = (i * QB + QB + KB - 1) // KB
         q_i = qkv[rows, :HEAD]
         do_i = do_own[rows, :]
 
@@ -307,13 +329,15 @@
             keys = pl.ds(pl.multiple_of(c * KB, KB), KB)
             scores = lax.dot_general(qkv[keys, HEAD : 2 * HEAD], q_i, NT, preferred_element_type=F32)
             if masked:
-                scores = jnp.where(key_at <= row_at + (i * QB - (chunks - 1) * KB), scores, LOW)
+                key_at = lax.broadcasted_iota(jnp.int32, (KB, QB), 0)
+                row_at = lax.broadcasted_iota(jnp.int32, (KB, QB), 1)
+                scores = jnp.where(key_at - row_at <= i * QB - (chunks - 1) * KB, scores, LOW)
             p_buf[keys, :] = scores
             return jnp.max(scores, axis=0, keepdims=True)
 
-        top = scores_of(chunks - 1, True)
-        if chunks > 1:
-            top = lax.fori_loop(0, chunks - 1, lambda c, m: jnp.maximum(m, scores_of(c, False)), top)
+        top = lax.fori_loop(
+            0, chunks - 1, lambda c, m: jnp.maximum(m, scores_of(c, False)), scores_of(chunks - 1, True)
+        )
 
         def weigh(c, carry):
             total, acc = carry
@@ -330,10 +354,7 @@
         inv = 1.0 / total
         o_t = acc * inv
         delta = jnp.sum(o_t * do_t[:, rows].astype(F32), axis=0, keepdims=True)
-        o_i = o_t.T.astype(BF16)
-        for b in range(QB // BLK):
-            slot = dest[i * (QB // BLK) + b]
-            out[pl.ds(pl.multiple_of(slot * BLK, BLK), BLK), :] = o_i[b * BLK : (b + 1) * BLK, :]
+        out[rows, :] = o_t.T.astype(BF16)
 
         def back(c, acc):
             keys = pl.ds(pl.multiple_of(c * KB, KB), KB)
@@ -357,22 +378,59 @@
             d_all_t[which * HEAD : (which + 1) * HEAD, at] = value.T.astype(BF16)
         return carry
 
-    lax.fori_loop(0, total_rows // QB, finish, 0)
-
-
-def causal(dest, qkv, cot):
+    def weight_block(g, carry):
+        at = pl.ds(pl.multiple_of(g * QB, QB), QB)
+        value = jnp.dot(d_all_t[...], rows_in[:, at], preferred_element_type=F32)
+        for which in range(3):
+            grads[which, at, :] = value[which * HEAD : (which + 1) * HEAD, :].T.astype(BF16)
+        return carry
+
+    col_blocks = rows_in.shape[1] // QB
+    share = (col_blocks + 2) // 3
+
+    def step(t, carry):
+        flow.step(t)
+
+        @pl.when(t < blocks)
+        def _():
+            query_block(blocks - 1 - t)
+
+        @pl.when(t == blocks)
+        def _():
+            lax.fori_loop(0, blocks, finish, 0)
+            rows_copy.wait()
+
+        @pl.when(t >= blocks)
+        def _():
+            low = (t - blocks) * share
+            lax.fori_loop(low, jnp.minimum(low + share, col_blocks), weight_block, 0)
+
+        return carry
+
+    lax.fori_loop(0, blocks + 3, step, 0)
+    flow.drain()
+
+
+def causal(dest, sel, qkv, cot, normed, query, key, value, per_chunk, ident):
     total_rows, local = qkv.shape
+    tok, full = key.shape
+    rows = sel.shape[0] // 3 * BLK
     vmem = pl.BlockSpec(memory_space=pltpu.VMEM)
+    smem = pl.BlockSpec(memory_space=pltpu.SMEM)
     return pl.pallas_call(
         causal_kernel,
         out_shape=(
             jax.ShapeDtypeStruct((total_rows, HEAD), BF16),
             jax.ShapeDtypeStruct((total_rows, local), BF16),
-            jax.ShapeDtypeStruct((local, total_rows), BF16),
-        ),
-        in_specs=[pl.BlockSpec(memory_space=pltpu.SMEM), vmem, vmem],
-        out_specs=[vmem, vmem, vmem],
+            jax.ShapeDtypeStruct((3, full, HEAD), BF16),
+            jax.ShapeDtypeStruct((rows, full), BF16),
+        ),
+        in_specs=[smem, smem, vmem, vmem, pl.BlockSpec(memory_space=pl.ANY), vmem, vmem, vmem],
+        out_specs=[vmem, vmem, vmem, vmem],
         scratch_shapes=[
+            pltpu.VMEM((total_rows, full), BF16),
+            pltpu.SemaphoreType.DMA,
+            pltpu.VMEM((local, total_rows), BF16),
             pltpu.VMEM((HEAD, total_rows), BF16),
             pltpu.VMEM((HEAD, total_rows), BF16),
             pltpu.VMEM((total_rows, HEAD), BF16),
@@ -381,10 +439,16 @@
             pltpu.VMEM((total_rows, HEAD), F32),
             pltpu.VMEM((total_rows, HEAD), F32),
             pltpu.VMEM((HEAD, total_rows), F32),
+            *Flow.scratch(rows, tok, full, per_chunk),
         ],
-        compiler_params=pltpu.CompilerParams(vmem_limit_bytes=VMEM_LIMIT),
+        compiler_params=pltpu.CompilerParams(
+            collective_id=ident, has_side_effects=True, vmem_limit_bytes=VMEM_LIMIT
+        ),
+        cost_estimate=pl.CostEstimate(
+            flops=20 * 10**9, bytes_accessed=32 * 1024 * 1024, transcendentals=0
+        ),
         name="causal",
-    )(dest, qkv, cot)
+    )(dest, sel, qkv, cot, normed, query, key, value)
 
 
 SIDE = 4
@@ -556,31 +620,14 @@
     )(slot_at, d_all, weights)
 
 
-def weight_grad_kernel(d_t, normed, out):
-    value = jnp.dot(d_t[...], normed[...], preferred_element_type=F32)
-    for at in range(3):
-        out[at] = value[at * HEAD : (at + 1) * HEAD, :].T.astype(BF16)
-
-
-def weight_grad(d_t, normed, step=256):
-    local, total_rows = d_t.shape
-    full = normed.shape[1]
-    return pl.pallas_call(
-        weight_grad_kernel,
-        out_shape=jax.ShapeDtypeStruct((3, full, HEAD), BF16),
-        grid=(full // step,),
-        in_specs=[
-            pl.BlockSpec((local, total_rows), lambda g: (0, 0)),
-            pl.BlockSpec((total_rows, step), lambda g: (0, g)),
-        ],
-        out_specs=pl.BlockSpec((3, step, HEAD), lambda g: (0, g, 0)),
-        compiler_params=pltpu.CompilerParams(vmem_limit_bytes=VMEM_LIMIT),
-        name="weight_grad",
-    )(d_t, normed)
-
-
-def assemble_kernel(table, head, rest, out):
-    first = table[3 * pl.program_id(0)] == 1
+def assemble_kernel(table, head, rest, sorted_out, out, causal_out):
+    kept = sorted_out.shape[0] // BLK
+    first = table[kept + 3 * pl.program_id(0)] == 1
+
+    @pl.when(pl.program_id(0) == 0)
+    def _():
+        for j in range(kept):
+            causal_out[pl.ds(pl.multiple_of(table[j] * BLK, BLK), BLK), :] = sorted_out[j * BLK : (j + 1) * BLK, :]
 
     @pl.when(first)
     def _():
@@ -591,22 +638,28 @@
         out[...] = rest[...]
 
 
-def assemble(table, head, rest):
+def assemble(table, head, rest, sorted_out):
     rows, full = head.shape
+    kept = sorted_out.shape[0] // BLK
+    whole = pl.BlockSpec(sorted_out.shape, lambda g, t: (0, 0))
     return pl.pallas_call(
         assemble_kernel,
-        out_shape=jax.ShapeDtypeStruct((2 * rows, full), BF16),
+        out_shape=(
+            jax.ShapeDtypeStruct((2 * rows, full), BF16),
+            jax.ShapeDtypeStruct(sorted_out.shape, BF16),
+        ),
         grid_spec=pltpu.PrefetchScalarGridSpec(
             num_scalar_prefetch=1,
             grid=(2 * rows // BLK,),
             in_specs=[
-                pl.BlockSpec((BLK, full), lambda g, t: (t[3 * g + 1], 0)),
-                pl.BlockSpec((BLK, full), lambda g, t: (t[3 * g + 2], 0)),
+                pl.BlockSpec((BLK, full), lambda g, t: (t[kept + 3 * g + 1], 0)),
+                pl.BlockSpec((BLK, full), lambda g, t: (t[kept + 3 * g + 2], 0)),
+                whole,
             ],
-            out_specs=pl.BlockSpec((BLK, full), lambda g, t: (g, 0)),
+            out_specs=[pl.BlockSpec((BLK, full), lambda g, t: (g, 0)), whole],
         ),
         name="assemble",
-    )(table, head, rest)
+    )(table, head, rest, sorted_out)
 
 
 def shards(query_input, key_input, value_input, keep_blocks, dest_slots, proj_weights, cotangent):
@@ -650,19 +703,15 @@
         axis=1,
     ).astype(jnp.int32)
 
-    first = window(sel_first, query, key, value, 0, 1, 2, 0)
+    first = window(sel_first, query, key, value, 2, 0)
     gathered = lax.all_gather(first, SEQ, axis=0, tiled=True)
-    sel_late, _ = lax.optimization_barrier((sel_rest, first))
-    rest = window(sel_late, query, key, value, 0, 1, 2, 1)
-    window_out = assemble(table, first, rest)
-
-    packed_late, _ = lax.optimization_barrier((packed, rest))
-    normed, qkv = project(packed_late, gathered, weights)
-    causal_out, d_all, d_all_t = causal(dest, qkv, cotangent[0])
-    local_grads = weight_grad(d_all_t, normed)
+    normed, qkv = project(packed, gathered, weights)
+    sorted_out, d_all, local_grads, rest = causal(
+        dest, sel_rest, qkv, cotangent.reshape(dest.shape[0], BLK, -1), normed, query, key, value, 2, 1
+    )
     grads = lax.psum(local_grads, "dp").astype(F32)
-    slot_late, _ = lax.optimization_barrier((slot_at, local_grads))
-    row_grad = scatter_terms(slot_late, d_all.reshape(dest.shape[0], BLK, -1), weights, 2)
+    window_out, causal_out = assemble(jnp.concatenate([dest, table]), first, rest, sorted_out)
+    row_grad = scatter_terms(slot_at, d_all.reshape(dest.shape[0], BLK, -1), weights, 2)
     return (window_out[None], causal_out[None], grads, row_grad[None])
 
 

time: 378 us -> 358 us (0.947)
  Pallas kernels: 299 us -> 222 us
  waiting for transfers between devices: 53.9 us -> 111 us
    pallas_call x4 -> x2, Pallas kernels: 212 us -> 82.2 us  [the longest x1 77 us: window(): pl.pallas_call(window_kernel, out_shape=jax.ShapeDtypeStruct((rows, full)...]
    all_gather x1, waiting for transfers between devices: 48.4 us -> 105 us  [shards(): gathered = lax.all_gather(first, SEQ, axis=0, tiled=True)]
    pallas_call x1, Pallas kernels: 24.7 us -> 78.5 us  [causal(): pl.pallas_call(causal_kernel, out_shape=(jax.ShapeDtypeStruct((total_rows...]
  transfers between devices with their start and end apart: 2 -> 2, of which waited for: 2 -> 2; matrix products, arithmetic and copies ran while one was open for 1% -> 1% of each run, Pallas kernels for 45% -> 15%
where the time goes in v3:
time: 358 us
  Pallas kernels  222 us (62%)
  waiting for transfers between devices  111 us (31%)
  between operations  14.1 us (4%)
  other arithmetic  7.58 us (2%)
    all_gather x1, waiting for transfers between devices, shards(): gathered = lax.all_gather(first, SEQ, axis=0, tiled=True)  105 us
    pallas_call x1, Pallas kernels, causal(): pl.pallas_call(causal_kernel, out_shape=(jax.ShapeDtypeStruct((total_rows...  78.5 us
    pallas_call x1, Pallas kernels, window(): pl.pallas_call(window_kernel, out_shape=jax.ShapeDtypeStruct((rows, full)...  77 us
    pallas_call x1, Pallas kernels, scatter_terms(): pl.pallas_call(scatter_kernel, out_shape=jax.ShapeDtypeStruct((BLK, full)...  49.2 us
    pallas_call x1, Pallas kernels, project(): pl.pallas_call(project_kernel, out_shape=(jax.ShapeDtypeStruct((kept * BL...  12 us
  transfers between devices with their start and end apart: 2, of which 2 were waited for; matrix products, arithmetic and copies ran while one was open for 1% of the time, Pallas kernels for 15%

profile of v3, /device:TPU:0, one launch (start us, length us, event | category | flops | bytes accessed | tf_op | source)
XLA Modules:
  0.0 357.7 jit_solution(9823568075369100036)
XLA Ops:
  7.2 0.0 all-gather.2.cloned.1.call-start
  7.2 0.9 compare_reduce_fusion
  8.2 0.1 pad_add_fusion.1
  8.2 0.1 constant_dynamic-slice_fusion
  8.3 0.1 copy.20
  8.4 0.6 reshape.176.sel
  9.0 77.0 %window.1.head = bf16[256,2048]{1,0:T(8,128)(2,1)} custom-call(s32[6]{0:T(128)} %reshape.176.sel, bf16[4,128,2048]{2,1,0:T(8,128)(2,1)} %bitcast.36, bf16[512,2048]{1,0:T(8,128)(2,1)} %bitcast.38, bf16[512,2048]{1,0:T(8,128)(2,1)} %bitcast.40), custom_call_target="tpu_custom_call" | custom-call | flops 3221225472 | bytes 16777216 | tf_op jit(solution)/shard_map/window/pallas_call | solution.py:241
  86.0 0.0 all-gather.2.cloned.1.call-update
  86.0 0.2 all-reduce.2.cloned.1.call-start
  86.3 0.2 dynamic-slice_reduce_fusion
  86.4 0.1 copy.21
  86.5 0.6 reshape.178.sel
  87.1 0.0 copy-done.2
  87.2 0.2 convert_reduce_fusion
  87.4 0.5 multiply_add_fusion.1.index
  87.9 0.0 copy-done
  87.9 0.1 slice_bitcast_fusion.2
  88.0 1.3 pad_maximum_fusion.weights
  89.3 104.6 %all-gather.2.cloned.1.call-done.first.second = bf16[4096,2048]{1,0:T(8,128)(2,1)} async-done(((bf16[256,2048]{1,0:T(8,128)(2,1)}), bf16[4096,2048]{1,0:T(8,128)(2,1)}) %all-gather.2.cloned.1.call-update) | async-done | bytes 16777232 | tf_op jit(solution)/shard_map/all_gather | solution.py:707
  194.0 12.0 %project.1 = (bf16[2048,2048]{1,0:T(8,128)(2,1)}, bf16[2048,384]{1,0:T(8,128)(2,1)}) custom-call(s32[16]{0:T(128)} %multiply_add_fusion.1.index, bf16[4096,2048]{1,0:T(8,128)(2,1)} %all-gather.2.cloned.1.call-done.first.second, bf16[4096,2048]{1,0:T(8,128)(2,1)} %all-gather.2.cloned.1.call-done.first.second, bf16[2048,384]{1,0:T(8,128)(2,1)} %pad_maximum_fusion.weights), custom_call_target="tpu_custom_call" | custom-call | tf_op jit(solution)/shard_map/project/pallas_call | solution.py:268
  206.0 78.5 %causal.1 = (bf16[2048,128]{1,0:T(8,128)(2,1)}, bf16[2048,384]{1,0:T(8,128)(2,1)}, bf16[3,2048,128]{2,1,0:T(8,128)(2,1)}, bf16[256,2048]{1,0:T(8,128)(2,1)}) custom-call(s32[16]{0:T(128)} %bitcast.45, s32[6]{0:T(128)} %reshape.178.sel, bf16[2048,384]{1,0:T(8,128)(2,1)} %get-tuple-element.12.qkv, bf16[16,128,128]{2,1,0:T(8,128)(2,1)} %bitcast.43, ...), custom_call_target="tpu_custom_call" | custom-call | flops 20000000000 | bytes 33554432 | tf_op jit(solution)/shard_map/causal/pallas_call | solution.py:420
  284.5 0.0 all-reduce.2.cloned.1.call-update
  284.6 0.1 copy.19
  284.7 0.1 reshape.175
  284.7 0.0 copy-done.3
  284.7 0.6 pad_add_fusion.2.table
  285.3 0.6 select_reduce_fusion.slot_at
  286.0 49.2 %scatter_terms.1 = bf16[128,2048]{1,0:T(8,128)(2,1)} custom-call(s32[16]{0:T(128)} %select_reduce_fusion.slot_at, bf16[16,128,384]{2,1,0:T(8,128)(2,1)} %bitcast.48, bf16[2048,384]{1,0:T(8,128)(2,1)} %pad_maximum_fusion.weights), custom_call_target="tpu_custom_call" | custom-call | flops 3221225472 | bytes 104857600 | tf_op jit(solution)/shard_map/scatter_terms/pallas_call | solution.py:597
  335.2 5.2 %assemble.1 = (bf16[512,2048]{1,0:T(8,128)(2,1)}, bf16[2048,128]{1,0:T(8,128)(2,1)}) custom-call(s32[28]{0:T(128)} %pad_add_fusion.2.table, bf16[256,2048]{1,0:T(8,128)(2,1)} %window.1.head, bf16[256,2048]{1,0:T(8,128)(2,1)} %get-tuple-element.14.rest, bf16[2048,128]{1,0:T(8,128)(2,1)} %get-tuple-element.15.sorted_out), custom_call_target="tpu_custom_call" | custom-call | tf_op jit(solution)/shard_map/assemble/pallas_call | solution.py:645
  340.4 6.4 %all-reduce.2.cloned.1.call-done = bf16[3,2048,128]{2,1,0:T(8,128)(2,1)} async-done(((bf16[3,2048,128]{2,1,0:T(8,128)(2,1)}), bf16[3,2048,128]{2,1,0:T(8,128)(2,1)}) %all-reduce.2.cloned.1.call-update) | async-done | bytes 1572880 | tf_op jit(solution)/shard_map/psum | solution.py:712
  346.8 3.3 convert_element_type.26
  350.1 0.8 copy.24
  (15 shorter events, 0.1 us)
Async XLA Ops:
  7.2 186.8 %all-gather.2.cloned.1.call-start = ((), (), s32[]{:S(2)}) async-start(), calls=%async_computation | async-start | bytes 17825792 | tf_op jit(solution)/shard_map/all_gather | solution.py:707
  9.0 78.1 %copy-start.2 = (s32[1,16]{1,0:T(1,128)S(1)}, s32[1,16]{1,0:T(1,128)}, u32[]{:S(2)}) copy-start(s32[1,16]{1,0:T(1,128)} %param.10) | copy-start | bytes 196
  9.0 78.9 %copy-start = (bf16[3,2048,128]{2,1,0:T(8,128)(2,1)S(1)}, bf16[3,2048,128]{2,1,0:T(8,128)(2,1)}, u32[]{:S(2)}) copy-start(bf16[3,2048,128]{2,1,0:T(8,128)(2,1)} %param.12) | copy-start | bytes 4718596
  86.0 260.8 %all-reduce.2.cloned.1.call-start = ((), (), s32[]{:S(2)}) async-start(), calls=%async_computation.1 | async-start | bytes 3145728 | tf_op jit(solution)/shard_map/psum | solution.py:712
  206.0 78.8 %copy-start.3 = (s32[1,16]{1,0:T(1,128)S(1)}, s32[1,16]{1,0:T(1,128)}, u32[]{:S(2)}) copy-start(s32[1,16]{1,0:T(1,128)} %param.11) | copy-start | bytes 196
  340.4 9.7 %copy-start.1 = (bf16[128,2048]{1,0:T(8,128)(2,1)S(1)}, bf16[128,2048]{1,0:T(8,128)(2,1)}, u32[]{:S(2)}) copy-start(bf16[128,2048]{1,0:T(8,128)(2,1)} %scatter_terms.1) | copy-start | bytes 1572868
Sparse Core Ops, SparseCore 0:
  86.1 107.7 all-gather.1
  284.7 62.1 all-reduce.1

commit v4 on v3

--- a/solution.py
+++ b/solution.py
@@ -81,16 +81,17 @@
             self.copy(5, c, self.l_snd1, self.l_got1, self.right),
         )
 
-    def begin(self, ahead):
+    def begin(self, ahead, others=()):
         barrier = pltpu.get_barrier_semaphore()
-        for neighbour in (self.left, self.right):
+        greeted = (self.left, self.right, *others)
+        for neighbour in greeted:
             pl.semaphore_signal(barrier, inc=1, device_id={SEQ: neighbour}, device_id_type=MESH)
         picks = self.rows // BLK
         for a in range(picks):
             block = self.q_in[self.sel[a]]
             for c in range(self.chunks):
                 self.q_own[c, a * BLK : (a + 1) * BLK, :] = block[:, c * self.width : (c + 1) * self.width]
-        pl.semaphore_wait(barrier, 2)
+        pl.semaphore_wait(barrier, len(greeted))
         for c in range(ahead):
             self.hop_one(c).start()
         self.ahead = ahead
@@ -177,7 +178,10 @@
                 self.o_own[c, self.head(h), :], self.l_own[c, first : first + 1, :],
                 self.o_got1[c, self.head(h), :].astype(F32), self.incoming(self.l_got1, h, c),
             )
-            self.out[:, self.cols(c, h)] = part.T.astype(BF16)
+            self.store(c, h, part.T.astype(BF16))
+
+    def store(self, c, h, value):
+        self.out[:, self.cols(c, h)] = value
 
     def step(self, t):
         @pl.when(t < self.chunks)
@@ -193,7 +197,7 @@
         def _():
             self.one(t - 2)
 
-        @pl.when(t >= 3)
+        @pl.when((t >= 3) & (t <= self.chunks + 2))
         def _():
             self.final(t - 3)
 
@@ -222,71 +226,260 @@
         ]
 
 
-def window_kernel(sel, q_in, k_in, v_in, out, *scratch):
+SIDE = 4
+
+
+class Spread:
+    OFFSETS = (0, 1, SIDE - 1, 2)
+
+    def __init__(self, got, send_sem, recv_sem):
+        self.got, self.send_sem, self.recv_sem = got, send_sem, recv_sem
+        shard = lax.axis_index(SEQ)
+        self.row, self.col = shard // SIDE, lax.rem(shard, SIDE)
+
+    @staticmethod
+    def turn(at, by):
+        return lax.rem(at + by + SIDE, SIDE)
+
+    def neighbours(self):
+        return [self.row * SIDE + self.turn(self.col, by) for by in (1, -1)] + [
+            self.turn(self.row, by) * SIDE + self.col for by in (1, -1)
+        ]
+
+    def places(self, c):
+        rows_first = (c >= 3) & (lax.rem(c, 2) == 1)
+        return rows_first, jnp.where(rows_first, self.row, self.col), jnp.where(rows_first, self.col, self.row)
+
+    def message(self, c, which, place, half, target):
+        rows_first, _, _ = self.places(c)
+        a, b = place
+        ta, tb = target
+        slot = jnp.where(rows_first, a * SIDE + b, b * SIDE + a)
+        device = jnp.where(rows_first, ta * SIDE + tb, tb * SIDE + ta)
+        ref = self.got.at[c, slot] if half is None else self.got.at[c, slot, half]
+        return pltpu.make_async_remote_copy(
+            src_ref=ref, dst_ref=ref, send_sem=self.send_sem.at[c, which], recv_sem=self.recv_sem.at[c, which],
+            device_id={SEQ: device}, device_id_type=MESH,
+        )
+
+    def ring(self, c, base, near):
+        here, up, down, far = near(0), near(1), near(-1), near(2)
+        direct = (
+            self.message(c, base, here, None, up), self.message(c, base + 1, here, None, down),
+        )
+        direct_in = (
+            self.message(c, base, down, None, up), self.message(c, base + 1, up, None, down),
+        )
+        half = (
+            self.message(c, base + 2, down, 0, up), self.message(c, base + 3, up, 1, down),
+        )
+        half_in = (
+            self.message(c, base + 2, far, 0, up), self.message(c, base + 3, far, 1, down),
+        )
+        return direct, direct_in, half, half_in
+
+    def first_ring(self, c):
+        _, a, b = self.places(c)
+        return self.ring(c, 0, lambda by: (self.turn(a, by), b))
+
+    def second_ring(self, c, k):
+        _, a, b = self.places(c)
+        origin = self.turn(a, self.OFFSETS[k])
+        direct, direct_in, half, half_in = self.ring(c, 4 + 4 * k, lambda by: (origin, self.turn(b, by)))
+        return direct, direct_in, half, half_in
+
+    def second_sends(self, c, k):
+        _, a, b = self.places(c)
+        origin = self.turn(a, self.OFFSETS[k])
+        up, down = (a, self.turn(b, 1)), (a, self.turn(b, -1))
+        base = 4 + 4 * k
+        direct = (
+            self.message(c, base, (origin, b), None, up), self.message(c, base + 1, (origin, b), None, down),
+        )
+        half = (
+            self.message(c, base + 2, (origin, self.turn(b, -1)), 0, up),
+            self.message(c, base + 3, (origin, self.turn(b, 1)), 1, down),
+        )
+        return direct, half
+
+    def launch(self, c):
+        for each in self.first_ring(c)[0]:
+            each.start()
+
+    def relay(self, c):
+        _, direct_in, half, _ = self.first_ring(c)
+        for each in direct_in:
+            each.wait_recv()
+        for each in half:
+            each.start()
+        for k in range(3):
+            for each in self.second_sends(c, k)[0]:
+                each.start()
+
+    def relay_far(self, c):
+        for each in self.first_ring(c)[3]:
+            each.wait_recv()
+        for each in self.second_sends(c, 3)[0]:
+            each.start()
+
+    def second_relay(self, c):
+        for k in range(4):
+            for each in self.second_ring(c, k)[1]:
+                each.wait_recv()
+            for each in self.second_sends(c, k)[1]:
+                each.start()
+
+    def settle(self, c):
+        for k in range(4):
+            for each in self.second_ring(c, k)[3]:
+                each.wait_recv()
+
+    def drain(self, c):
+        direct, _, half, _ = self.first_ring(c)
+        for each in direct + half:
+            each.wait_send()
+        for k in range(4):
+            direct, half = self.second_sends(c, k)
+            for each in direct + half:
+                each.wait_send()
+
+
+def front_kernel(
+    kept_shard, kept_at, sel, q_in, k_in, v_in, weights, out, rows_out, projected, scale_out,
+    got, held, staged, staged_sem, total, squares, spread_send, spread_recv, *scratch,
+):
+    kept = kept_shard.shape[0]
     flow = Flow(sel, q_in, k_in, v_in, out, scratch)
-    flow.begin(2)
+    spread = Spread(got, spread_send, spread_recv)
+    chunks, width = flow.chunks, flow.width
+    total_rows, local = projected.shape
+    full = k_in.shape[1]
+    block = 512
+
+    def store(c, h, value):
+        out[:, flow.cols(c, h)] = value
+        for a in range(flow.rows // BLK):
+            got[c, flow.shard, a, :, flow.head(h)] = value[a * BLK : (a + 1) * BLK, :]
+
+    flow.store = store
+    flow.begin(3, spread.neighbours())
+    total[...] = jnp.zeros_like(total)
+    squares[...] = jnp.zeros_like(squares)
+
+    def staged_copy(c):
+        which = lax.rem(c, 2)
+        return pltpu.make_async_copy(staged.at[which], rows_out.at[c], staged_sem.at[which])
+
+    def project_chunk(c):
+        which = lax.rem(c, 2)
+
+        @pl.when(c >= 2)
+        def _():
+            staged_copy(c - 2).wait()
+
+        def hold(i, carry):
+            held[i] = got[c, i]
+            return carry
+
+        lax.fori_loop(0, SIDE * SIDE, hold, 0)
+
+        def pick(j, carry):
+            at = pl.ds(pl.multiple_of(j * BLK, BLK), BLK)
+            staged[which, at, :] = held[kept_shard[j], kept_at[j]]
+            return carry
+
+        lax.fori_loop(0, kept, pick, 0)
+        staged_copy(c).start()
+        weight = weights[pl.ds(pl.multiple_of(c * width, width), width), :]
+
+        def multiply(r, carry):
+            at = pl.ds(pl.multiple_of(r * block, block), block)
+            rows = staged[which, at, :]
+            total[at, :] += jnp.dot(rows, weight, preferred_element_type=F32)
+            wide = rows.astype(F32)
+            square = wide * wide
+            squares[at, :] += sum(square[:, h * HEAD : (h + 1) * HEAD] for h in range(flow.per_chunk))
+            return carry
+
+        lax.fori_loop(0, total_rows // block, multiply, 0)
 
     def step(t, carry):
         flow.step(t)
+
+        def stage(late, call):
+            @pl.when((t >= late) & (t < chunks + late))
+            def _():
+                call(t - late)
+
+        stage(3, spread.launch)
+        stage(4, spread.relay)
+        stage(5, spread.relay_far)
+        stage(6, spread.second_relay)
+
+        @pl.when(t >= 7)
+        def _():
+            spread.settle(t - 7)
+            project_chunk(t - 7)
+
         return carry
 
-    lax.fori_loop(0, flow.chunks + 3, step, 0)
+    lax.fori_loop(0, chunks + 7, step, 0)
+
+    def finish(r, carry):
+        at = pl.ds(pl.multiple_of(r * block, block), block)
+        square = squares[at, :]
+        inv = lax.rsqrt(jnp.sum(square, axis=1, keepdims=True) * (1.0 / full) + 1e-06)
+        projected[at, :] = (total[at, :] * inv).astype(BF16)
+        scale_out[:, at] = lax.rsqrt(jnp.sum(square.T, axis=0, keepdims=True) * (1.0 / full) + 1e-06)
+        return carry
+
+    lax.fori_loop(0, total_rows // block, finish, 0)
+
+    def drain(c, carry):
+        spread.drain(c)
+        return carry
+
+    lax.fori_loop(0, chunks, drain, 0)
+    for c in (chunks - 2, chunks - 1):
+        staged_copy(c).wait()
     flow.drain()
 
 
-def window(sel, query, key, value, per_chunk, ident):
+def front(kept_shard, kept_at, sel, query, key, value, weights, per_chunk, ident):
     tok, full = key.shape
+    local = weights.shape[1]
     rows = sel.shape[0] // 3 * BLK
+    total_rows = kept_shard.shape[0] * BLK
+    width = per_chunk * HEAD
+    chunks = full // width
     vmem = pl.BlockSpec(memory_space=pltpu.VMEM)
+    smem = pl.BlockSpec(memory_space=pltpu.SMEM)
     return pl.pallas_call(
-        window_kernel,
-        out_shape=jax.ShapeDtypeStruct((rows, full), BF16),
-        in_specs=[pl.BlockSpec(memory_space=pltpu.SMEM), vmem, vmem, vmem],
-        out_specs=vmem,
-        scratch_shapes=Flow.scratch(rows, tok, full, per_chunk),
+        front_kernel,
+        out_shape=(
+            jax.ShapeDtypeStruct((rows, full), BF16),
+            jax.ShapeDtypeStruct((chunks, total_rows, width), BF16),
+            jax.ShapeDtypeStruct((total_rows, local), BF16),
+            jax.ShapeDtypeStruct((1, total_rows), F32),
+        ),
+        in_specs=[smem, smem, smem, vmem, vmem, vmem, vmem],
+        out_specs=[vmem, pl.BlockSpec(memory_space=pl.ANY), vmem, vmem],
+        scratch_shapes=[
+            pltpu.VMEM((chunks, SIDE * SIDE, rows // BLK, BLK, width), BF16),
+            pltpu.VMEM((SIDE * SIDE, rows // BLK, BLK, width), BF16),
+            pltpu.VMEM((2, total_rows, width), BF16),
+            pltpu.SemaphoreType.DMA((2,)),
+            pltpu.VMEM((total_rows, local), F32),
+            pltpu.VMEM((total_rows, HEAD), F32),
+            pltpu.SemaphoreType.DMA((chunks, 20)),
+            pltpu.SemaphoreType.DMA((chunks, 20)),
+            *Flow.scratch(rows, tok, full, per_chunk),
+        ],
         compiler_params=pltpu.CompilerParams(
             collective_id=ident, has_side_effects=True, vmem_limit_bytes=VMEM_LIMIT
         ),
-        cost_estimate=pl.CostEstimate(
-            flops=12 * rows * tok * full, bytes_accessed=16 * 1024 * 1024, transcendentals=0
-        ),
-        name="window",
-    )(sel, query, key, value)
-
-
-def project_kernel(index, first, second, weights, normed, projected):
-    for at, block in enumerate((first, second)):
-        x = block[...].astype(F32)
-        mean = jnp.sum(x * x, axis=1, keepdims=True) * (1.0 / x.shape[1])
-        normed[at * BLK : (at + 1) * BLK, :] = (x * lax.rsqrt(mean + 1e-06)).astype(BF16)
-    projected[...] = jnp.dot(normed[...], weights[...], preferred_element_type=F32).astype(BF16)
-
-
-def project(index, rows, weights):
-    kept = index.shape[0]
-    full, local = weights.shape
-    return pl.pallas_call(
-        project_kernel,
-        out_shape=(
-            jax.ShapeDtypeStruct((kept * BLK, full), BF16),
-            jax.ShapeDtypeStruct((kept * BLK, local), BF16),
-        ),
-        grid_spec=pltpu.PrefetchScalarGridSpec(
-            num_scalar_prefetch=1,
-            grid=(kept // 2,),
-            in_specs=[
-                pl.BlockSpec((BLK, full), lambda g, idx: (idx[2 * g], 0)),
-                pl.BlockSpec((BLK, full), lambda g, idx: (idx[2 * g + 1], 0)),
-                pl.BlockSpec((full, local), lambda g, idx: (0, 0)),
-            ],
-            out_specs=[
-                pl.BlockSpec((2 * BLK, full), lambda g, idx: (g, 0)),
-                pl.BlockSpec((2 * BLK, local), lambda g, idx: (g, 0)),
-            ],
-        ),
-        compiler_params=pltpu.CompilerParams(vmem_limit_bytes=VMEM_LIMIT),
-        name="project",
-    )(index, rows, rows, weights)
+        name="front",
+    )(kept_shard, kept_at, sel, query, key, value, weights)
 
 
 QB = 256
@@ -294,16 +487,16 @@
 
 
 def causal_kernel(
-    dest, sel, qkv, cot, normed, q_in, k_in, v_in, out, d_all, grads, rest,
+    dest, sel, qkv, scale, cot, gathered, q_in, k_in, v_in, out, d_all, grads, rest,
     rows_in, rows_sem, d_all_t, v_t, k_t, do_own, do_t, p_buf, dk_acc, dv_acc, dq_t, *scratch,
 ):
     kept = dest.shape[0]
     total_rows = qkv.shape[0]
     blocks = total_rows // QB
-    rows_copy = pltpu.make_async_copy(normed, rows_in, rows_sem)
+    rows_copy = pltpu.make_async_copy(gathered, rows_in, rows_sem)
     rows_copy.start()
     flow = Flow(sel, q_in, k_in, v_in, rest, scratch)
-    flow.begin(2)
+    flow.begin(3)
 
     for j in range(kept):
         do_own[j * BLK : (j + 1) * BLK, :] = cot[dest[j]]
@@ -370,22 +563,22 @@
     def finish(c, carry):
         at = pl.ds(pl.multiple_of(c * QB, QB), QB)
         d_q = dq_t[:, at]
-        d_all_t[:HEAD, at] = d_q.astype(BF16)
+        d_all_t[:HEAD, at] = (d_q * scale[:, at]).astype(BF16)
         d_all[at, :HEAD] = d_q.T.astype(BF16)
         for which, acc in ((1, dk_acc), (2, dv_acc)):
             value = acc[at, :]
             d_all[at, which * HEAD : (which + 1) * HEAD] = value.astype(BF16)
-            d_all_t[which * HEAD : (which + 1) * HEAD, at] = value.T.astype(BF16)
+            d_all_t[which * HEAD : (which + 1) * HEAD, at] = (value.T * scale[:, at]).astype(BF16)
         return carry
 
     def weight_block(g, carry):
         at = pl.ds(pl.multiple_of(g * QB, QB), QB)
-        value = jnp.dot(d_all_t[...], rows_in[:, at], preferred_element_type=F32)
+        value = jnp.dot(d_all_t[...], rows_in[g], preferred_element_type=F32)
         for which in range(3):
             grads[which, at, :] = value[which * HEAD : (which + 1) * HEAD, :].T.astype(BF16)
         return carry
 
-    col_blocks = rows_in.shape[1] // QB
+    col_blocks = rows_in.shape[0]
     share = (col_blocks + 2) // 3
 
     def step(t, carry):
@@ -411,7 +604,7 @@
     flow.drain()
 
 
-def causal(dest, sel, qkv, cot, normed, query, key, value, per_chunk, ident):
+def causal(dest, sel, qkv, scale, cot, gathered, query, key, value, per_chunk, ident):
     total_rows, local = qkv.shape
     tok, full = key.shape
     rows = sel.shape[0] // 3 * BLK
@@ -425,10 +618,10 @@
             jax.ShapeDtypeStruct((3, full, HEAD), BF16),
             jax.ShapeDtypeStruct((rows, full), BF16),
         ),
-        in_specs=[smem, smem, vmem, vmem, pl.BlockSpec(memory_space=pl.ANY), vmem, vmem, vmem],
+        in_specs=[smem, smem, vmem, vmem, vmem, pl.BlockSpec(memory_space=pl.ANY), vmem, vmem, vmem],
         out_specs=[vmem, vmem, vmem, vmem],
         scratch_shapes=[
-            pltpu.VMEM((total_rows, full), BF16),
+            pltpu.VMEM(gathered.shape, BF16),
             pltpu.SemaphoreType.DMA,
             pltpu.VMEM((local, total_rows), BF16),
             pltpu.VMEM((HEAD, total_rows), BF16),
@@ -448,10 +641,7 @@
             flops=20 * 10**9, bytes_accessed=32 * 1024 * 1024, transcendentals=0
         ),
         name="causal",
-    )(dest, sel, qkv, cot, normed, query, key, value)
-
-
-SIDE = 4
+    )(dest, sel, qkv, scale, cot, gathered, query, key, value)
 
 
 def scatter_kernel(
@@ -695,7 +885,6 @@
     table = jnp.stack([in_first, at * in_first, at * (1 - in_first)], axis=1).reshape(-1)
     keep_shard = keep // per_shard
     before = jnp.sum((keep_shard[None, :] == keep_shard[:, None]) & (keep[None, :] < keep[:, None]), axis=1)
-    packed = (keep_shard * half_blocks + before).astype(jnp.int32)
     weights = jnp.concatenate([proj_weights[0], proj_weights[1], proj_weights[2]], axis=1)
 
     slot_at = jnp.sum(
@@ -703,11 +892,11 @@
         axis=1,
     ).astype(jnp.int32)
 
-    first = window(sel_first, query, key, value, 2, 0)
-    gathered = lax.all_gather(first, SEQ, axis=0, tiled=True)
-    normed, qkv = project(packed, gathered, weights)
+    first, gathered, qkv, scale = front(
+        keep_shard.astype(jnp.int32), before.astype(jnp.int32), sel_first, query, key, value, weights, 2, 0
+    )
     sorted_out, d_all, local_grads, rest = causal(
-        dest, sel_rest, qkv, cotangent.reshape(dest.shape[0], BLK, -1), normed, query, key, value, 2, 1
+        dest, sel_rest, qkv, scale, cotangent.reshape(dest.shape[0], BLK, -1), gathered, query, key, value, 2, 1
     )
     grads = lax.psum(local_grads, "dp").astype(F32)
     window_out, causal_out = assemble(jnp.concatenate([dest, table]), first, rest, sorted_out)

time: 358 us -> 356 us (level)
  waiting for transfers between devices: 111 us -> 11.8 us
  Pallas kernels: 222 us -> 317 us
    all_gather x1 -> x0, waiting for transfers between devices: 105 us -> none  [shards(): gathered = lax.all_gather(first, SEQ, axis=0, tiled=True)]
    pallas_call x2 -> x1, Pallas kernels: 89 us -> 188 us  [front(): pl.pallas_call(front_kernel, out_shape=(jax.ShapeDtypeStruct((rows, full)...]
    psum x1, waiting for transfers between devices: 6.45 us -> 11.8 us  [shards(): grads = lax.psum(local_grads, 'dp').astype(F32)]
    pallas_call x1, Pallas kernels: 49.2 us -> 44 us  [scatter_terms(): pl.pallas_call(scatter_kernel, out_shape=jax.ShapeDtypeStruct((BLK, full)...]
  transfers between devices with their start and end apart: 2 -> 1, of which waited for: 2 -> 1; matrix products, arithmetic and copies ran while one was open for 1% -> 0% of each run, Pallas kernels for 15% -> 14%
where the time goes in v4:
time: 356 us
  Pallas kernels  317 us (89%)
  between operations  14.1 us (4%)
  waiting for transfers between devices  11.8 us (3%)
  other arithmetic  8.88 us (2%)
  local copies, waits for them, and re-layouts  4.17 us (1%)
    pallas_call x1, Pallas kernels, front(): pl.pallas_call(front_kernel, out_shape=(jax.ShapeDtypeStruct((rows, full)...  188 us
    pallas_call x1, Pallas kernels, causal(): pl.pallas_call(causal_kernel, out_shape=(jax.ShapeDtypeStruct((total_rows...  79.4 us
    pallas_call x1, Pallas kernels, scatter_terms(): pl.pallas_call(scatter_kernel, out_shape=jax.ShapeDtypeStruct((BLK, full)...  44 us
    psum x1, waiting for transfers between devices, shards(): grads = lax.psum(local_grads, 'dp').astype(F32)  11.8 us
  transfers between devices with their start and end apart: 1, of which 1 were waited for; matrix products, arithmetic and copies ran while one was open for 0% of the time, Pallas kernels for 14%

profile of v4, /device:TPU:0, one launch (start us, length us, event | category | flops | bytes accessed | tf_op | source)
XLA Modules:
  0.0 355.5 jit_solution(8168445549251360625)
XLA Ops:
  7.2 0.0 copy-start.1
  7.2 0.0 all-reduce.2.cloned.1.call-start
  7.2 0.7 and_select_fusion.1.kept_shard
  7.9 0.7 fusion.1
  8.6 0.9 compare_reduce_fusion
  9.5 0.1 pad_add_fusion.1
  9.6 0.1 constant_dynamic-slice_fusion
  9.7 0.1 copy.20
  9.8 0.6 reshape.176.sel
  10.4 1.5 slice_bitcast_fusion.2
  11.8 0.1 copy.21
  11.9 0.7 reshape.178.sel
  12.6 0.0 copy-done.1
  12.6 0.7 convert_reduce_fusion.kept_at
  13.3 1.3 pad_maximum_fusion.weights
  14.6 0.0 copy-done.2
  14.6 188.2 %front.1 = (bf16[256,2048]{1,0:T(8,128)(2,1)}, bf16[8,2048,256]{2,1,0:T(8,128)(2,1)}, bf16[2048,384]{1,0:T(8,128)(2,1)}, f32[1,2048]{1,0:T(1,128)}) custom-call(s32[16]{0:T(128)} %copy-done.2, s32[16]{0:T(128)} %convert_reduce_fusion.kept_at, s32[6]{0:T(128)} %reshape.176.sel, bf16[4,128,2048]{2,1,0:T(8,128)(2,1)} %bitcast.30, bf16[512,2048]{1,0:T(8,128)(2,1)} %bitcast.32, ...), custom_call_target="tpu_custom_call" | custom-call | tf_op jit(solution)/shard_map/front/pallas_call | solution.py:457
  202.8 0.0 copy-start.3
  202.8 79.4 %causal.1 = (bf16[2048,128]{1,0:T(8,128)(2,1)}, bf16[2048,384]{1,0:T(8,128)(2,1)}, bf16[3,2048,128]{2,1,0:T(8,128)(2,1)}, bf16[256,2048]{1,0:T(8,128)(2,1)}) custom-call(s32[16]{0:T(128)} %bitcast.43, s32[6]{0:T(128)} %reshape.178.sel, bf16[2048,384]{1,0:T(8,128)(2,1)} %get-tuple-element.15.qkv, f32[1,2048]{1,0:T(1,128)} %get-tuple-element.16.scale, ...), custom_call_target="tpu_custom_call" | custom-call | flops 20000000000 | bytes 33554432 | tf_op jit(solution)/shard_map/causal/pallas_call | solution.py:613
  282.2 0.0 all-reduce.2.cloned.1.call-update
  282.2 0.2 dynamic-slice_reduce_fusion
  282.5 0.1 copy.19
  282.5 0.1 reshape.175
  282.6 0.0 copy-done.3
  282.6 0.6 select_reduce_fusion.slot_at
  283.3 44.0 %scatter_terms.1 = bf16[128,2048]{1,0:T(8,128)(2,1)} custom-call(s32[16]{0:T(128)} %select_reduce_fusion.slot_at, bf16[16,128,384]{2,1,0:T(8,128)(2,1)} %bitcast.46, bf16[2048,384]{1,0:T(8,128)(2,1)} %pad_maximum_fusion.weights), custom_call_target="tpu_custom_call" | custom-call | flops 3221225472 | bytes 104857600 | tf_op jit(solution)/shard_map/scatter_terms/pallas_call | solution.py:787
  327.3 0.6 pad_add_fusion.2.table
  327.8 5.0 %assemble.1 = (bf16[512,2048]{1,0:T(8,128)(2,1)}, bf16[2048,128]{1,0:T(8,128)(2,1)}) custom-call(s32[28]{0:T(128)} %pad_add_fusion.2.table, bf16[256,2048]{1,0:T(8,128)(2,1)} %get-tuple-element.14.head, bf16[256,2048]{1,0:T(8,128)(2,1)} %get-tuple-element.18.rest, bf16[2048,128]{1,0:T(8,128)(2,1)} %get-tuple-element.19.sorted_out), custom_call_target="tpu_custom_call" | custom-call | tf_op jit(solution)/shard_map/assemble/pallas_call | solution.py:835
  332.9 11.8 %all-reduce.2.cloned.1.call-done = bf16[3,2048,128]{2,1,0:T(8,128)(2,1)} async-done(((bf16[3,2048,128]{2,1,0:T(8,128)(2,1)}), bf16[3,2048,128]{2,1,0:T(8,128)(2,1)}) %all-reduce.2.cloned.1.call-update) | async-done | bytes 1572880 | tf_op jit(solution)/shard_map/psum | solution.py:901
  344.6 3.3 convert_element_type.26
  347.9 0.0 copy-done
  347.9 0.8 copy.24
  (10 shorter events, 0.1 us)
Async XLA Ops:
  7.2 5.4 %copy-start.1 = (s32[1,16]{1,0:T(1,128)S(1)}, s32[1,16]{1,0:T(1,128)}, u32[]{:S(2)}) copy-start(s32[1,16]{1,0:T(1,128)} %param.10) | copy-start | bytes 196
  7.2 337.4 %all-reduce.2.cloned.1.call-start = ((), (), s32[]{:S(2)}) async-start(), calls=%async_computation | async-start | bytes 3145728 | tf_op jit(solution)/shard_map/psum | solution.py:901
  7.9 6.7 %copy-start.2 = (s32[16]{0:T(128)}, s32[16]{0:T(128)S(1)}, u32[]{:S(2)}) copy-start(s32[16]{0:T(128)S(1)} %and_select_fusion.1.kept_shard) | copy-start | bytes 196
  202.8 79.9 %copy-start.3 = (s32[1,16]{1,0:T(1,128)S(1)}, s32[1,16]{1,0:T(1,128)}, u32[]{:S(2)}) copy-start(s32[1,16]{1,0:T(1,128)} %param.11) | copy-start | bytes 196
  332.9 15.0 %copy-start = (bf16[128,2048]{1,0:T(8,128)(2,1)S(1)}, bf16[128,2048]{1,0:T(8,128)(2,1)}, u32[]{:S(2)}) copy-start(bf16[128,2048]{1,0:T(8,128)(2,1)} %scatter_terms.1) | copy-start | bytes 1572868
Sparse Core Ops, SparseCore 0:
  282.3 62.2 all-reduce.1

commit v5 on v4

--- a/solution.py
+++ b/solution.py
@@ -231,122 +231,109 @@
 
 class Spread:
     OFFSETS = (0, 1, SIDE - 1, 2)
+    MESSAGES = 20
 
     def __init__(self, got, send_sem, recv_sem):
         self.got, self.send_sem, self.recv_sem = got, send_sem, recv_sem
         shard = lax.axis_index(SEQ)
-        self.row, self.col = shard // SIDE, lax.rem(shard, SIDE)
+        row, col = shard // SIDE, lax.rem(shard, SIDE)
+        self.here = ((col, row), (row, col))
 
     @staticmethod
     def turn(at, by):
         return lax.rem(at + by + SIDE, SIDE)
 
+    @staticmethod
+    def slot(kind, place):
+        a, b = place
+        return b * SIDE + a if kind == 0 else a * SIDE + b
+
     def neighbours(self):
-        return [self.row * SIDE + self.turn(self.col, by) for by in (1, -1)] + [
-            self.turn(self.row, by) * SIDE + self.col for by in (1, -1)
+        a, b = self.here[0]
+        return [self.slot(0, (self.turn(a, by), b)) for by in (1, -1)] + [
+            self.slot(0, (a, self.turn(b, by))) for by in (1, -1)
         ]
 
-    def places(self, c):
-        rows_first = (c >= 3) & (lax.rem(c, 2) == 1)
-        return rows_first, jnp.where(rows_first, self.row, self.col), jnp.where(rows_first, self.col, self.row)
-
-    def message(self, c, which, place, half, target):
-        rows_first, _, _ = self.places(c)
-        a, b = place
-        ta, tb = target
-        slot = jnp.where(rows_first, a * SIDE + b, b * SIDE + a)
-        device = jnp.where(rows_first, ta * SIDE + tb, tb * SIDE + ta)
-        ref = self.got.at[c, slot] if half is None else self.got.at[c, slot, half]
+    def message(self, c, kind, which, place, half, target):
+        slot = self.slot(kind, place)
+        ref = self.got.at[c, kind, slot] if half is None else self.got.at[c, kind, slot, half]
+        at = kind * self.MESSAGES + which
         return pltpu.make_async_remote_copy(
-            src_ref=ref, dst_ref=ref, send_sem=self.send_sem.at[c, which], recv_sem=self.recv_sem.at[c, which],
-            device_id={SEQ: device}, device_id_type=MESH,
-        )
-
-    def ring(self, c, base, near):
-        here, up, down, far = near(0), near(1), near(-1), near(2)
-        direct = (
-            self.message(c, base, here, None, up), self.message(c, base + 1, here, None, down),
-        )
-        direct_in = (
-            self.message(c, base, down, None, up), self.message(c, base + 1, up, None, down),
-        )
-        half = (
-            self.message(c, base + 2, down, 0, up), self.message(c, base + 3, up, 1, down),
-        )
-        half_in = (
-            self.message(c, base + 2, far, 0, up), self.message(c, base + 3, far, 1, down),
-        )
-        return direct, direct_in, half, half_in
-
-    def first_ring(self, c):
-        _, a, b = self.places(c)
-        return self.ring(c, 0, lambda by: (self.turn(a, by), b))
-
-    def second_ring(self, c, k):
-        _, a, b = self.places(c)
+            src_ref=ref, dst_ref=ref, send_sem=self.send_sem.at[c, at], recv_sem=self.recv_sem.at[c, at],
+            device_id={SEQ: self.slot(kind, target)}, device_id_type=MESH,
+        )
+
+    def first(self, c, kind, what):
+        a, b = self.here[kind]
+        up, down = (self.turn(a, 1), b), (self.turn(a, -1), b)
+        return self.four(c, kind, 0, (a, b), up, down, (self.turn(a, 2), b), up, down, what)
+
+    def second(self, c, kind, k, what):
+        a, b = self.here[kind]
         origin = self.turn(a, self.OFFSETS[k])
-        direct, direct_in, half, half_in = self.ring(c, 4 + 4 * k, lambda by: (origin, self.turn(b, by)))
-        return direct, direct_in, half, half_in
-
-    def second_sends(self, c, k):
-        _, a, b = self.places(c)
-        origin = self.turn(a, self.OFFSETS[k])
-        up, down = (a, self.turn(b, 1)), (a, self.turn(b, -1))
-        base = 4 + 4 * k
-        direct = (
-            self.message(c, base, (origin, b), None, up), self.message(c, base + 1, (origin, b), None, down),
-        )
-        half = (
-            self.message(c, base + 2, (origin, self.turn(b, -1)), 0, up),
-            self.message(c, base + 3, (origin, self.turn(b, 1)), 1, down),
-        )
-        return direct, half
+        return self.four(
+            c, kind, 4 + 4 * k, (origin, b), (origin, self.turn(b, 1)), (origin, self.turn(b, -1)),
+            (origin, self.turn(b, 2)), (a, self.turn(b, 1)), (a, self.turn(b, -1)), what,
+        )
+
+    def four(self, c, kind, base, here, up, down, far, to_up, to_down, what):
+        pairs = {
+            "send": ((base, here, None, to_up), (base + 1, here, None, to_down)),
+            "came": ((base, down, None, to_up), (base + 1, up, None, to_down)),
+            "pass": ((base + 2, down, 0, to_up), (base + 3, up, 1, to_down)),
+            "last": ((base + 2, far, 0, to_up), (base + 3, far, 1, to_down)),
+        }[what]
+        return [self.message(c, kind, *pair) for pair in pairs]
 
     def launch(self, c):
-        for each in self.first_ring(c)[0]:
-            each.start()
+        for kind in range(2):
+            for each in self.first(c, kind, "send"):
+                each.start()
 
     def relay(self, c):
-        _, direct_in, half, _ = self.first_ring(c)
-        for each in direct_in:
-            each.wait_recv()
-        for each in half:
-            each.start()
-        for k in range(3):
-            for each in self.second_sends(c, k)[0]:
+        for kind in range(2):
+            for each in self.first(c, kind, "came"):
+                each.wait_recv()
+            for each in self.first(c, kind, "pass"):
                 each.start()
+            for k in range(3):
+                for each in self.second(c, kind, k, "send"):
+                    each.start()
 
     def relay_far(self, c):
-        for each in self.first_ring(c)[3]:
-            each.wait_recv()
-        for each in self.second_sends(c, 3)[0]:
-            each.start()
+        for kind in range(2):
+            for each in self.first(c, kind, "last"):
+                each.wait_recv()
+            for each in self.second(c, kind, 3, "send"):
+                each.start()
 
     def second_relay(self, c):
         for k in range(4):
-            for each in self.second_ring(c, k)[1]:
-                each.wait_recv()
-            for each in self.second_sends(c, k)[1]:
-                each.start()
+            for kind in range(2):
+                for each in self.second(c, kind, k, "came"):
+                    each.wait_recv()
+                for each in self.second(c, kind, k, "pass"):
+                    each.start()
 
     def settle(self, c):
         for k in range(4):
-            for each in self.second_ring(c, k)[3]:
-                each.wait_recv()
+            for kind in range(2):
+                for each in self.second(c, kind, k, "last"):
+                    each.wait_recv()
 
     def drain(self, c):
-        direct, _, half, _ = self.first_ring(c)
-        for each in direct + half:
-            each.wait_send()
-        for k in range(4):
-            direct, half = self.second_sends(c, k)
-            for each in direct + half:
-                each.wait_send()
+        for kind in range(2):
+            for what in ("send", "pass"):
+                for each in self.first(c, kind, what):
+                    each.wait_send()
+                for k in range(4):
+                    for each in self.second(c, kind, k, what):
+                        each.wait_send()
 
 
 def front_kernel(
-    kept_shard, kept_at, sel, q_in, k_in, v_in, weights, out, rows_out, projected, scale_out,
-    got, held, staged, staged_sem, total, squares, spread_send, spread_recv, *scratch,
+    kept_shard, kept_at, sel, q_in, k_in, v_in, three, out, rows_out, projected, scale_out,
+    weights, got, held, staged, staged_sem, total, squares, spread_send, spread_recv, *scratch,
 ):
     kept = kept_shard.shape[0]
     flow = Flow(sel, q_in, k_in, v_in, out, scratch)
@@ -359,10 +346,12 @@
     def store(c, h, value):
         out[:, flow.cols(c, h)] = value
         for a in range(flow.rows // BLK):
-            got[c, flow.shard, a, :, flow.head(h)] = value[a * BLK : (a + 1) * BLK, :]
+            got[c, h, flow.shard, a] = value[a * BLK : (a + 1) * BLK, :]
 
     flow.store = store
     flow.begin(3, spread.neighbours())
+    for which in range(3):
+        weights[:, which * HEAD : (which + 1) * HEAD] = three[which]
     total[...] = jnp.zeros_like(total)
     squares[...] = jnp.zeros_like(squares)
 
@@ -378,7 +367,8 @@
             staged_copy(c - 2).wait()
 
         def hold(i, carry):
-            held[i] = got[c, i]
+            for h in range(flow.per_chunk):
+                held[i, :, :, flow.head(h)] = got[c, h, i]
             return carry
 
         lax.fori_loop(0, SIDE * SIDE, hold, 0)
@@ -447,7 +437,7 @@
 
 def front(kept_shard, kept_at, sel, query, key, value, weights, per_chunk, ident):
     tok, full = key.shape
-    local = weights.shape[1]
+    local = 3 * HEAD
     rows = sel.shape[0] // 3 * BLK
     total_rows = kept_shard.shape[0] * BLK
     width = per_chunk * HEAD
@@ -465,14 +455,15 @@
         in_specs=[smem, smem, smem, vmem, vmem, vmem, vmem],
         out_specs=[vmem, pl.BlockSpec(memory_space=pl.ANY), vmem, vmem],
         scratch_shapes=[
-            pltpu.VMEM((chunks, SIDE * SIDE, rows // BLK, BLK, width), BF16),
+            pltpu.VMEM((full, local), BF16),
+            pltpu.VMEM((chunks, 2, SIDE * SIDE, rows // BLK, BLK, HEAD), BF16),
             pltpu.VMEM((SIDE * SIDE, rows // BLK, BLK, width), BF16),
             pltpu.VMEM((2, total_rows, width), BF16),
             pltpu.SemaphoreType.DMA((2,)),
             pltpu.VMEM((total_rows, local), F32),
             pltpu.VMEM((total_rows, HEAD), F32),
-            pltpu.SemaphoreType.DMA((chunks, 20)),
-            pltpu.SemaphoreType.DMA((chunks, 20)),
+            pltpu.SemaphoreType.DMA((chunks, 2 * Spread.MESSAGES)),
+            pltpu.SemaphoreType.DMA((chunks, 2 * Spread.MESSAGES)),
             *Flow.scratch(rows, tok, full, per_chunk),
         ],
         compiler_params=pltpu.CompilerParams(
@@ -644,9 +635,118 @@
     )(dest, sel, qkv, scale, cot, gathered, query, key, value)
 
 
+class Reduce:
+    def __init__(self, value, pair_got, own, snd, got1, got2, whole, send_sem, recv_sem):
+        self.value, self.pair_got, self.own, self.snd = value, pair_got, own, snd
+        self.got1, self.got2, self.whole = got1, got2, whole
+        self.send_sem, self.recv_sem = send_sem, recv_sem
+        at = lax.axis_index("dp")
+        self.y, self.core = at // 2, lax.rem(at, 2)
+        self.partner = self.y * 2 + 1 - self.core
+        self.next = [self.turn(by) * 2 + self.core for by in (1, -1)]
+        middle = value.shape[3] // 2
+        self.halves = (slice(0, middle), slice(middle, 2 * middle))
+
+    def turn(self, by):
+        return lax.rem(self.y + by + SIDE, SIDE)
+
+    def copy(self, which, src, dst, target):
+        return pltpu.make_async_remote_copy(
+            src_ref=src, dst_ref=dst, send_sem=self.send_sem.at[which], recv_sem=self.recv_sem.at[which],
+            device_id={"dp": target}, device_id_type=MESH,
+        )
+
+    def pair(self):
+        return self.copy(0, self.value.at[:, 1 - self.core], self.pair_got, self.partner)
+
+    def ring1(self, d):
+        return self.copy(1 + d, self.snd.at[d, 0, :, self.halves[0]], self.got1.at[d], self.next[d])
+
+    def ring2(self, d):
+        return self.copy(3 + d, self.snd.at[d, 1], self.got2.at[d], self.next[d])
+
+    def quarter(self, by, half=None):
+        ref = self.whole.at[:, self.core, self.turn(by)]
+        return ref if half is None else self.whole.at[:, self.core, self.turn(by), self.halves[half]]
+
+    def spread1(self, d, by):
+        return self.copy(5 + d, self.quarter(by), self.quarter(by), self.next[d])
+
+    def spread2(self, d, by):
+        return self.copy(7 + d, self.quarter(by, d), self.quarter(by, d), self.next[d])
+
+    def back(self, core):
+        return self.copy(9, self.whole.at[:, core], self.whole.at[:, core], self.partner)
+
+    def stage1(self):
+        self.pair().wait_recv()
+
+        def add(q, carry):
+            self.own[q] = self.value[:, self.core, q].astype(F32) + self.pair_got[:, q].astype(F32)
+            return carry
+
+        lax.fori_loop(0, SIDE, add, 0)
+        for d in range(2):
+            self.snd[d, 0, :, self.halves[0]] = self.own[self.turn(2), :, self.halves[d]].astype(BF16)
+            self.ring1(d).start()
+
+    def stage2(self):
+        for d in range(2):
+            self.ring1(d).wait_recv()
+            near = self.turn(1 - 2 * d)
+            self.snd[d, 1, :, self.halves[1 - d]] = self.own[near, :, self.halves[1 - d]].astype(BF16)
+            self.snd[d, 1, :, self.halves[d]] = (
+                self.own[near, :, self.halves[d]] + self.got1[d].astype(F32)
+            ).astype(BF16)
+            self.ring2(d).start()
+
+    def stage3(self):
+        for d in range(2):
+            self.ring2(d).wait_recv()
+        total = self.own[self.y] + self.got2[0].astype(F32) + self.got2[1].astype(F32)
+        self.whole[:, self.core, self.y] = total.astype(BF16)
+        for d in range(2):
+            self.spread1(d, 0).start()
+
+    def stage4(self):
+        for d in range(2):
+            self.spread1(d, 2 * d - 1).wait_recv()
+            self.spread2(d, 2 * d - 1).start()
+
+    def stage5(self):
+        for d in range(2):
+            self.spread2(d, 2).wait_recv()
+        self.back(self.core).start()
+
+    def stage6(self, out):
+        self.back(1 - self.core).wait_recv()
+        out[...] = self.whole[...]
+        self.pair().wait_send()
+        for d in range(2):
+            self.ring1(d).wait_send()
+            self.ring2(d).wait_send()
+            self.spread1(d, 0).wait_send()
+            self.spread2(d, 2 * d - 1).wait_send()
+        self.back(self.core).wait_send()
+
+    @staticmethod
+    def scratch(shape):
+        three, _, quarters, rows, width = shape
+        return [
+            pltpu.VMEM((three, quarters, rows, width), BF16),
+            pltpu.VMEM((quarters, three, rows, width), F32),
+            pltpu.VMEM((2, 2, three, rows, width), BF16),
+            pltpu.VMEM((2, three, rows // 2, width), BF16),
+            pltpu.VMEM((2, three, rows, width), BF16),
+            pltpu.VMEM(shape, BF16),
+            pltpu.SemaphoreType.DMA((10,)),
+            pltpu.SemaphoreType.DMA((10,)),
+        ]
+
+
 def scatter_kernel(
-    slot_at, d_all, weights, out, terms, got1, snd2, got2, sums, last1, lasts2, last2,
-    send1, recv1, send2, recv2, send3, recv3, send4, recv4,
+    slot_at, d_all, three, value, out, summed, weights, terms, got1, snd2, got2, sums, last1, lasts2, last2,
+    send1, recv1, send2, recv2, send3, recv3, send4, recv4, *reduce_scratch,
 ):
     shard = lax.axis_index(SEQ)
     row, col = shard // SIDE, lax.rem(shard, SIDE)
@@ -668,6 +768,11 @@
             pl.semaphore_signal(
                 barrier, inc=1, device_id={SEQ: slot(h, turn(a, by), b)}, device_id_type=MESH
             )
+    reduce = Reduce(value, *reduce_scratch)
+    for target in (reduce.partner, *reduce.next):
+        pl.semaphore_signal(barrier, inc=1, device_id={"dp": target}, device_id_type=MESH)
+    for which in range(3):
+        weights[:, which * HEAD : (which + 1) * HEAD] = three[which]
 
     def group(h, a):
         slots = [jnp.where(h == 0, a * SIDE + s, s * SIDE + a) for s in range(SIDE)]
@@ -720,13 +825,15 @@
         return carry
 
     lax.fori_loop(0, 2, group_far, 0)
-    pl.semaphore_wait(barrier, 4)
+    pl.semaphore_wait(barrier, 7)
+    reduce.pair().start()
     for k in (2, 1, 3, 0):
         for h in range(2):
             s = turn(place[h][1], k)
             for d in range(2):
                 first_send(h, d, s).start()
     lax.fori_loop(0, 6, group_rest, 0)
+    reduce.stage1()
     for k in (2, 1, 3, 0):
         for h in range(2):
             a, b = place[h]
@@ -740,6 +847,7 @@
                     terms[h, near, s, :, halves[d]].astype(F32) + got1[h, d, s].astype(F32)
                 ).astype(BF16)
                 second_send(h, d, s).start()
+    reduce.stage2()
     for k in (2, 1, 3, 0):
         for h in range(2):
             a, b = place[h]
@@ -767,6 +875,13 @@
                 out[:, h * wide : (h + 1) * wide] = (
                     total + last2[h, 0].astype(F32) + last2[h, 1].astype(F32)
                 ).astype(BF16)
+        if k == 2:
+            reduce.stage3()
+        elif k == 1:
+            reduce.stage4()
+        elif k == 3:
+            reduce.stage5()
+    reduce.stage6(summed)
     for h in range(2):
         for d in range(2):
             for s in range(SIDE):
@@ -776,9 +891,9 @@
             fourth_send(h, d).wait_send()
 
 
-def scatter_terms(slot_at, d_all, weights, ident):
+def scatter_terms(slot_at, d_all, three, value, ident):
     blocks, _, local = d_all.shape
-    full = weights.shape[0]
+    full = three.shape[1]
     wide = full // 2
     part = wide // 2
     vmem = pl.BlockSpec(memory_space=pltpu.VMEM)
@@ -786,10 +901,11 @@
     two = pltpu.SemaphoreType.DMA((2, 2))
     return pl.pallas_call(
         scatter_kernel,
-        out_shape=jax.ShapeDtypeStruct((BLK, full), BF16),
-        in_specs=[pl.BlockSpec(memory_space=pltpu.SMEM), vmem, vmem],
-        out_specs=vmem,
+        out_shape=(jax.ShapeDtypeStruct((BLK, full), BF16), jax.ShapeDtypeStruct(value.shape, BF16)),
+        in_specs=[pl.BlockSpec(memory_space=pltpu.SMEM), vmem, vmem, vmem],
+        out_specs=[vmem, vmem],
         scratch_shapes=[
+            pltpu.VMEM((full, local), BF16),
             pltpu.VMEM((2, SIDE, SIDE, BLK, wide), BF16),
             pltpu.VMEM((2, 2, SIDE, BLK, part), BF16),
             pltpu.VMEM((2, 2, SIDE, BLK, wide), BF16),
@@ -799,6 +915,7 @@
             pltpu.VMEM((2, 2, BLK, wide), BF16),
             pltpu.VMEM((2, 2, BLK, wide), BF16),
             four, four, four, four, two, two, two, two,
+            *Reduce.scratch(value.shape),
         ],
         compiler_params=pltpu.CompilerParams(
             collective_id=ident, has_side_effects=True, vmem_limit_bytes=VMEM_LIMIT
@@ -807,7 +924,7 @@
             flops=2 * blocks * BLK * local * full, bytes_accessed=100 * 1024 * 1024, transcendentals=0
         ),
         name="scatter_terms",
-    )(slot_at, d_all, weights)
+    )(slot_at, d_all, three, value)
 
 
 def assemble_kernel(table, head, rest, sorted_out, out, causal_out):
@@ -885,7 +1002,6 @@
     table = jnp.stack([in_first, at * in_first, at * (1 - in_first)], axis=1).reshape(-1)
     keep_shard = keep // per_shard
     before = jnp.sum((keep_shard[None, :] == keep_shard[:, None]) & (keep[None, :] < keep[:, None]), axis=1)
-    weights = jnp.concatenate([proj_weights[0], proj_weights[1], proj_weights[2]], axis=1)
 
     slot_at = jnp.sum(
         jnp.where(dest[None, :] == jnp.arange(dest.shape[0])[:, None], jnp.arange(dest.shape[0])[None, :], 0),
@@ -893,14 +1009,17 @@
     ).astype(jnp.int32)
 
     first, gathered, qkv, scale = front(
-        keep_shard.astype(jnp.int32), before.astype(jnp.int32), sel_first, query, key, value, weights, 2, 0
+        keep_shard.astype(jnp.int32), before.astype(jnp.int32), sel_first, query, key, value, proj_weights, 2, 0
     )
     sorted_out, d_all, local_grads, rest = causal(
         dest, sel_rest, qkv, scale, cotangent.reshape(dest.shape[0], BLK, -1), gathered, query, key, value, 2, 1
     )
-    grads = lax.psum(local_grads, "dp").astype(F32)
     window_out, causal_out = assemble(jnp.concatenate([dest, table]), first, rest, sorted_out)
-    row_grad = scatter_terms(slot_at, d_all.reshape(dest.shape[0], BLK, -1), weights, 2)
+    row_grad, grads = scatter_terms(
+        slot_at, d_all.reshape(dest.shape[0], BLK, -1), proj_weights,
+        local_grads.reshape(3, 2, SIDE, full // 2 // SIDE, HEAD), 2,
+    )
+    grads = grads.reshape(proj_weights.shape).astype(F32)
     return (window_out[None], causal_out[None], grads, row_grad[None])
 
 

time: 356 us -> 328 us (0.921)
  between operations: 14.1 us -> 0.72 us
  waiting for transfers between devices: 11.8 us -> 0 us
    pallas_call x1, Pallas kernels: 188 us -> 174 us  [front(): pl.pallas_call(front_kernel, out_shape=(jax.ShapeDtypeStruct((rows, full)...]
    psum x1 -> x0, waiting for transfers between devices: 11.8 us -> none  [shards(): grads = lax.psum(local_grads, 'dp').astype(F32)]
    pallas_call x1, Pallas kernels: 44 us -> 53.7 us  [scatter_terms(): pl.pallas_call(scatter_kernel, out_shape=(jax.ShapeDtypeStruct((BLK, full...]
  transfers between devices with their start and end apart: 1 -> 0, of which waited for: 1 -> 0; matrix products, arithmetic and copies ran while one was open for 0% -> 0% of each run, Pallas kernels for 14% -> 0%
where the time goes in v5:
time: 328 us; the launch traced here: 326 us
  Pallas kernels  314 us (96%)
  other arithmetic  8.98 us (3%)
    pallas_call x1, Pallas kernels, front(): pl.pallas_call(front_kernel, out_shape=(jax.ShapeDtypeStruct((rows, full)...  174 us
    pallas_call x1, Pallas kernels, causal(): pl.pallas_call(causal_kernel, out_shape=(jax.ShapeDtypeStruct((total_rows...  80.7 us
    pallas_call x1, Pallas kernels, scatter_terms(): pl.pallas_call(scatter_kernel, out_shape=(jax.ShapeDtypeStruct((BLK, full...  53.7 us

profile of v5, /device:TPU:0, one launch (start us, length us, event | category | flops | bytes accessed | tf_op | source)
XLA Modules:
  0.0 326.3 jit_solution(789926573712293063)
XLA Ops:
  0.6 0.9 compare_reduce_fusion
  1.6 0.2 dynamic-slice_reduce_fusion
  1.8 0.1 copy.19
  1.9 0.1 reshape.181
  2.0 1.2 pad_add_fusion.2.table
  3.2 0.7 and_select_fusion.1.kept_shard
  3.9 0.0 copy-start.1
  3.9 0.7 fusion.1
  4.5 1.4 convert_reduce_fusion.kept_at
  6.0 0.1 pad_add_fusion.1
  6.1 0.1 constant_dynamic-slice_fusion
  6.1 0.1 copy.20
  6.2 0.6 reshape.182.sel
  6.8 0.0 copy-done.1
  6.8 174.4 %front.1 = (bf16[256,2048]{1,0:T(8,128)(2,1)}, bf16[8,2048,256]{2,1,0:T(8,128)(2,1)}, bf16[2048,384]{1,0:T(8,128)(2,1)}, f32[1,2048]{1,0:T(1,128)}) custom-call(s32[16]{0:T(128)} %copy-done.1, s32[16]{0:T(128)} %convert_reduce_fusion.kept_at, s32[6]{0:T(128)} %reshape.182.sel, bf16[4,128,2048]{2,1,0:T(8,128)(2,1)} %bitcast.28, bf16[512,2048]{1,0:T(8,128)(2,1)} %bitcast.30, ...), custom_call_target="tpu_custom_call" | custom-call | tf_op jit(solution)/shard_map/front/pallas_call | solution.py:447
  181.2 0.1 copy.21
  181.3 0.6 reshape.184.sel
  181.9 80.7 %causal.1 = (bf16[2048,128]{1,0:T(8,128)(2,1)}, bf16[2048,384]{1,0:T(8,128)(2,1)}, bf16[3,2048,128]{2,1,0:T(8,128)(2,1)}, bf16[256,2048]{1,0:T(8,128)(2,1)}) custom-call(s32[16]{0:T(128)} %bitcast.42, s32[6]{0:T(128)} %reshape.184.sel, bf16[2048,384]{1,0:T(8,128)(2,1)} %get-tuple-element.17.qkv, f32[1,2048]{1,0:T(1,128)} %get-tuple-element.18.scale, ...), custom_call_target="tpu_custom_call" | custom-call | flops 20000000000 | bytes 33554432 | tf_op jit(solution)/shard_map/causal/pallas_call | solution.py:604
  262.6 0.0 copy-start.2
  262.7 5.1 %assemble.1 = (bf16[512,2048]{1,0:T(8,128)(2,1)}, bf16[2048,128]{1,0:T(8,128)(2,1)}) custom-call(s32[28]{0:T(128)} %pad_add_fusion.2.table, bf16[256,2048]{1,0:T(8,128)(2,1)} %get-tuple-element.16.head, bf16[256,2048]{1,0:T(8,128)(2,1)} %get-tuple-element.20.rest, bf16[2048,128]{1,0:T(8,128)(2,1)} %get-tuple-element.21.sorted_out), custom_call_target="tpu_custom_call" | custom-call | tf_op jit(solution)/shard_map/assemble/pallas_call | solution.py:952
  267.8 0.0 copy-done.2
  267.8 0.6 select_reduce_fusion.slot_at
  268.4 53.7 %scatter_terms.1 = (bf16[128,2048]{1,0:T(8,128)(2,1)}, bf16[3,2,4,256,128]{4,3,2,1,0:T(8,128)(2,1)}) custom-call(s32[16]{0:T(128)} %select_reduce_fusion.slot_at, bf16[16,128,384]{2,1,0:T(8,128)(2,1)} %bitcast.44, bf16[3,2048,128]{2,1,0:T(8,128)(2,1)} %three.3, bf16[3,2,4,256,128]{4,3,2,1,0:T(8,128)(2,1)} %bitcast.45), custom_call_target="tpu_custom_call" | custom-call | flops 3221225472 | bytes 104857600 | tf_op jit(solution)/shard_map/scatter_terms/pallas_call | solution.py:902
  322.1 0.0 copy-start
  322.1 3.3 %bitcast_convert_fusion = f32[3,2048,128]{2,1,0:T(8,128)} fusion(bf16[3,2,4,256,128]{4,3,2,1,0:T(8,128)(2,1)} %get-tuple-element.26), kind=kLoop, calls=%fused_computation | loop fusion | flops 786432 | bytes 4718592 | tf_op jit(solution)/shard_map/convert_element_type | solution.py:1022
  325.5 0.0 copy-done
  325.5 0.8 copy.23
  (8 shorter events, 0.1 us)
Async XLA Ops:
  3.9 3.0 copy-start.1
  262.6 5.2 %copy-start.2 = (s32[1,16]{1,0:T(1,128)S(1)}, s32[1,16]{1,0:T(1,128)}, u32[]{:S(2)}) copy-start(s32[1,16]{1,0:T(1,128)} %param.11) | copy-start | bytes 196
  322.1 3.3 %copy-start = (bf16[128,2048]{1,0:T(8,128)(2,1)S(1)}, bf16[128,2048]{1,0:T(8,128)(2,1)}, u32[]{:S(2)}) copy-start(bf16[128,2048]{1,0:T(8,128)(2,1)} %get-tuple-element.27) | copy-start | bytes 1572868

commit v6 on v5

--- a/solution.py
+++ b/solution.py
@@ -394,23 +394,21 @@
         lax.fori_loop(0, total_rows // block, multiply, 0)
 
     def step(t, carry):
-        flow.step(t)
-
-        def stage(late, call):
+        def stage(late, *calls):
             @pl.when((t >= late) & (t < chunks + late))
             def _():
-                call(t - late)
-
-        stage(3, spread.launch)
+                for call in calls:
+                    call(t - late)
+
+        stage(0, flow.pump)
         stage(4, spread.relay)
+        stage(0, flow.own)
         stage(5, spread.relay_far)
+        stage(1, flow.two)
+        stage(2, flow.one)
         stage(6, spread.second_relay)
-
-        @pl.when(t >= 7)
-        def _():
-            spread.settle(t - 7)
-            project_chunk(t - 7)
-
+        stage(3, flow.final, spread.launch)
+        stage(7, spread.settle, project_chunk)
         return carry
 
     lax.fori_loop(0, chunks + 7, step, 0)
@@ -487,7 +485,7 @@
     rows_copy = pltpu.make_async_copy(gathered, rows_in, rows_sem)
     rows_copy.start()
     flow = Flow(sel, q_in, k_in, v_in, rest, scratch)
-    flow.begin(3)
+    flow.begin(4)
 
     for j in range(kept):
         do_own[j * BLK : (j + 1) * BLK, :] = cot[dest[j]]
@@ -571,27 +569,28 @@
 
     col_blocks = rows_in.shape[0]
     share = (col_blocks + 2) // 3
+    every = flow.chunks // blocks
 
     def step(t, carry):
         flow.step(t)
 
-        @pl.when(t < blocks)
+        @pl.when((t < flow.chunks) & (lax.rem(t, every) == 0))
         def _():
-            query_block(blocks - 1 - t)
-
-        @pl.when(t == blocks)
+            query_block(blocks - 1 - t // every)
+
+        @pl.when(t == flow.chunks)
         def _():
             lax.fori_loop(0, blocks, finish, 0)
             rows_copy.wait()
 
-        @pl.when(t >= blocks)
+        @pl.when(t >= flow.chunks)
         def _():
-            low = (t - blocks) * share
+            low = (t - flow.chunks) * share
             lax.fori_loop(low, jnp.minimum(low + share, col_blocks), weight_block, 0)
 
         return carry
 
-    lax.fori_loop(0, blocks + 3, step, 0)
+    lax.fori_loop(0, flow.chunks + 3, step, 0)
     flow.drain()
 
 
@@ -832,8 +831,10 @@
             s = turn(place[h][1], k)
             for d in range(2):
                 first_send(h, d, s).start()
-    lax.fori_loop(0, 6, group_rest, 0)
+    lax.fori_loop(0, 2, group_rest, 0)
     reduce.stage1()
+    lax.fori_loop(2, 6, group_rest, 0)
+    reduce.stage2()
     for k in (2, 1, 3, 0):
         for h in range(2):
             a, b = place[h]
@@ -847,7 +848,7 @@
                     terms[h, near, s, :, halves[d]].astype(F32) + got1[h, d, s].astype(F32)
                 ).astype(BF16)
                 second_send(h, d, s).start()
-    reduce.stage2()
+    reduce.stage3()
     for k in (2, 1, 3, 0):
         for h in range(2):
             a, b = place[h]
@@ -876,12 +877,11 @@
                     total + last2[h, 0].astype(F32) + last2[h, 1].astype(F32)
                 ).astype(BF16)
         if k == 2:
-            reduce.stage3()
+            reduce.stage4()
         elif k == 1:
-            reduce.stage4()
+            reduce.stage5()
         elif k == 3:
-            reduce.stage5()
-    reduce.stage6(summed)
+            reduce.stage6(summed)
     for h in range(2):
         for d in range(2):
             for s in range(SIDE):
@@ -1012,7 +1012,7 @@
         keep_shard.astype(jnp.int32), before.astype(jnp.int32), sel_first, query, key, value, proj_weights, 2, 0
     )
     sorted_out, d_all, local_grads, rest = causal(
-        dest, sel_rest, qkv, scale, cotangent.reshape(dest.shape[0], BLK, -1), gathered, query, key, value, 2, 1
+        dest, sel_rest, qkv, scale, cotangent.reshape(dest.shape[0], BLK, -1), gathered, query, key, value, 1, 1
     )
     window_out, causal_out = assemble(jnp.concatenate([dest, table]), first, rest, sorted_out)
     row_grad, grads = scatter_terms(

time: 328 us -> 349 us (1.064)
  Pallas kernels: 314 us -> 336 us
    pallas_call x1, Pallas kernels: 80.7 us -> 100 us  [causal(): pl.pallas_call(causal_kernel, out_shape=(jax.ShapeDtypeStruct((total_rows...]
    pallas_call x1, Pallas kernels: 174 us -> 180 us  [front(): pl.pallas_call(front_kernel, out_shape=(jax.ShapeDtypeStruct((rows, full)...]
where the time goes in v6:
time: 349 us
  Pallas kernels  336 us (96%)
  other arithmetic  8.98 us (3%)
    pallas_call x1, Pallas kernels, front(): pl.pallas_call(front_kernel, out_shape=(jax.ShapeDtypeStruct((rows, full)...  180 us
    pallas_call x1, Pallas kernels, causal(): pl.pallas_call(causal_kernel, out_shape=(jax.ShapeDtypeStruct((total_rows...  100 us
    pallas_call x1, Pallas kernels, scatter_terms(): pl.pallas_call(scatter_kernel, out_shape=(jax.ShapeDtypeStruct((BLK, full...  50.5 us

profile of v6, /device:TPU:0, one launch (start us, length us, event | category | flops | bytes accessed | tf_op | source)
XLA Modules:
  0.0 348.6 jit_solution(15306456006895621454)
XLA Ops:
  0.6 0.9 compare_reduce_fusion
  1.6 0.2 dynamic-slice_reduce_fusion
  1.8 0.1 copy.19
  1.9 0.1 reshape.181
  2.0 1.2 pad_add_fusion.2.table
  3.2 0.7 and_select_fusion.1.kept_shard
  3.9 0.0 copy-start.1
  3.9 0.7 fusion.1
  4.5 1.4 convert_reduce_fusion.kept_at
  6.0 0.1 pad_add_fusion.1
  6.1 0.1 constant_dynamic-slice_fusion
  6.1 0.1 copy.20
  6.2 0.6 reshape.182.sel
  6.8 0.0 copy-done.1
  6.8 180.4 %front.1 = (bf16[256,2048]{1,0:T(8,128)(2,1)}, bf16[8,2048,256]{2,1,0:T(8,128)(2,1)}, bf16[2048,384]{1,0:T(8,128)(2,1)}, f32[1,2048]{1,0:T(1,128)}) custom-call(s32[16]{0:T(128)} %copy-done.1, s32[16]{0:T(128)} %convert_reduce_fusion.kept_at, s32[6]{0:T(128)} %reshape.182.sel, bf16[4,128,2048]{2,1,0:T(8,128)(2,1)} %bitcast.28, bf16[512,2048]{1,0:T(8,128)(2,1)} %bitcast.30, ...), custom_call_target="tpu_custom_call" | custom-call | tf_op jit(solution)/shard_map/front/pallas_call | solution.py:445
  187.2 0.1 copy.21
  187.3 0.6 reshape.184.sel
  187.9 100.1 %causal.1 = (bf16[2048,128]{1,0:T(8,128)(2,1)}, bf16[2048,384]{1,0:T(8,128)(2,1)}, bf16[3,2048,128]{2,1,0:T(8,128)(2,1)}, bf16[256,2048]{1,0:T(8,128)(2,1)}) custom-call(s32[16]{0:T(128)} %bitcast.42, s32[6]{0:T(128)} %reshape.184.sel, bf16[2048,384]{1,0:T(8,128)(2,1)} %get-tuple-element.17.qkv, f32[1,2048]{1,0:T(1,128)} %get-tuple-element.18.scale, ...), custom_call_target="tpu_custom_call" | custom-call | flops 20000000000 | bytes 33554432 | tf_op jit(solution)/shard_map/causal/pallas_call | solution.py:603
  288.0 0.0 copy-start.2
  288.0 5.3 %assemble.1 = (bf16[512,2048]{1,0:T(8,128)(2,1)}, bf16[2048,128]{1,0:T(8,128)(2,1)}) custom-call(s32[28]{0:T(128)} %pad_add_fusion.2.table, bf16[256,2048]{1,0:T(8,128)(2,1)} %get-tuple-element.16.head, bf16[256,2048]{1,0:T(8,128)(2,1)} %get-tuple-element.20.rest, bf16[2048,128]{1,0:T(8,128)(2,1)} %get-tuple-element.21.sorted_out), custom_call_target="tpu_custom_call" | custom-call | tf_op jit(solution)/shard_map/assemble/pallas_call | solution.py:952
  293.3 0.0 copy-done.2
  293.3 0.6 select_reduce_fusion.slot_at
  293.9 50.5 %scatter_terms.1 = (bf16[128,2048]{1,0:T(8,128)(2,1)}, bf16[3,2,4,256,128]{4,3,2,1,0:T(8,128)(2,1)}) custom-call(s32[16]{0:T(128)} %select_reduce_fusion.slot_at, bf16[16,128,384]{2,1,0:T(8,128)(2,1)} %bitcast.44, bf16[3,2048,128]{2,1,0:T(8,128)(2,1)} %three.3, bf16[3,2,4,256,128]{4,3,2,1,0:T(8,128)(2,1)} %bitcast.45), custom_call_target="tpu_custom_call" | custom-call | flops 3221225472 | bytes 104857600 | tf_op jit(solution)/shard_map/scatter_terms/pallas_call | solution.py:902
  344.4 0.0 copy-start
  344.5 3.3 bitcast_convert_fusion
  347.8 0.0 copy-done
  347.8 0.8 copy.23
  (8 shorter events, 0.1 us)
Async XLA Ops:
  3.9 3.0 copy-start.1
  288.0 5.3 %copy-start.2 = (s32[1,16]{1,0:T(1,128)S(1)}, s32[1,16]{1,0:T(1,128)}, u32[]{:S(2)}) copy-start(s32[1,16]{1,0:T(1,128)} %param.11) | copy-start | bytes 196
  344.4 3.3 copy-start

commit v7 on v5

--- a/solution.py
+++ b/solution.py
@@ -38,6 +38,28 @@
     weight_b = jnp.exp2(lse_b - top)
     total = weight_a + weight_b
     return out_a * (weight_a / total) + out_b * (weight_b / total), top + jnp.log2(total)
+
+
+def block_ranks(keep, shard, per_shard):
+    kept = [
+        functools.reduce(
+            lambda found, j: jnp.where(keep[0, j] == shard * per_shard + b, 1, found), range(keep.shape[1]), 0
+        )
+        for b in range(per_shard)
+    ]
+    total = sum(kept)
+    return [
+        jnp.where(kept[b] == 1, sum(kept[:b], 0), total + b - sum(kept[:b], 0)) for b in range(per_shard)
+    ]
+
+
+def picked(ranks, places):
+    return [functools.reduce(lambda got, b: jnp.where(ranks[b] == at, b, got), range(len(ranks)), 0) for at in places]
+
+
+def near_ranks(keep, per_shard):
+    shard, count = lax.axis_index(SEQ), lax.axis_size(SEQ)
+    return [block_ranks(keep, lax.rem(shard + by, count), per_shard) for by in range(3)]
 
 
 class Flow:
@@ -183,23 +205,17 @@
     def store(self, c, h, value):
         self.out[:, self.cols(c, h)] = value
 
-    def step(self, t):
-        @pl.when(t < self.chunks)
-        def _():
-            self.pump(t)
-            self.own(t)
-
-        @pl.when((t >= 1) & (t <= self.chunks))
-        def _():
-            self.two(t - 1)
-
-        @pl.when((t >= 2) & (t <= self.chunks + 1))
-        def _():
-            self.one(t - 2)
-
-        @pl.when((t >= 3) & (t <= self.chunks + 2))
-        def _():
-            self.final(t - 3)
+    def step(self, t, lag):
+        def stage(late, *calls):
+            @pl.when((t >= late) & (t < self.chunks + late))
+            def _():
+                for call in calls:
+                    call(t - late)
+
+        stage(0, self.pump, self.own)
+        stage(lag, self.two)
+        stage(2 * lag, self.one)
+        stage(3 * lag, self.final)
 
     def drain(self):
         def body(c, carry):
@@ -332,21 +348,33 @@
 
 
 def front_kernel(
-    kept_shard, kept_at, sel, q_in, k_in, v_in, three, out, rows_out, projected, scale_out,
+    keep, q_in, k_in, v_in, three, out, rows_out, projected, scale_out, table,
     weights, got, held, staged, staged_sem, total, squares, spread_send, spread_recv, *scratch,
 ):
-    kept = kept_shard.shape[0]
+    kept = keep.shape[1]
+    per_shard = q_in.shape[0]
+    ranks = near_ranks(keep, per_shard)
+    half = per_shard // 2
+    sel = [at for each in ranks for at in picked(each, range(half))]
+    for b in range(per_shard):
+        late = jnp.where(ranks[0][b] >= half, 1, 0)
+        table[3 * b] = late
+        table[3 * b + 1] = ranks[0][b] * (1 - late)
+        table[3 * b + 2] = (ranks[0][b] - half) * late
+    owner = [keep[0, j] // per_shard for j in range(kept)]
+    nth = [0] + [jnp.where(owner[j] == owner[j - 1], 1, 0) for j in range(1, kept)]
     flow = Flow(sel, q_in, k_in, v_in, out, scratch)
     spread = Spread(got, spread_send, spread_recv)
     chunks, width = flow.chunks, flow.width
     total_rows, local = projected.shape
     full = k_in.shape[1]
     block = 512
+    per_kind = flow.per_chunk // 2
 
     def store(c, h, value):
         out[:, flow.cols(c, h)] = value
         for a in range(flow.rows // BLK):
-            got[c, h, flow.shard, a] = value[a * BLK : (a + 1) * BLK, :]
+            got[c, h // per_kind, flow.shard, a, :, flow.head(h % per_kind)] = value[a * BLK : (a + 1) * BLK, :]
 
     flow.store = store
     flow.begin(3, spread.neighbours())
@@ -367,18 +395,14 @@
             staged_copy(c - 2).wait()
 
         def hold(i, carry):
-            for h in range(flow.per_chunk):
-                held[i, :, :, flow.head(h)] = got[c, h, i]
+            for kind in range(2):
+                held[i, :, :, kind * width // 2 : (kind + 1) * width // 2] = got[c, kind, i]
             return carry
 
         lax.fori_loop(0, SIDE * SIDE, hold, 0)
 
-        def pick(j, carry):
-            at = pl.ds(pl.multiple_of(j * BLK, BLK), BLK)
-            staged[which, at, :] = held[kept_shard[j], kept_at[j]]
-            return carry
-
-        lax.fori_loop(0, kept, pick, 0)
+        for j in range(kept):
+            staged[which, j * BLK : (j + 1) * BLK, :] = held[owner[j], nth[j]]
         staged_copy(c).start()
         weight = weights[pl.ds(pl.multiple_of(c * width, width), width), :]
 
@@ -394,7 +418,7 @@
         lax.fori_loop(0, total_rows // block, multiply, 0)
 
     def step(t, carry):
-        flow.step(t)
+        flow.step(t, 1)
 
         def stage(late, call):
             @pl.when((t >= late) & (t < chunks + late))
@@ -435,11 +459,11 @@
     flow.drain()
 
 
-def front(kept_shard, kept_at, sel, query, key, value, weights, per_chunk, ident):
+def front(keep, query, key, value, weights, per_chunk, ident):
     tok, full = key.shape
     local = 3 * HEAD
-    rows = sel.shape[0] // 3 * BLK
-    total_rows = kept_shard.shape[0] * BLK
+    rows = query.shape[0] // 2 * BLK
+    total_rows = keep.shape[1] * BLK
     width = per_chunk * HEAD
     chunks = full // width
     vmem = pl.BlockSpec(memory_space=pltpu.VMEM)
@@ -451,12 +475,13 @@
             jax.ShapeDtypeStruct((chunks, total_rows, width), BF16),
             jax.ShapeDtypeStruct((total_rows, local), BF16),
             jax.ShapeDtypeStruct((1, total_rows), F32),
+            jax.ShapeDtypeStruct((3 * query.shape[0],), jnp.int32),
         ),
-        in_specs=[smem, smem, smem, vmem, vmem, vmem, vmem],
-        out_specs=[vmem, pl.BlockSpec(memory_space=pl.ANY), vmem, vmem],
+        in_specs=[smem, vmem, vmem, vmem, vmem],
+        out_specs=[vmem, pl.BlockSpec(memory_space=pl.ANY), vmem, vmem, smem],
         scratch_shapes=[
             pltpu.VMEM((full, local), BF16),
-            pltpu.VMEM((chunks, 2, SIDE * SIDE, rows // BLK, BLK, HEAD), BF16),
+            pltpu.VMEM((chunks, 2, SIDE * SIDE, rows // BLK, BLK, width // 2), BF16),
             pltpu.VMEM((SIDE * SIDE, rows // BLK, BLK, width), BF16),
             pltpu.VMEM((2, total_rows, width), BF16),
             pltpu.SemaphoreType.DMA((2,)),
@@ -470,7 +495,7 @@
             collective_id=ident, has_side_effects=True, vmem_limit_bytes=VMEM_LIMIT
         ),
         name="front",
-    )(kept_shard, kept_at, sel, query, key, value, weights)
+    )(keep, query, key, value, weights)
 
 
 QB = 256
@@ -478,11 +503,13 @@
 
 
 def causal_kernel(
-    dest, sel, qkv, scale, cot, gathered, q_in, k_in, v_in, out, d_all, grads, rest,
+    dest, keep, qkv, scale, cot, gathered, q_in, k_in, v_in, out, d_all, grads, rest,
     rows_in, rows_sem, d_all_t, v_t, k_t, do_own, do_t, p_buf, dk_acc, dv_acc, dq_t, *scratch,
 ):
-    kept = dest.shape[0]
+    kept = dest.shape[1]
     total_rows = qkv.shape[0]
+    per_shard = q_in.shape[0]
+    sel = [at for each in near_ranks(keep, per_shard) for at in picked(each, range(per_shard // 2, per_shard))]
     blocks = total_rows // QB
     rows_copy = pltpu.make_async_copy(gathered, rows_in, rows_sem)
     rows_copy.start()
@@ -490,7 +517,7 @@
     flow.begin(3)
 
     for j in range(kept):
-        do_own[j * BLK : (j + 1) * BLK, :] = cot[dest[j]]
+        do_own[j * BLK : (j + 1) * BLK, :] = cot[dest[0, j]]
 
     def prepare(c, carry):
         at = pl.ds(pl.multiple_of(c * QB, QB), QB)
@@ -563,17 +590,19 @@
         return carry
 
     def weight_block(g, carry):
-        at = pl.ds(pl.multiple_of(g * QB, QB), QB)
+        wide = rows_in.shape[2]
+        at = pl.ds(pl.multiple_of(g * wide, wide), wide)
         value = jnp.dot(d_all_t[...], rows_in[g], preferred_element_type=F32)
         for which in range(3):
             grads[which, at, :] = value[which * HEAD : (which + 1) * HEAD, :].T.astype(BF16)
         return carry
 
     col_blocks = rows_in.shape[0]
-    share = (col_blocks + 2) // 3
+    lag = 2
+    share = (col_blocks + 3 * lag - 2) // (3 * lag - 1)
 
     def step(t, carry):
-        flow.step(t)
+        flow.step(t, lag)
 
         @pl.when(t < blocks)
         def _():
@@ -591,14 +620,14 @@
 
         return carry
 
-    lax.fori_loop(0, blocks + 3, step, 0)
+    lax.fori_loop(0, blocks + 3 * lag, step, 0)
     flow.drain()
 
 
-def causal(dest, sel, qkv, scale, cot, gathered, query, key, value, per_chunk, ident):
+def causal(dest, keep, qkv, scale, cot, gathered, query, key, value, per_chunk, ident):
     total_rows, local = qkv.shape
     tok, full = key.shape
-    rows = sel.shape[0] // 3 * BLK
+    rows = query.shape[0] // 2 * BLK
     vmem = pl.BlockSpec(memory_space=pltpu.VMEM)
     smem = pl.BlockSpec(memory_space=pltpu.SMEM)
     return pl.pallas_call(
@@ -632,7 +661,7 @@
             flops=20 * 10**9, bytes_accessed=32 * 1024 * 1024, transcendentals=0
         ),
         name="causal",
-    )(dest, sel, qkv, scale, cot, gathered, query, key, value)
+    )(dest, keep, qkv, scale, cot, gathered, query, key, value)
 
 
 class Reduce:
@@ -745,7 +774,7 @@
 
 
 def scatter_kernel(
-    slot_at, d_all, three, value, out, summed, weights, terms, got1, snd2, got2, sums, last1, lasts2, last2,
+    dest, d_all, three, value, out, summed, slot_at, weights, terms, got1, snd2, got2, sums, last1, lasts2, last2,
     send1, recv1, send2, recv2, send3, recv3, send4, recv4, *reduce_scratch,
 ):
     shard = lax.axis_index(SEQ)
@@ -768,6 +797,9 @@
             pl.semaphore_signal(
                 barrier, inc=1, device_id={SEQ: slot(h, turn(a, by), b)}, device_id_type=MESH
             )
+    kept = dest.shape[1]
+    for at in range(kept):
+        slot_at[at] = functools.reduce(lambda got, j: jnp.where(dest[0, j] == at, j, got), range(kept), 0)
     reduce = Reduce(value, *reduce_scratch)
     for target in (reduce.partner, *reduce.next):
         pl.semaphore_signal(barrier, inc=1, device_id={"dp": target}, device_id_type=MESH)
@@ -832,8 +864,10 @@
             s = turn(place[h][1], k)
             for d in range(2):
                 first_send(h, d, s).start()
-    lax.fori_loop(0, 6, group_rest, 0)
+    lax.fori_loop(0, 2, group_rest, 0)
     reduce.stage1()
+    lax.fori_loop(2, 6, group_rest, 0)
+    reduce.stage2()
     for k in (2, 1, 3, 0):
         for h in range(2):
             a, b = place[h]
@@ -847,7 +881,7 @@
                     terms[h, near, s, :, halves[d]].astype(F32) + got1[h, d, s].astype(F32)
                 ).astype(BF16)
                 second_send(h, d, s).start()
-    reduce.stage2()
+    reduce.stage3()
     for k in (2, 1, 3, 0):
         for h in range(2):
             a, b = place[h]
@@ -876,12 +910,11 @@
                     total + last2[h, 0].astype(F32) + last2[h, 1].astype(F32)
                 ).astype(BF16)
         if k == 2:
-            reduce.stage3()
+            reduce.stage4()
         elif k == 1:
-            reduce.stage4()
+            reduce.stage5()
         elif k == 3:
-            reduce.stage5()
-    reduce.stage6(summed)
+            reduce.stage6(summed)
     for h in range(2):
         for d in range(2):
             for s in range(SIDE):
@@ -891,7 +924,7 @@
             fourth_send(h, d).wait_send()
 
 
-def scatter_terms(slot_at, d_all, three, value, ident):
+def scatter_terms(dest, d_all, three, value, ident):
     blocks, _, local = d_all.shape
     full = three.shape[1]
     wide = full // 2
@@ -905,6 +938,7 @@
         in_specs=[pl.BlockSpec(memory_space=pltpu.SMEM), vmem, vmem, vmem],
         out_specs=[vmem, vmem],
         scratch_shapes=[
+            pltpu.SMEM((blocks,), jnp.int32),
             pltpu.VMEM((full, local), BF16),
             pltpu.VMEM((2, SIDE, SIDE, BLK, wide), BF16),
             pltpu.VMEM((2, 2, SIDE, BLK, part), BF16),
@@ -924,102 +958,74 @@
             flops=2 * blocks * BLK * local * full, bytes_accessed=100 * 1024 * 1024, transcendentals=0
         ),
         name="scatter_terms",
-    )(slot_at, d_all, three, value)
-
-
-def assemble_kernel(table, head, rest, sorted_out, out, causal_out):
+    )(dest, d_all, three, value)
+
+
+def assemble_kernel(dest, table, head, rest, sorted_out, summed, out, causal_out, grads):
     kept = sorted_out.shape[0] // BLK
-    first = table[kept + 3 * pl.program_id(0)] == 1
+    late = table[3 * pl.program_id(0)] == 1
+    grads[...] = summed[...].astype(F32)
 
     @pl.when(pl.program_id(0) == 0)
     def _():
         for j in range(kept):
-            causal_out[pl.ds(pl.multiple_of(table[j] * BLK, BLK), BLK), :] = sorted_out[j * BLK : (j + 1) * BLK, :]
-
-    @pl.when(first)
+            causal_out[pl.ds(pl.multiple_of(dest[j] * BLK, BLK), BLK), :] = sorted_out[j * BLK : (j + 1) * BLK, :]
+
+    @pl.when(late)
+    def _():
+        out[...] = rest[...]
+
+    @pl.when(jnp.logical_not(late))
     def _():
         out[...] = head[...]
 
-    @pl.when(jnp.logical_not(first))
-    def _():
-        out[...] = rest[...]
-
-
-def assemble(table, head, rest, sorted_out):
+
+def assemble(dest, table, head, rest, sorted_out, summed):
     rows, full = head.shape
-    kept = sorted_out.shape[0] // BLK
-    whole = pl.BlockSpec(sorted_out.shape, lambda g, t: (0, 0))
+    steps = 2 * rows // BLK
+    whole = pl.BlockSpec(sorted_out.shape, lambda g, d, t: (0, 0))
+    part = pl.BlockSpec((3, full // steps, HEAD), lambda g, d, t: (0, g, 0))
     return pl.pallas_call(
         assemble_kernel,
         out_shape=(
             jax.ShapeDtypeStruct((2 * rows, full), BF16),
             jax.ShapeDtypeStruct(sorted_out.shape, BF16),
+            jax.ShapeDtypeStruct(summed.shape, F32),
         ),
         grid_spec=pltpu.PrefetchScalarGridSpec(
-            num_scalar_prefetch=1,
-            grid=(2 * rows // BLK,),
+            num_scalar_prefetch=2,
+            grid=(steps,),
             in_specs=[
-                pl.BlockSpec((BLK, full), lambda g, t: (t[kept + 3 * g + 1], 0)),
-                pl.BlockSpec((BLK, full), lambda g, t: (t[kept + 3 * g + 2], 0)),
+                pl.BlockSpec((BLK, full), lambda g, d, t: (t[3 * g + 1], 0)),
+                pl.BlockSpec((BLK, full), lambda g, d, t: (t[3 * g + 2], 0)),
                 whole,
+                part,
             ],
-            out_specs=[pl.BlockSpec((BLK, full), lambda g, t: (g, 0)), whole],
+            out_specs=[pl.BlockSpec((BLK, full), lambda g, d, t: (g, 0)), whole, part],
         ),
+        compiler_params=pltpu.CompilerParams(vmem_limit_bytes=VMEM_LIMIT),
         name="assemble",
-    )(table, head, rest, sorted_out)
+    )(dest, table, head, rest, sorted_out, summed)
 
 
 def shards(query_input, key_input, value_input, keep_blocks, dest_slots, proj_weights, cotangent):
     tok, full = query_input.shape[1:]
     per_shard = tok // BLK
-    shard = lax.axis_index(SEQ)
-    count = lax.axis_size(SEQ)
-    half_blocks = per_shard // 2
+    kept = keep_blocks.shape[1]
     query = query_input.reshape(per_shard, BLK, full)
     key = key_input[0]
     value = value_input[0]
-    keep = keep_blocks[0]
-    dest = dest_slots[0]
-
-    kept = jnp.any(
-        keep[None, None, :] == jnp.arange(count * per_shard).reshape(count, per_shard)[:, :, None], axis=2
+    first, gathered, qkv, scale, table = front(keep_blocks, query, key, value, proj_weights, 4, 0)
+    sorted_out, d_all, local_grads, rest = causal(
+        dest_slots, keep_blocks, qkv, scale, cotangent.reshape(kept, BLK, -1), gathered, query, key, value, 2, 1
     )
-    order_key = jnp.where(kept, 0, per_shard) + jnp.arange(per_shard)[None, :]
-    rank = jnp.sum(order_key[:, None, :] < order_key[:, :, None], axis=2).astype(jnp.int32)
-    order = jnp.sum(
-        jnp.where(
-            rank[:, None, :] == jnp.arange(per_shard)[None, :, None], jnp.arange(per_shard)[None, None, :], 0
-        ),
-        axis=2,
-    ).astype(jnp.int32)
-    wrapped = jnp.concatenate([order, order[:2]], axis=0)
-    near = lax.dynamic_slice_in_dim(wrapped, shard, 3, 0)
-    sel_first = near[:, :half_blocks].reshape(-1)
-    sel_rest = near[:, half_blocks:].reshape(-1)
-    own_rank = lax.dynamic_slice_in_dim(rank, shard, 1, 0)[0]
-    in_first = (own_rank < half_blocks).astype(jnp.int32)
-    at = own_rank % half_blocks
-    table = jnp.stack([in_first, at * in_first, at * (1 - in_first)], axis=1).reshape(-1)
-    keep_shard = keep // per_shard
-    before = jnp.sum((keep_shard[None, :] == keep_shard[:, None]) & (keep[None, :] < keep[:, None]), axis=1)
-
-    slot_at = jnp.sum(
-        jnp.where(dest[None, :] == jnp.arange(dest.shape[0])[:, None], jnp.arange(dest.shape[0])[None, :], 0),
-        axis=1,
-    ).astype(jnp.int32)
-
-    first, gathered, qkv, scale = front(
-        keep_shard.astype(jnp.int32), before.astype(jnp.int32), sel_first, query, key, value, proj_weights, 2, 0
-    )
-    sorted_out, d_all, local_grads, rest = causal(
-        dest, sel_rest, qkv, scale, cotangent.reshape(dest.shape[0], BLK, -1), gathered, query, key, value, 2, 1
-    )
-    window_out, causal_out = assemble(jnp.concatenate([dest, table]), first, rest, sorted_out)
-    row_grad, grads = scatter_terms(
-        slot_at, d_all.reshape(dest.shape[0], BLK, -1), proj_weights,
+    row_grad, summed = scatter_terms(
+        dest_slots, d_all.reshape(kept, BLK, -1), proj_weights,
         local_grads.reshape(3, 2, SIDE, full // 2 // SIDE, HEAD), 2,
     )
-    grads = grads.reshape(proj_weights.shape).astype(F32)
+    window_out, causal_out, grads = assemble(
+        dest_slots[0], table, first, rest, sorted_out, summed.reshape(proj_weights.shape)
+    )
     return (window_out[None], causal_out[None], grads, row_grad[None])
 
 

time: 328 us -> 324 us (0.988)
  other arithmetic: 8.98 us -> 0 us
  Pallas kernels: 314 us -> 322 us
    pallas_call x1, Pallas kernels: 174 us -> 184 us  [front(): pl.pallas_call(front_kernel, out_shape=(jax.ShapeDtypeStruct((rows, full)...]
    convert_element_type x2 -> x0, other arithmetic: 3.34 us -> none  [the longest x1 3.33 us: shards(): grads = grads.reshape(proj_weights.shape).astype(F32)]
where the time goes in v7:
time: 324 us
  Pallas kernels  322 us (99%)
    pallas_call x1, Pallas kernels, front(): pl.pallas_call(front_kernel, out_shape=(jax.ShapeDtypeStruct((rows, full)...  184 us
    pallas_call x1, Pallas kernels, causal(): pl.pallas_call(causal_kernel, out_shape=(jax.ShapeDtypeStruct((total_rows...  80.6 us
    pallas_call x1, Pallas kernels, scatter_terms(): pl.pallas_call(scatter_kernel, out_shape=(jax.ShapeDtypeStruct((BLK, full...  51.3 us

profile of v7, /device:TPU:0, one launch (start us, length us, event | category | flops | bytes accessed | tf_op | source)
XLA Modules:
  0.0 323.7 jit_solution(481688459695437964)
XLA Ops:
  0.6 184.2 %front.1 = (bf16[256,2048]{1,0:T(8,128)(2,1)}, bf16[4,2048,512]{2,1,0:T(8,128)(2,1)}, bf16[2048,384]{1,0:T(8,128)(2,1)}, f32[1,2048]{1,0:T(1,128)}, s32[12]{0:T(128)}) custom-call(s32[1,16]{1,0:T(1,128)} %keep.3, bf16[4,128,2048]{2,1,0:T(8,128)(2,1)} %bitcast.11, bf16[512,2048]{1,0:T(8,128)(2,1)} %bitcast.13, bf16[512,2048]{1,0:T(8,128)(2,1)} %bitcast.15, ...), custom_call_target="tpu_custom_call" | custom-call | tf_op jit(solution)/shard_map/front/pallas_call | solution.py:471
  184.8 80.6 %causal.1 = (bf16[2048,128]{1,0:T(8,128)(2,1)}, bf16[2048,384]{1,0:T(8,128)(2,1)}, bf16[3,2048,128]{2,1,0:T(8,128)(2,1)}, bf16[256,2048]{1,0:T(8,128)(2,1)}) custom-call(s32[1,16]{1,0:T(1,128)} %dest.3, s32[1,16]{1,0:T(1,128)} %keep.3, bf16[2048,384]{1,0:T(8,128)(2,1)} %get-tuple-element.20.qkv, f32[1,2048]{1,0:T(1,128)} %get-tuple-element.21.scale, ...), custom_call_target="tpu_custom_call" | custom-call | flops 20000000000 | bytes 33554432 | tf_op jit(solution)/shard_map/causal/pallas_call | solution.py:633
  265.4 51.3 %scatter_terms.1 = (bf16[128,2048]{1,0:T(8,128)(2,1)}, bf16[3,2,4,256,128]{4,3,2,1,0:T(8,128)(2,1)}) custom-call(s32[1,16]{1,0:T(1,128)} %dest.3, bf16[16,128,384]{2,1,0:T(8,128)(2,1)} %bitcast.23, bf16[3,2048,128]{2,1,0:T(8,128)(2,1)} %three.3, bf16[3,2,4,256,128]{4,3,2,1,0:T(8,128)(2,1)} %bitcast.24), custom_call_target="tpu_custom_call" | custom-call | flops 3221225472 | bytes 104857600 | tf_op jit(solution)/shard_map/scatter_terms/pallas_call | solution.py:935
  316.7 0.0 copy-start
  316.7 6.2 %assemble.1 = (bf16[512,2048]{1,0:T(8,128)(2,1)}, bf16[2048,128]{1,0:T(8,128)(2,1)}, f32[3,2048,128]{2,1,0:T(8,128)}) custom-call(s32[16]{0:T(128)} %bitcast.19, s32[12]{0:T(128)} %get-tuple-element.18.table, bf16[256,2048]{1,0:T(8,128)(2,1)} %get-tuple-element.19.head, bf16[256,2048]{1,0:T(8,128)(2,1)} %get-tuple-element.23.rest, ...), custom_call_target="tpu_custom_call" | custom-call | tf_op jit(solution)/shard_map/assemble/pallas_call | solution.py:988
  322.9 0.0 copy-done
  322.9 0.8 copy.12
Async XLA Ops:
  316.7 6.2 %copy-start = (bf16[128,2048]{1,0:T(8,128)(2,1)S(1)}, bf16[128,2048]{1,0:T(8,128)(2,1)}, u32[]{:S(2)}) copy-start(bf16[128,2048]{1,0:T(8,128)(2,1)} %get-tuple-element.31) | copy-start | bytes 1572868

commit v8 on v7

--- a/solution.py
+++ b/solution.py
@@ -21,15 +21,27 @@
 VMEM_LIMIT = 56 * 1024 * 1024
 
 
-def window_part(query, key, value_t, bias):
-    scores = lax.dot_general(key, query, NT, preferred_element_type=F32)
-    if bias is not None:
-        scores = scores + bias
-    top = jnp.max(scores, axis=0, keepdims=True)
-    weight = jnp.exp2((scores - top) * SCALE2)
-    total = jnp.sum(weight, axis=0, keepdims=True)
-    out = jnp.dot(value_t, weight.astype(BF16), preferred_element_type=F32)
-    return out / total, top * SCALE2 + jnp.log2(total)
+def window_parts(heads):
+    def scores_of(query, key, value_t, bias):
+        scores = lax.dot_general(key, query, NT, preferred_element_type=F32)
+        if bias is not None:
+            scores = scores + bias
+        return scores, jnp.max(scores, axis=0, keepdims=True), value_t
+
+    def rest_of(scores, top, value_t):
+        weight = jnp.exp2((scores - top) * SCALE2)
+        total = jnp.sum(weight, axis=0, keepdims=True)
+        out = jnp.dot(value_t, weight.astype(BF16), preferred_element_type=F32)
+        return out * (1.0 / total), top * SCALE2 + jnp.log2(total)
+
+    done = []
+    ahead = scores_of(*heads[0])
+    for h in range(len(heads)):
+        current = ahead
+        if h + 1 < len(heads):
+            ahead = scores_of(*heads[h + 1])
+        done.append(rest_of(*current))
+    return done
 
 
 def merged(out_a, lse_a, out_b, lse_b):
@@ -147,23 +159,23 @@
             self.hop_one(c + self.ahead).start()
 
     def own(self, c):
+        heads = []
         for h in range(self.per_chunk):
             cols = self.cols(c, h)
             value_t = self.v_in[:, cols].T
             self.v_t[cols, :] = value_t
-            part, lse = window_part(
-                self.q_own[c, :, self.head(h)], self.k_in[:, cols], value_t, self.bias_own[...]
-            )
+            heads.append((self.q_own[c, :, self.head(h)], self.k_in[:, cols], value_t, self.bias_own[...]))
+        for h, (part, lse) in enumerate(window_parts(heads)):
             self.o_own[c, self.head(h), :] = part
             self.l_own[c, self.lse_at(h), :] = self.spread(lse)
 
     def two(self, c):
         self.hop_two(c).wait_recv()
-        for h in range(self.per_chunk):
-            cols = self.cols(c, h)
-            part, lse = window_part(
-                self.q_two[c, :, self.head(h)], self.k_in[:, cols], self.v_t[cols, :], self.bias_two[...]
-            )
+        heads = [
+            (self.q_two[c, :, self.head(h)], self.k_in[:, self.cols(c, h)], self.v_t[self.cols(c, h), :], self.bias_two[...])
+            for h in range(self.per_chunk)
+        ]
+        for h, (part, lse) in enumerate(window_parts(heads)):
             self.o_snd2[c, self.head(h), :] = part.astype(BF16)
             self.l_snd2[c, self.lse_at(h), :] = self.spread(lse)
         for each in self.back_two(c):
@@ -174,12 +186,10 @@
         return jnp.where(self.shard == 0, LOW, got[c, first : first + 1, :])
 
     def one(self, c):
-        parts = []
-        for h in range(self.per_chunk):
-            cols = self.cols(c, h)
-            parts.append(
-                window_part(self.q_one[c, :, self.head(h)], self.k_in[:, cols], self.v_t[cols, :], None)
-            )
+        parts = window_parts([
+            (self.q_one[c, :, self.head(h)], self.k_in[:, self.cols(c, h)], self.v_t[self.cols(c, h), :], None)
+            for h in range(self.per_chunk)
+        ])
         for each in self.back_two(c):
             each.wait_recv()
         for h in range(self.per_chunk):
@@ -514,7 +524,7 @@
     rows_copy = pltpu.make_async_copy(gathered, rows_in, rows_sem)
     rows_copy.start()
     flow = Flow(sel, q_in, k_in, v_in, rest, scratch)
-    flow.begin(3)
+    flow.begin(2)
 
     for j in range(kept):
         do_own[j * BLK : (j + 1) * BLK, :] = cot[dest[0, j]]
@@ -598,29 +608,34 @@
         return carry
 
     col_blocks = rows_in.shape[0]
-    lag = 2
+    lag = 1
+    per_step = blocks // flow.chunks
     share = (col_blocks + 3 * lag - 2) // (3 * lag - 1)
 
     def step(t, carry):
         flow.step(t, lag)
 
-        @pl.when(t < blocks)
+        @pl.when(t < flow.chunks)
         def _():
-            query_block(blocks - 1 - t)
-
-        @pl.when(t == blocks)
+            def one_block(r, carry):
+                query_block(blocks - 1 - t * per_step - r)
+                return carry
+
+            lax.fori_loop(0, per_step, one_block, 0)
+
+        @pl.when(t == flow.chunks)
         def _():
             lax.fori_loop(0, blocks, finish, 0)
             rows_copy.wait()
 
-        @pl.when(t >= blocks)
+        @pl.when(t >= flow.chunks)
         def _():
-            low = (t - blocks) * share
+            low = (t - flow.chunks) * share
             lax.fori_loop(low, jnp.minimum(low + share, col_blocks), weight_block, 0)
 
         return carry
 
-    lax.fori_loop(0, blocks + 3 * lag, step, 0)
+    lax.fori_loop(0, flow.chunks + 3 * lag, step, 0)
     flow.drain()
 
 
@@ -1015,9 +1030,9 @@
     query = query_input.reshape(per_shard, BLK, full)
     key = key_input[0]
     value = value_input[0]
-    first, gathered, qkv, scale, table = front(keep_blocks, query, key, value, proj_weights, 4, 0)
+    first, gathered, qkv, scale, table = front(keep_blocks, query, key, value, proj_weights, 2, 0)
     sorted_out, d_all, local_grads, rest = causal(
-        dest_slots, keep_blocks, qkv, scale, cotangent.reshape(kept, BLK, -1), gathered, query, key, value, 2, 1
+        dest_slots, keep_blocks, qkv, scale, cotangent.reshape(kept, BLK, -1), gathered, query, key, value, 4, 1
     )
     row_grad, summed = scatter_terms(
         dest_slots, d_all.reshape(kept, BLK, -1), proj_weights,

time: 324 us -> 315 us (0.972)
  Pallas kernels: 322 us -> 313 us
    pallas_call x1, Pallas kernels: 184 us -> 174 us  [front(): pl.pallas_call(front_kernel, out_shape=(jax.ShapeDtypeStruct((rows, full)...]
where the time goes in v8:
time: 315 us; the launch traced here: 314 us
  Pallas kernels  313 us (99%)
    pallas_call x1, Pallas kernels, front(): pl.pallas_call(front_kernel, out_shape=(jax.ShapeDtypeStruct((rows, full)...  174 us
    pallas_call x1, Pallas kernels, causal(): pl.pallas_call(causal_kernel, out_shape=(jax.ShapeDtypeStruct((total_rows...  81.7 us
    pallas_call x1, Pallas kernels, scatter_terms(): pl.pallas_call(scatter_kernel, out_shape=(jax.ShapeDtypeStruct((BLK, full...  50.8 us

profile of v8, /device:TPU:0, one launch (start us, length us, event | category | flops | bytes accessed | tf_op | source)
XLA Modules:
  0.0 314.2 jit_solution(2408991545870308806)
XLA Ops:
  0.6 174.0 %front.1 = (bf16[256,2048]{1,0:T(8,128)(2,1)}, bf16[8,2048,256]{2,1,0:T(8,128)(2,1)}, bf16[2048,384]{1,0:T(8,128)(2,1)}, f32[1,2048]{1,0:T(1,128)}, s32[12]{0:T(128)}) custom-call(s32[1,16]{1,0:T(1,128)} %keep.3, bf16[4,128,2048]{2,1,0:T(8,128)(2,1)} %bitcast.11, bf16[512,2048]{1,0:T(8,128)(2,1)} %bitcast.13, bf16[512,2048]{1,0:T(8,128)(2,1)} %bitcast.15, ...), custom_call_target="tpu_custom_call" | custom-call | tf_op jit(solution)/shard_map/front/pallas_call | solution.py:481
  174.7 81.7 %causal.1 = (bf16[2048,128]{1,0:T(8,128)(2,1)}, bf16[2048,384]{1,0:T(8,128)(2,1)}, bf16[3,2048,128]{2,1,0:T(8,128)(2,1)}, bf16[256,2048]{1,0:T(8,128)(2,1)}) custom-call(s32[1,16]{1,0:T(1,128)} %dest.3, s32[1,16]{1,0:T(1,128)} %keep.3, bf16[2048,384]{1,0:T(8,128)(2,1)} %get-tuple-element.20.qkv, f32[1,2048]{1,0:T(1,128)} %get-tuple-element.21.scale, ...), custom_call_target="tpu_custom_call" | custom-call | flops 20000000000 | bytes 33554432 | tf_op jit(solution)/shard_map/causal/pallas_call | solution.py:648
  256.3 50.8 %scatter_terms.1 = (bf16[128,2048]{1,0:T(8,128)(2,1)}, bf16[3,2,4,256,128]{4,3,2,1,0:T(8,128)(2,1)}) custom-call(s32[1,16]{1,0:T(1,128)} %dest.3, bf16[16,128,384]{2,1,0:T(8,128)(2,1)} %bitcast.23, bf16[3,2048,128]{2,1,0:T(8,128)(2,1)} %three.3, bf16[3,2,4,256,128]{4,3,2,1,0:T(8,128)(2,1)} %bitcast.24), custom_call_target="tpu_custom_call" | custom-call | flops 3221225472 | bytes 104857600 | tf_op jit(solution)/shard_map/scatter_terms/pallas_call | solution.py:950
  307.1 0.0 copy-start
  307.1 6.2 %assemble.1 = (bf16[512,2048]{1,0:T(8,128)(2,1)}, bf16[2048,128]{1,0:T(8,128)(2,1)}, f32[3,2048,128]{2,1,0:T(8,128)}) custom-call(s32[16]{0:T(128)} %bitcast.19, s32[12]{0:T(128)} %get-tuple-element.18.table, bf16[256,2048]{1,0:T(8,128)(2,1)} %get-tuple-element.19.head, bf16[256,2048]{1,0:T(8,128)(2,1)} %get-tuple-element.23.rest, ...), custom_call_target="tpu_custom_call" | custom-call | tf_op jit(solution)/shard_map/assemble/pallas_call | solution.py:1003
  313.4 0.0 copy-done
  313.4 0.8 copy.12
Async XLA Ops:
  307.1 6.2 %copy-start = (bf16[128,2048]{1,0:T(8,128)(2,1)S(1)}, bf16[128,2048]{1,0:T(8,128)(2,1)}, u32[]{:S(2)}) copy-start(bf16[128,2048]{1,0:T(8,128)(2,1)} %get-tuple-element.31) | copy-start | bytes 1572868

commit v9 on v8

--- a/solution.py
+++ b/solution.py
@@ -257,7 +257,6 @@
 
 class Spread:
     OFFSETS = (0, 1, SIDE - 1, 2)
-    MESSAGES = 20
 
     def __init__(self, got, send_sem, recv_sem):
         self.got, self.send_sem, self.recv_sem = got, send_sem, recv_sem
@@ -280,81 +279,70 @@
             self.slot(0, (a, self.turn(b, by))) for by in (1, -1)
         ]
 
-    def message(self, c, kind, which, place, half, target):
+    def message(self, c, kind, group, place, half, target):
         slot = self.slot(kind, place)
         ref = self.got.at[c, kind, slot] if half is None else self.got.at[c, kind, slot, half]
-        at = kind * self.MESSAGES + which
         return pltpu.make_async_remote_copy(
-            src_ref=ref, dst_ref=ref, send_sem=self.send_sem.at[c, at], recv_sem=self.recv_sem.at[c, at],
+            src_ref=ref, dst_ref=ref, send_sem=self.send_sem.at[c, kind], recv_sem=self.recv_sem.at[c, kind, group],
             device_id={SEQ: self.slot(kind, target)}, device_id_type=MESH,
         )
 
-    def first(self, c, kind, what):
+    def whole(self, c, kind, group, pieces):
+        a, b = self.here[kind]
+        ref = self.got.at[c, kind, pl.ds(0, pieces)]
+        return pltpu.make_async_remote_copy(
+            src_ref=ref, dst_ref=ref, send_sem=self.send_sem.at[c, kind], recv_sem=self.recv_sem.at[c, kind, group],
+            device_id={SEQ: self.slot(kind, (self.turn(a, 1), b))}, device_id_type=MESH,
+        )
+
+    def ring(self, c, kind, group, here, up, down, to_up, to_down):
+        if group % 2 == 0:
+            pairs = ((here, None, to_up), (here, None, to_down))
+        else:
+            pairs = ((down, 0, to_up), (up, 1, to_down))
+        for pair in pairs:
+            self.message(c, kind, group, *pair).start()
+
+    def first(self, c, kind, group):
         a, b = self.here[kind]
         up, down = (self.turn(a, 1), b), (self.turn(a, -1), b)
-        return self.four(c, kind, 0, (a, b), up, down, (self.turn(a, 2), b), up, down, what)
-
-    def second(self, c, kind, k, what):
+        self.ring(c, kind, group, (a, b), up, down, up, down)
+
+    def second(self, c, kind, group, k):
         a, b = self.here[kind]
         origin = self.turn(a, self.OFFSETS[k])
-        return self.four(
-            c, kind, 4 + 4 * k, (origin, b), (origin, self.turn(b, 1)), (origin, self.turn(b, -1)),
-            (origin, self.turn(b, 2)), (a, self.turn(b, 1)), (a, self.turn(b, -1)), what,
-        )
-
-    def four(self, c, kind, base, here, up, down, far, to_up, to_down, what):
-        pairs = {
-            "send": ((base, here, None, to_up), (base + 1, here, None, to_down)),
-            "came": ((base, down, None, to_up), (base + 1, up, None, to_down)),
-            "pass": ((base + 2, down, 0, to_up), (base + 3, up, 1, to_down)),
-            "last": ((base + 2, far, 0, to_up), (base + 3, far, 1, to_down)),
-        }[what]
-        return [self.message(c, kind, *pair) for pair in pairs]
+        up, down = self.turn(b, 1), self.turn(b, -1)
+        self.ring(c, kind, group, (origin, b), (origin, up), (origin, down), (a, up), (a, down))
 
     def launch(self, c):
         for kind in range(2):
-            for each in self.first(c, kind, "send"):
-                each.start()
+            self.first(c, kind, 0)
 
     def relay(self, c):
         for kind in range(2):
-            for each in self.first(c, kind, "came"):
-                each.wait_recv()
-            for each in self.first(c, kind, "pass"):
-                each.start()
+            self.whole(c, kind, 0, 2).wait_recv()
+            self.first(c, kind, 1)
             for k in range(3):
-                for each in self.second(c, kind, k, "send"):
-                    each.start()
+                self.second(c, kind, 2, k)
 
     def relay_far(self, c):
         for kind in range(2):
-            for each in self.first(c, kind, "last"):
-                each.wait_recv()
-            for each in self.second(c, kind, 3, "send"):
-                each.start()
+            self.whole(c, kind, 1, 1).wait_recv()
+            self.second(c, kind, 2, 3)
 
     def second_relay(self, c):
-        for k in range(4):
-            for kind in range(2):
-                for each in self.second(c, kind, k, "came"):
-                    each.wait_recv()
-                for each in self.second(c, kind, k, "pass"):
-                    each.start()
+        for kind in range(2):
+            self.whole(c, kind, 2, 8).wait_recv()
+            for k in range(4):
+                self.second(c, kind, 3, k)
 
     def settle(self, c):
-        for k in range(4):
-            for kind in range(2):
-                for each in self.second(c, kind, k, "last"):
-                    each.wait_recv()
+        for kind in range(2):
+            self.whole(c, kind, 3, 4).wait_recv()
 
     def drain(self, c):
         for kind in range(2):
-            for what in ("send", "pass"):
-                for each in self.first(c, kind, what):
-                    each.wait_send()
-                for k in range(4):
-                    for each in self.second(c, kind, k, what):
-                        each.wait_send()
+            self.whole(c, kind, 0, 15).wait_send()
 
 
 def front_kernel(
@@ -497,8 +485,8 @@
             pltpu.SemaphoreType.DMA((2,)),
             pltpu.VMEM((total_rows, local), F32),
             pltpu.VMEM((total_rows, HEAD), F32),
-            pltpu.SemaphoreType.DMA((chunks, 2 * Spread.MESSAGES)),
-            pltpu.SemaphoreType.DMA((chunks, 2 * Spread.MESSAGES)),
+            pltpu.SemaphoreType.DMA((chunks, 2)),
+            pltpu.SemaphoreType.DMA((chunks, 2, 4)),
             *Flow.scratch(rows, tok, full, per_chunk),
         ],
         compiler_params=pltpu.CompilerParams(
@@ -608,34 +596,42 @@
         return carry
 
     col_blocks = rows_in.shape[0]
-    lag = 1
-    per_step = blocks // flow.chunks
-    share = (col_blocks + 3 * lag - 2) // (3 * lag - 1)
-
-    def step(t, carry):
-        flow.step(t, lag)
-
-        @pl.when(t < flow.chunks)
+    halves = blocks // flow.chunks
+    share = (col_blocks + 2 * halves - 1) // (2 * halves)
+
+    def step(u, carry):
+        t, r = u // halves, lax.rem(u, halves)
+
+        def stage(at, late, *calls):
+            @pl.when((r == at) & (t >= late) & (t < flow.chunks + late))
+            def _():
+                for call in calls:
+                    call(t - late)
+
+        stage(0, 0, flow.own)
+
+        @pl.when(u < blocks)
         def _():
-            def one_block(r, carry):
-                query_block(blocks - 1 - t * per_step - r)
-                return carry
-
-            lax.fori_loop(0, per_step, one_block, 0)
-
-        @pl.when(t == flow.chunks)
+            query_block(blocks - 1 - u)
+
+        stage(0, 0, flow.pump)
+        stage(0, 1, flow.two)
+        stage(halves - 1, 2, flow.one)
+        stage(halves - 1, 3, flow.final)
+
+        @pl.when(u == blocks)
         def _():
             lax.fori_loop(0, blocks, finish, 0)
             rows_copy.wait()
 
-        @pl.when(t >= flow.chunks)
+        @pl.when(u >= blocks)
         def _():
-            low = (t - flow.chunks) * share
+            low = (u - blocks) * share
             lax.fori_loop(low, jnp.minimum(low + share, col_blocks), weight_block, 0)
 
         return carry
 
-    lax.fori_loop(0, flow.chunks + 3 * lag, step, 0)
+    lax.fori_loop(0, (flow.chunks + 3) * halves, step, 0)
     flow.drain()
 
 

time: 315 us -> 309 us (0.981)
  Pallas kernels: 313 us -> 307 us
    pallas_call x1, Pallas kernels: 174 us -> 169 us  [front(): pl.pallas_call(front_kernel, out_shape=(jax.ShapeDtypeStruct((rows, full)...]
where the time goes in v9:
time: 309 us
  Pallas kernels  307 us (99%)
    pallas_call x1, Pallas kernels, front(): pl.pallas_call(front_kernel, out_shape=(jax.ShapeDtypeStruct((rows, full)...  169 us
    pallas_call x1, Pallas kernels, causal(): pl.pallas_call(causal_kernel, out_shape=(jax.ShapeDtypeStruct((total_rows...  81.7 us
    pallas_call x1, Pallas kernels, scatter_terms(): pl.pallas_call(scatter_kernel, out_shape=(jax.ShapeDtypeStruct((BLK, full...  50.8 us
    pallas_call x1, Pallas kernels, assemble(): pl.pallas_call(assemble_kernel, out_shape=(jax.ShapeDtypeStruct((2 * rows...  6.24 us

profile of v9, /device:TPU:0, one launch (start us, length us, event | category | flops | bytes accessed | tf_op | source)
XLA Modules:
  0.0 308.8 jit_solution(8785200313553399956)
XLA Ops:
  0.6 168.5 %front.1 = (bf16[256,2048]{1,0:T(8,128)(2,1)}, bf16[8,2048,256]{2,1,0:T(8,128)(2,1)}, bf16[2048,384]{1,0:T(8,128)(2,1)}, f32[1,2048]{1,0:T(1,128)}, s32[12]{0:T(128)}) custom-call(s32[1,16]{1,0:T(1,128)} %keep.3, bf16[4,128,2048]{2,1,0:T(8,128)(2,1)} %bitcast.11, bf16[512,2048]{1,0:T(8,128)(2,1)} %bitcast.13, bf16[512,2048]{1,0:T(8,128)(2,1)} %bitcast.15, ...), custom_call_target="tpu_custom_call" | custom-call | tf_op jit(solution)/shard_map/front/pallas_call | solution.py:469
  169.2 81.7 %causal.1 = (bf16[2048,128]{1,0:T(8,128)(2,1)}, bf16[2048,384]{1,0:T(8,128)(2,1)}, bf16[3,2048,128]{2,1,0:T(8,128)(2,1)}, bf16[256,2048]{1,0:T(8,128)(2,1)}) custom-call(s32[1,16]{1,0:T(1,128)} %dest.3, s32[1,16]{1,0:T(1,128)} %keep.3, bf16[2048,384]{1,0:T(8,128)(2,1)} %get-tuple-element.20.qkv, f32[1,2048]{1,0:T(1,128)} %get-tuple-element.21.scale, ...), custom_call_target="tpu_custom_call" | custom-call | flops 20000000000 | bytes 33554432 | tf_op jit(solution)/shard_map/causal/pallas_call | solution.py:644
  250.9 50.8 %scatter_terms.1 = (bf16[128,2048]{1,0:T(8,128)(2,1)}, bf16[3,2,4,256,128]{4,3,2,1,0:T(8,128)(2,1)}) custom-call(s32[1,16]{1,0:T(1,128)} %dest.3, bf16[16,128,384]{2,1,0:T(8,128)(2,1)} %bitcast.23, bf16[3,2048,128]{2,1,0:T(8,128)(2,1)} %three.3, bf16[3,2,4,256,128]{4,3,2,1,0:T(8,128)(2,1)} %bitcast.24), custom_call_target="tpu_custom_call" | custom-call | flops 3221225472 | bytes 104857600 | tf_op jit(solution)/shard_map/scatter_terms/pallas_call | solution.py:946
  301.8 0.0 copy-start
  301.8 6.2 %assemble.1 = (bf16[512,2048]{1,0:T(8,128)(2,1)}, bf16[2048,128]{1,0:T(8,128)(2,1)}, f32[3,2048,128]{2,1,0:T(8,128)}) custom-call(s32[16]{0:T(128)} %bitcast.19, s32[12]{0:T(128)} %get-tuple-element.18.table, bf16[256,2048]{1,0:T(8,128)(2,1)} %get-tuple-element.19.head, bf16[256,2048]{1,0:T(8,128)(2,1)} %get-tuple-element.23.rest, ...), custom_call_target="tpu_custom_call" | custom-call | tf_op jit(solution)/shard_map/assemble/pallas_call | solution.py:999
  308.0 0.0 copy-done
  308.0 0.8 copy.12
Async XLA Ops:
  301.8 6.2 %copy-start = (bf16[128,2048]{1,0:T(8,128)(2,1)S(1)}, bf16[128,2048]{1,0:T(8,128)(2,1)}, u32[]{:S(2)}) copy-start(bf16[128,2048]{1,0:T(8,128)(2,1)} %get-tuple-element.31) | copy-start | bytes 1572868

commit v10 on v9

--- a/solution.py
+++ b/solution.py
@@ -512,7 +512,7 @@
     rows_copy = pltpu.make_async_copy(gathered, rows_in, rows_sem)
     rows_copy.start()
     flow = Flow(sel, q_in, k_in, v_in, rest, scratch)
-    flow.begin(2)
+    flow.begin(3)
 
     for j in range(kept):
         do_own[j * BLK : (j + 1) * BLK, :] = cot[dest[0, j]]
@@ -1028,7 +1028,7 @@
     value = value_input[0]
     first, gathered, qkv, scale, table = front(keep_blocks, query, key, value, proj_weights, 2, 0)
     sorted_out, d_all, local_grads, rest = causal(
-        dest_slots, keep_blocks, qkv, scale, cotangent.reshape(kept, BLK, -1), gathered, query, key, value, 4, 1
+        dest_slots, keep_blocks, qkv, scale, cotangent.reshape(kept, BLK, -1), gathered, query, key, value, 2, 1
     )
     row_grad, summed = scatter_terms(
         dest_slots, d_all.reshape(kept, BLK, -1), proj_weights,

time: 309 us -> 307 us (level)
  no operation moved by 1% of the time
where the time goes in v10:
time: 307 us
  Pallas kernels  305 us (99%)
    pallas_call x1, Pallas kernels, front(): pl.pallas_call(front_kernel, out_shape=(jax.ShapeDtypeStruct((rows, full)...  169 us
    pallas_call x1, Pallas kernels, causal(): pl.pallas_call(causal_kernel, out_shape=(jax.ShapeDtypeStruct((total_rows...  79.7 us
    pallas_call x1, Pallas kernels, scatter_terms(): pl.pallas_call(scatter_kernel, out_shape=(jax.ShapeDtypeStruct((BLK, full...  50.8 us
    pallas_call x1, Pallas kernels, assemble(): pl.pallas_call(assemble_kernel, out_shape=(jax.ShapeDtypeStruct((2 * rows...  6.24 us

profile of v10, /device:TPU:0, one launch (start us, length us, event | category | flops | bytes accessed | tf_op | source)
XLA Modules:
  0.0 306.7 jit_solution(9888093758997371171)
XLA Ops:
  0.6 168.6 %front.1 = (bf16[256,2048]{1,0:T(8,128)(2,1)}, bf16[8,2048,256]{2,1,0:T(8,128)(2,1)}, bf16[2048,384]{1,0:T(8,128)(2,1)}, f32[1,2048]{1,0:T(1,128)}, s32[12]{0:T(128)}) custom-call(s32[1,16]{1,0:T(1,128)} %keep.3, bf16[4,128,2048]{2,1,0:T(8,128)(2,1)} %bitcast.11, bf16[512,2048]{1,0:T(8,128)(2,1)} %bitcast.13, bf16[512,2048]{1,0:T(8,128)(2,1)} %bitcast.15, ...), custom_call_target="tpu_custom_call" | custom-call | tf_op jit(solution)/shard_map/front/pallas_call | solution.py:469
  169.2 79.7 %causal.1 = (bf16[2048,128]{1,0:T(8,128)(2,1)}, bf16[2048,384]{1,0:T(8,128)(2,1)}, bf16[3,2048,128]{2,1,0:T(8,128)(2,1)}, bf16[256,2048]{1,0:T(8,128)(2,1)}) custom-call(s32[1,16]{1,0:T(1,128)} %dest.3, s32[1,16]{1,0:T(1,128)} %keep.3, bf16[2048,384]{1,0:T(8,128)(2,1)} %get-tuple-element.20.qkv, f32[1,2048]{1,0:T(1,128)} %get-tuple-element.21.scale, ...), custom_call_target="tpu_custom_call" | custom-call | flops 20000000000 | bytes 33554432 | tf_op jit(solution)/shard_map/causal/pallas_call | solution.py:644
  248.9 50.8 %scatter_terms.1 = (bf16[128,2048]{1,0:T(8,128)(2,1)}, bf16[3,2,4,256,128]{4,3,2,1,0:T(8,128)(2,1)}) custom-call(s32[1,16]{1,0:T(1,128)} %dest.3, bf16[16,128,384]{2,1,0:T(8,128)(2,1)} %bitcast.23, bf16[3,2048,128]{2,1,0:T(8,128)(2,1)} %three.3, bf16[3,2,4,256,128]{4,3,2,1,0:T(8,128)(2,1)} %bitcast.24), custom_call_target="tpu_custom_call" | custom-call | flops 3221225472 | bytes 104857600 | tf_op jit(solution)/shard_map/scatter_terms/pallas_call | solution.py:946
  299.7 0.0 copy-start
  299.7 6.2 %assemble.1 = (bf16[512,2048]{1,0:T(8,128)(2,1)}, bf16[2048,128]{1,0:T(8,128)(2,1)}, f32[3,2048,128]{2,1,0:T(8,128)}) custom-call(s32[16]{0:T(128)} %bitcast.19, s32[12]{0:T(128)} %get-tuple-element.18.table, bf16[256,2048]{1,0:T(8,128)(2,1)} %get-tuple-element.19.head, bf16[256,2048]{1,0:T(8,128)(2,1)} %get-tuple-element.23.rest, ...), custom_call_target="tpu_custom_call" | custom-call | tf_op jit(solution)/shard_map/assemble/pallas_call | solution.py:999
  305.9 0.0 copy-done
  305.9 0.8 copy.12
Async XLA Ops:
  299.7 6.2 %copy-start = (bf16[128,2048]{1,0:T(8,128)(2,1)S(1)}, bf16[128,2048]{1,0:T(8,128)(2,1)}, u32[]{:S(2)}) copy-start(bf16[128,2048]{1,0:T(8,128)(2,1)} %get-tuple-element.31) | copy-start | bytes 1572868
